TPU v7x, 256 devices: a whole 4x4x8 slice. The times are simulated.
256 devices in a mesh: seq: 32 (over x, z), head: 8 (over y, core).
Axes of the slice: x: 4, y: 4, z: 8, core: 2. Of those that a mesh axis runs over, the one named last changes fastest.
Arguments:
- queries: bfloat16 [2, 8192, 2048], P(None, 'seq', 'head'), may hold values from -1.75 to 1.75
- keys: bfloat16 [2, 8192, 2048], P(None, 'seq', 'head'), may hold values from -1.75 to 1.75
- values: bfloat16 [2, 8192, 2048], P(None, 'seq', 'head'), may hold values from -6 to 6
- gate_pre: bfloat16 [2, 8192, 2048], P(None, 'seq', 'head'), may hold values from -8 to 8
- grad_out: bfloat16 [2, 8192, 4096], P(None, 'seq', 'head'), may hold values from -6 to 6
- w_query: bfloat16 [4096, 2048], P(None, 'head'), may hold values from -0.09375 to 0.09375
- w_key: bfloat16 [4096, 2048], P(None, 'head'), may hold values from -0.09375 to 0.09375
- w_value: bfloat16 [4096, 2048], P(None, 'head'), may hold values from -0.09375 to 0.09375
- w_gate: bfloat16 [4096, 2048], P(None, 'head'), may hold values from -0.09375 to 0.09375
- w_out: bfloat16 [2048, 4096], P('head'), may hold values from -0.125 to 0.125
Outputs:
- grad_in: bfloat16 [2, 8192, 4096], P(None, 'seq', 'head')
All inputs are finite; a program needn't handle non-finite values.
Results may differ from a plain program's by a relative error of at most 0.022.
Values may be sent and summed in bfloat16 or wider, within the bound.
No kernel may reach another device: no remote copies, remote signals or barrier semaphores. Data moves between devices by JAX's collectives and lax.ppermute only.
A program may use at most 128 MiB of HBM per device.

v0:
```python
import jax
import jax.numpy as jnp
from jax import lax
from jax.sharding import PartitionSpec as P

HD = 128


def entering(x, axis, combine, identity, reverse):
    peers, here = (lax.axis_size(axis), lax.axis_index(axis))
    everything = lax.all_gather(x.astype(jnp.bfloat16), axis)
    start = jnp.broadcast_to(jnp.asarray(identity, x.dtype), x.shape)

    def step(k, before):
        at = peers - 1 - k if reverse else k
        reached = at > here if reverse else at < here
        new = combine(before, everything[at].astype(x.dtype))
        return jnp.where(reached, new, before)

    return lax.fori_loop(0, peers, step, start)


def add_states(earlier, later):
    return earlier + later


def body(queries, keys, values, gate_pre, grad_out, w_query, w_key, w_value, w_gate, w_out):
    seq_count, block_len, columns = queries.shape
    head_count = columns // HD
    factor = (lax.axis_size("seq") * block_len) ** (-0.5)
    exact = lax.Precision.HIGHEST
    d_gated = jnp.einsum(
        "scd,jd->scj",
        lax.all_gather(grad_out, "head", axis=2, tiled=True),
        w_out,
        preferred_element_type=jnp.float32,
    )
    gate_open = jax.nn.sigmoid(gate_pre.astype(jnp.float32))
    d_output = (d_gated * gate_open).astype(jnp.bfloat16)

    def split_heads(tensor):
        return tensor.reshape(seq_count, block_len, head_count, HD)

    query_heads = split_heads(queries)
    key_heads = split_heads(keys)
    value_heads = split_heads(values)
    grad_heads = split_heads(d_output)
    key_state = jnp.einsum(
        "schk,schv->shkv", key_heads, value_heads, preferred_element_type=jnp.float32
    )
    query_state = jnp.einsum(
        "schk,schv->shkv", query_heads, grad_heads, preferred_element_type=jnp.float32
    )
    prefix = entering(key_state, "seq", add_states, jnp.zeros_like(key_state), False)
    suffix = entering(query_state, "seq", add_states, jnp.zeros_like(query_state), True)
    causal = jnp.tril(jnp.ones((block_len, block_len), dtype=bool))
    scores = jnp.where(
        causal,
        jnp.einsum("sthk,suhk->shtu", query_heads, key_heads, preferred_element_type=jnp.float32),
        0.0,
    ).astype(jnp.bfloat16)
    backward = jnp.where(
        causal,
        jnp.einsum("sthv,suhv->shtu", grad_heads, value_heads, preferred_element_type=jnp.float32),
        0.0,
    ).astype(jnp.bfloat16)
    attended = factor * (
        jnp.einsum("sthk,shkv->sthv", query_heads.astype(jnp.float32), prefix, precision=exact)
        + jnp.einsum("shtu,suhv->sthv", scores, value_heads, preferred_element_type=jnp.float32)
    )
    d_gate = (
        d_gated * attended.reshape(seq_count, block_len, columns) * gate_open * (1.0 - gate_open)
    ).astype(jnp.bfloat16)
    d_query = factor * (
        jnp.einsum("sthv,shkv->sthk", grad_heads.astype(jnp.float32), prefix, precision=exact)
        + jnp.einsum("shtu,suhk->sthk", backward, key_heads, preferred_element_type=jnp.float32)
    )
    d_key = factor * (
        jnp.einsum("shtu,sthk->suhk", backward, query_heads, preferred_element_type=jnp.float32)
        + jnp.einsum("suhv,shkv->suhk", value_heads.astype(jnp.float32), suffix, precision=exact)
    )
    d_value = factor * (
        jnp.einsum("shtu,sthv->suhv", scores, grad_heads, preferred_element_type=jnp.float32)
        + jnp.einsum("suhk,shkv->suhv", key_heads.astype(jnp.float32), suffix, precision=exact)
    )
    d_query = d_query.astype(jnp.bfloat16).reshape(seq_count, block_len, columns)
    d_key = d_key.astype(jnp.bfloat16).reshape(seq_count, block_len, columns)
    d_value = d_value.astype(jnp.bfloat16).reshape(seq_count, block_len, columns)
    partial_sum = jnp.einsum("scj,dj->scd", d_query, w_query, preferred_element_type=jnp.float32)
    partial_sum = partial_sum + jnp.einsum(
        "scj,dj->scd", d_key, w_key, preferred_element_type=jnp.float32
    )
    partial_sum = partial_sum + jnp.einsum(
        "scj,dj->scd", d_value, w_value, preferred_element_type=jnp.float32
    )
    partial_sum = partial_sum + jnp.einsum(
        "scj,dj->scd", d_gate, w_gate, preferred_element_type=jnp.float32
    )
    return lax.psum_scatter(
        partial_sum.astype(jnp.bfloat16), "head", scatter_dimension=2, tiled=True
    )


def solution(mesh):
    return jax.shard_map(
        body,
        mesh=mesh,
        in_specs=(
            P(None, "seq", "head"),
            P(None, "seq", "head"),
            P(None, "seq", "head"),
            P(None, "seq", "head"),
            P(None, "seq", "head"),
            P(None, "head"),
            P(None, "head"),
            P(None, "head"),
            P(None, "head"),
            P("head", None),
        ),
        out_specs=P(None, "seq", "head"),
        check_vma=False,
    )
```

profile of v0, /device:TPU:1, one launch (start us, length us, event | category | flops | bytes accessed | tf_op | source)
XLA Modules:
  0.0 316.2 jit_solution(5595434872024023321)
XLA Ops:
  6.5 1.2 copy.63
  7.8 1.9 convolution_convert_fusion.1
  10.6 1.8 copy.35
  12.4 1.3 fusion.10
  14.9 78.0 %all-gather.8.cloned.1.call-done = bf16[64,2,128,128]{3,2,1,0:T(8,128)(2,1)} async-done(((bf16[2,2,128,128]{3,2,1,0:T(8,128)(2,1)}), bf16[64,2,128,128]{3,2,1,0:T(8,128)(2,1)}) %all-gather.8.cloned.1.call-update) | async-done | bytes 4194320 | tf_op jit(solution)/shard_map/all_gather | solution.py:11
  92.9 34.0 %while.30 = (s32[]{:T(128)}, f32[2,2,128,128]{3,2,1,0:T(8,128)S(1)}, s32[]{:T(128)}, bf16[32,2,2,128,128]{4,3,2,1,0:T(8,128)(2,1)}, s32[]{:T(128)}, /*index=5*/s32[]{:T(128)}) while((s32[]{:T(128)}, f32[2,2,128,128]{3,2,1,0:T(8,128)S(1)}, s32[]{:T(128)}, bf16[32,2,2,128,128]{4,3,2,1,0:T(8,128)(2,1)}, s32[]{:T(128)}, ...), condition=%wide.region_1.2_spmd.clone, body=%wide.region_0.1_spmd.clone.sunk | while | flops 262148 | bytes 655461 | solution.py:20
  95.0 1.0 add_select_fusion.4
  96.1 1.0 add_select_fusion.4
  98.2 1.0 add_select_fusion.4
  99.2 1.0 add_select_fusion.4
  100.3 1.0 add_select_fusion.4
  101.4 1.0 add_select_fusion.4
  102.4 1.0 add_select_fusion.4
  103.5 1.0 add_select_fusion.4
  105.6 1.1 add_select_fusion.4
  106.7 1.1 add_select_fusion.4
  107.8 1.1 add_select_fusion.4
  108.8 1.0 add_select_fusion.4
  111.0 1.0 add_select_fusion.4
  112.0 1.0 add_select_fusion.4
  113.1 1.0 add_select_fusion.4
  114.1 1.1 add_select_fusion.4
  116.3 1.0 add_select_fusion.4
  117.3 1.0 add_select_fusion.4
  118.4 1.0 add_select_fusion.4
  119.5 1.0 add_select_fusion.4
  120.5 1.0 add_select_fusion.4
  121.6 1.0 add_select_fusion.4
  122.7 1.0 add_select_fusion.4
  123.7 1.0 add_select_fusion.4
  125.8 1.0 add_select_fusion.4
  126.9 1.2 fusion.16
  128.1 1.6 all-gather.6.cloned.1.call-done
  129.8 5.0 %fusion.24 = (bf16[2,256,256]{1,2,0:T(8,128)(2,1)}, bf16[2,256,256]{1,2,0:T(8,128)(2,1)S(1)}) fusion(f32[2,256,2,128]{1,3,2,0:T(8,128)} %fusion.16, bf16[2,256,256]{1,2,0:T(8,128)(2,1)} %copy.35, bf16[2,256,4096]{2,1,0:T(8,128)(2,1)} %all-gather.6.cloned.1.call-done, bf16[256,4096]{1,0:T(8,128)(2,1)} %param.23), kind=kOutput, calls=%fused_computation.39 | convolution fusion | flops 1075183616 | bytes 7602176 | tf_op jit(solution)/shard_map/scd,jd->scj/dot_general | solution.py:32
  135.9 1.2 fusion.9
  137.0 2.1 fusion.41
  139.1 2.1 convolution_bitcast_fusion
  141.9 4.6 %fusion.5 = f32[2,256,4096]{2,1,0:T(8,128)} fusion(bf16[2,256,256]{1,2,0:T(8,128)(2,1)S(1)} %bitcast.150, bf16[4096,256]{1,0:T(8,128)(2,1)S(1)} %copy-done), kind=kOutput, calls=%fused_computation.8 | convolution fusion | flops 1073741824 | bytes 10747904 | tf_op jit(solution)/shard_map/scj,dj->scd/dot_general | solution.py:89
  146.5 68.1 %all-gather.10.cloned.1.call-done = bf16[64,2,128,128]{3,2,1,0:T(8,128)(2,1)} async-done(((bf16[2,2,128,128]{3,2,1,0:T(8,128)(2,1)}), bf16[64,2,128,128]{3,2,1,0:T(8,128)(2,1)}) %all-gather.10.cloned.1.call-update) | async-done | bytes 4194320 | tf_op jit(solution)/shard_map/all_gather | solution.py:11
  214.6 34.1 %while.31 = (s32[]{:T(128)}, f32[2,2,128,128]{3,2,1,0:T(8,128)S(1)}, s32[]{:T(128)}, bf16[32,2,2,128,128]{4,3,2,1,0:T(8,128)(2,1)}, s32[]{:T(128)}, /*index=5*/s32[]{:T(128)}, s32[]{:T(128)}, s32[]{:T(128)}) while((s32[]{:T(128)}, f32[2,2,128,128]{3,2,1,0:T(8,128)S(1)}, s32[]{:T(128)}, bf16[32,2,2,128,128]{4,3,2,1,0:T(8,128)(2,1)}, ...), condition=%wide.region_3.4_spmd.clone, body=%wide.region_2.3_spmd.clone.sunk | while | flops 262152 | bytes 655523 | solution.py:20
  215.6 1.0 add_select_fusion.5
  216.7 1.0 add_select_fusion.5
  248.7 1.5 fusion.18
  250.1 1.4 fusion.19
  251.6 6.3 %fusion.3 = f32[2,256,4096]{2,1,0:T(8,128)} fusion(bf16[2,256,256]{1,2,0:T(8,128)(2,1)S(1)} %bitcast.151, bf16[4096,256]{1,0:T(8,128)(2,1)} %param.20), kind=kOutput, calls=%fused_computation.6 | convolution fusion | flops 1073741824 | bytes 10747904 | tf_op jit(solution)/shard_map/scj,dj->scd/dot_general | solution.py:90
  257.9 4.8 %fusion.1 = f32[2,256,4096]{2,1,0:T(8,128)} fusion(bf16[2,256,256]{1,2,0:T(8,128)(2,1)S(1)} %bitcast.149, bf16[4096,256]{1,0:T(8,128)(2,1)S(1)} %copy-done.4), kind=kOutput, calls=%fused_computation.4 | convolution fusion | flops 1073741824 | bytes 10747904 | tf_op jit(solution)/shard_map/scj,dj->scd/dot_general | solution.py:93
  262.7 9.4 %add_convert_fusion = bf16[2,256,4096]{2,1,0:T(8,128)(2,1)} fusion(f32[2,256,4096]{2,1,0:T(8,128)} %fusion.1, f32[2,256,4096]{2,1,0:T(8,128)S(1)} %bitcast.140, f32[2,256,4096]{2,1,0:T(8,128)} %fusion.3, bf16[2,256,256]{1,2,0:T(8,128)(2,1)S(1)} %copy-done.6, bf16[4096,256]{1,0:T(8,128)(2,1)S(1)} %copy-done.5), kind=kOutput, calls=%fused_computation.2 | convolution fusion | flops 1082130432 | bytes 31719424 | tf_op jit(solution)/shard_map/scj,dj->scd/dot_general | solution.py:96
  272.2 37.5 %reduce-scatter.2.cloned.1.call-done = bf16[2,256,512]{2,1,0:T(8,128)(2,1)} async-done(((bf16[2,256,4096]{2,1,0:T(8,128)(2,1)}), bf16[2,256,512]{2,1,0:T(8,128)(2,1)}) %reduce-scatter.2.cloned.1.call-update) | async-done | bytes 524304 | tf_op jit(solution)/shard_map/reduce_scatter | solution.py:99
  (74 shorter events, 42.1 us)
Async XLA Ops:
  6.5 135.3 %copy-start = (bf16[4096,256]{1,0:T(8,128)(2,1)S(1)}, bf16[4096,256]{1,0:T(8,128)(2,1)}, u32[]{:S(2)}) copy-start(bf16[4096,256]{1,0:T(8,128)(2,1)} %param.19) | copy-start | bytes 6291460
  6.5 120.4 %copy-start.2 = (bf16[2,256,256]{2,1,0:T(8,128)(2,1)S(1)}, bf16[2,256,256]{2,1,0:T(8,128)(2,1)}, u32[]{:S(2)}) copy-start(bf16[2,256,256]{2,1,0:T(8,128)(2,1)} %param.14) | copy-start | bytes 786436
  6.5 86.3 %all-gather.8.cloned.1.call-start = ((), (), s32[]{:S(2)}) async-start(), calls=%async_computation.3 | async-start | bytes 4325376 | tf_op jit(solution)/shard_map/all_gather | solution.py:11
  9.7 120.1 %all-gather.6.cloned.1.call-start = ((), (), s32[]{:S(2)}) async-start(), calls=%async_computation.1 | async-start | bytes 4718592 | tf_op jit(solution)/shard_map/all_gather | solution.py:34
  10.4 204.1 %all-gather.10.cloned.1.call-start = ((), (), s32[]{:S(2)}) async-start(), calls=%async_computation.4 | async-start | bytes 4325376 | tf_op jit(solution)/shard_map/all_gather | solution.py:11
  10.5 1.8 copy-start.7
  13.7 0.8 copy-start.3
  134.8 6.4 %copy-start.1 = (bf16[2,256,256]{2,1,0:T(8,128)(2,1)S(1)}, bf16[2,256,256]{2,1,0:T(8,128)(2,1)}, u32[]{:S(2)}) copy-start(bf16[2,256,256]{2,1,0:T(8,128)(2,1)} %param.15) | copy-start | bytes 786436
  135.8 173.9 %reduce-scatter.2.cloned.1.call-start = ((), (), s32[]{:S(2)}) async-start(), calls=%async_computation.2 | async-start | bytes 4718592 | tf_op jit(solution)/shard_map/reduce_scatter | solution.py:99
  251.5 6.3 %copy-start.4 = (bf16[4096,256]{1,0:T(8,128)(2,1)S(1)}, bf16[4096,256]{1,0:T(8,128)(2,1)}, u32[]{:S(2)}) copy-start(bf16[4096,256]{1,0:T(8,128)(2,1)} %param.21) | copy-start | bytes 6291460
  251.6 11.2 %slice-start = ((s8[8388608]{0:T(1024)(128)(4,1)}), s8[4194304]{0:T(1024)(128)(4,1)S(1)}, s32[]{:S(2)}) async-start(s8[8388608]{0:T(1024)(128)(4,1)} %bitcast.139), calls=%async_computation.5 | async-start | bytes 8388608
  257.9 4.8 %slice-start.1 = ((s8[8388608]{0:T(1024)(128)(4,1)}), s8[4194304]{0:T(1024)(128)(4,1)S(1)}, s32[]{:S(2)}) async-start(s8[8388608]{0:T(1024)(128)(4,1)} %bitcast.139), calls=%async_computation.6 | async-start | bytes 8388608
  257.9 4.8 %copy-start.5 = (bf16[4096,256]{1,0:T(8,128)(2,1)S(1)}, bf16[4096,256]{1,0:T(8,128)(2,1)}, u32[]{:S(2)}) copy-start(bf16[4096,256]{1,0:T(8,128)(2,1)} %param.22) | copy-start | bytes 6291460
  257.9 4.8 %copy-start.6 = (bf16[2,256,256]{1,2,0:T(8,128)(2,1)S(1)}, bf16[2,256,256]{1,2,0:T(8,128)(2,1)}, u32[]{:S(2)}) copy-start(bf16[2,256,256]{1,2,0:T(8,128)(2,1)} %get-tuple-element.246) | copy-start | bytes 786436
Sparse Core Ops, SparseCore 0:
  10.0 82.8 all-gather.7
  94.7 35.0 all-gather.5
  135.9 78.6 all-gather.9
  272.3 37.3 reduce-scatter.1
where the time goes:
time: 320 us; the launch traced here: 316 us
  waiting for transfers between devices  186 us (58%)
  other arithmetic  66.5 us (21%)
  matrix products  44 us (14%)
  between operations  13.3 us (4%)
  local copies, waits for them, and re-layouts  4.7 us (1%)
    all_gather x2, waiting for transfers between devices, entering(): everything = lax.all_gather(x.astype(jnp.bfloat16), axis)  146 us
    select_n x64, other arithmetic, step(): return jnp.where(reached, new, before)  66.5 us
    reduce_scatter x1, waiting for transfers between devices, body(): lax.psum_scatter(partial_sum.astype(jnp.bfloat16), 'head', scatter_dimens...  37.5 us
    dot_general x1, matrix products, body(): jnp.einsum('scj,dj->scd', d_gate, w_gate, preferred_element_type=jnp.floa...  9.45 us
  transfers between devices with their start and end apart: 4, of which 4 were waited for; matrix products, arithmetic and copies ran while one was open for 15% of the time, Pallas kernels for 0%

commit v1 on v0

v1 whole, which is shorter than its diff:
```python
import jax
import jax.numpy as jnp
from jax import lax
from jax.experimental import pallas as pl
from jax.experimental.pallas import tpu as pltpu
from jax.sharding import PartitionSpec as P

HD = 128
VMEM_LIMIT = 32 * 1024 * 1024
RELATIVE = (0, -1, 1, 2)


def params():
    return pltpu.CompilerParams(vmem_limit_bytes=VMEM_LIMIT)


def cost(flops, moved):
    return pl.CostEstimate(flops=int(flops), bytes_accessed=int(moved), transcendentals=0)


def mm(a, b, over_a, over_b):
    return lax.dot_general(
        a, b, (((over_a,), (over_b,)), ((), ())), preferred_element_type=jnp.float32
    )


def nn(a, b):
    return mm(a, b, 1, 0)


def nt(a, b):
    return mm(a, b, 1, 1)


def tn(a, b):
    return mm(a, b, 0, 0)


def whole(shape):
    return pl.BlockSpec(shape, lambda *at: (0,) * len(shape))


def key_state_kernel(k_ref, v_ref, out_ref):
    for s in range(out_ref.shape[0]):
        for h in range(out_ref.shape[1]):
            cols = slice(h * HD, (h + 1) * HD)
            out_ref[s, h] = tn(k_ref[s, :, cols], v_ref[s, :, cols]).astype(out_ref.dtype)


def pick_kernel(table_ref, w_ref, out_ref):
    out_ref[0] = w_ref[...]


def gated_start_kernel(table_ref, g_ref, a0, a1, b0, b1, w_ref, wo_ref, mine_ref, other_ref):
    k = pl.program_id(0)

    @pl.when(k == 0)
    def _():
        for s in range(2):
            mine_ref[s] = nt(g_ref[s], w_ref[...])
            other_ref[s] = nt(g_ref[s], wo_ref[0])

    for at, pair in ((1, (a0, a1)), (2, (b0, b1))):

        @pl.when(k == at)
        def _(pair=pair):
            for s in range(2):
                mine_ref[s] += nt(pair[s][...], w_ref[...])
                other_ref[s] += nt(pair[s][...], wo_ref[0])


def gated_end_kernel(table_ref, mine_in, other_in, c0, c1, w_ref, wo_ref, mine_ref, other_ref):
    for s, piece in enumerate((c0, c1)):
        other_ref[s] = other_in[s] + nt(piece[...], wo_ref[0])
        mine_ref[s] = mine_in[s] + nt(piece[...], w_ref[...])


def gate_kernel(mine_ref, theirs_ref, gate_ref, q_ref, d_out_ref, slope_ref, state_ref):
    for s in range(2):
        d_gated = mine_ref[s] + theirs_ref[s]
        gate_open = jax.nn.sigmoid(gate_ref[s].astype(jnp.float32))
        d_output = d_gated * gate_open
        rounded = d_output.astype(jnp.bfloat16)
        d_out_ref[s] = rounded
        slope_ref[s] = d_output * (1.0 - gate_open)
        for h in range(state_ref.shape[1]):
            cols = slice(h * HD, (h + 1) * HD)
            state_ref[s, h] = tn(q_ref[s, :, cols], rounded[:, cols]).astype(state_ref.dtype)


def make_inner_kernel(factor):
    def inner_kernel(q_ref, k_ref, v_ref, d_out_ref, slope_ref, prefix_ref, dq_ref, dg_ref, dk_ref, dv_ref):
        q, k, v, d_out = q_ref[0], k_ref[0], v_ref[0], d_out_ref[0]
        prefix = prefix_ref[0, 0]
        rows = q.shape[0]
        causal = lax.broadcasted_iota(jnp.int32, (rows, rows), 0) >= lax.broadcasted_iota(
            jnp.int32, (rows, rows), 1
        )
        scores = jnp.where(causal, nt(q, k), 0.0).astype(jnp.bfloat16)
        backward = jnp.where(causal, nt(d_out, v), 0.0).astype(jnp.bfloat16)
        attended = factor * (nn(q, prefix) + nn(scores, v))
        dg_ref[0] = (slope_ref[0] * attended).astype(jnp.bfloat16)
        dq_ref[0] = (factor * (nt(d_out, prefix) + nn(backward, k))).astype(jnp.bfloat16)
        dk_ref[0] = tn(backward, q)
        dv_ref[0] = tn(scores, d_out)

    return inner_kernel


def make_project_kernel(factor):
    def project_kernel(
        table_ref, dq_ref, dg_ref, dk_part, dv_part, k_ref, v_ref, suffix_ref, wq, wk, wv, wg, out_ref, dk_sc, dv_sc
    ):
        seq_count, rows, columns = k_ref.shape

        @pl.when(pl.program_id(0) == 0)
        def _():
            for s in range(seq_count):
                for h in range(columns // HD):
                    cols = slice(h * HD, (h + 1) * HD)
                    suffix = suffix_ref[s, h]
                    dk_sc[s, :, cols] = (
                        factor * (dk_part[s, :, cols] + nt(v_ref[s, :, cols], suffix))
                    ).astype(jnp.bfloat16)
                    dv_sc[s, :, cols] = (
                        factor * (dv_part[s, :, cols] + nn(k_ref[s, :, cols], suffix))
                    ).astype(jnp.bfloat16)

        for s in range(seq_count):
            total = nt(dq_ref[s], wq[...]) + nt(dk_sc[s], wk[...])
            total = total + nt(dv_sc[s], wv[...]) + nt(dg_ref[s], wg[...])
            out_ref[0, s] = total.astype(jnp.bfloat16)

    return project_kernel


def across_seq(state, reverse):
    peers, here = lax.axis_size("seq"), lax.axis_index("seq")

    def swap(x, by):
        return lax.ppermute(x, "seq", [(i, i ^ by) for i in range(peers)])

    def counted(x, bit):
        take = (here & bit) == 0 if reverse else (here & bit) != 0
        return jnp.where(take, x.astype(jnp.float32), 0.0)

    total, entering = state, jnp.zeros(state.shape, jnp.float32)
    for bit in (1, 2, 4):
        theirs = swap(total, bit)
        entering = entering + counted(theirs, bit)
        total = (total.astype(jnp.float32) + theirs.astype(jnp.float32)).astype(jnp.bfloat16)
    swapped = [swap(total, by) for by in (8, 16, 24)]
    for theirs, bit in zip(swapped, (8, 16, 16)):
        entering = entering + counted(theirs, bit)
    return entering.astype(jnp.bfloat16)


def body(queries, keys, values, gate_pre, grad_out, w_query, w_key, w_value, w_gate, w_out):
    seq_count, rows, columns = queries.shape
    head_count = columns // HD
    features = grad_out.shape[2]
    peers = lax.axis_size("head")
    ring = peers // 2
    factor = (lax.axis_size("seq") * rows) ** (-0.5)
    bf16, f32 = jnp.bfloat16, jnp.float32
    state_shape = (seq_count, head_count, HD, HD)
    cube = (seq_count, rows, columns)

    here = lax.axis_index("head")
    y, lane = here // 2, here % 2
    places = jnp.arange(8, dtype=jnp.int32)
    offset = places % 4
    offset = jnp.where(offset == 1, ring - 1, jnp.where(offset == 2, 1, jnp.where(offset == 3, 2, 0)))
    table = 2 * ((y + offset) % ring) + jnp.where(places < 4, 1 - lane, lane)
    table = table.astype(jnp.int32)

    def along_y(x, by):
        return lax.ppermute(x, "head", [(i, (i + 2 * by) % peers) for i in range(peers)])

    def other_core(x):
        return lax.ppermute(x, "head", [(i, i ^ 1) for i in range(peers)])

    g0, g1 = grad_out[0], grad_out[1]
    a0 = along_y(g0, 1)
    b1 = along_y(g1, -1)
    a1 = along_y(g1, 1)
    b0 = along_y(g0, -1)
    c0 = along_y(a0, 1)
    c1 = along_y(b1, -1)

    w_pick = pl.pallas_call(
        pick_kernel,
        out_shape=jax.ShapeDtypeStruct((4, columns, features), bf16),
        grid_spec=pltpu.PrefetchScalarGridSpec(
            num_scalar_prefetch=1,
            grid=(4,),
            in_specs=[pl.BlockSpec((columns, features), lambda k, t: (0, t[k]))],
            out_specs=pl.BlockSpec((1, columns, features), lambda k, t: (k, 0, 0)),
        ),
        compiler_params=params(),
        cost_estimate=cost(0, 2 * 4 * columns * features * 2),
    )(table, w_out)
    w_theirs = other_core(w_pick)

    key_state = pl.pallas_call(
        key_state_kernel,
        out_shape=jax.ShapeDtypeStruct(state_shape, bf16),
        compiler_params=params(),
        cost_estimate=cost(2 * seq_count * rows * columns * HD, 4 * seq_count * rows * columns),
    )(keys, values)
    prefix = across_seq(key_state, False)

    flat = (rows, features)
    two = [jax.ShapeDtypeStruct(cube, f32)] * 2
    piece_flops = 4 * seq_count * rows * features * columns
    mine, other = pl.pallas_call(
        gated_start_kernel,
        out_shape=two,
        grid_spec=pltpu.PrefetchScalarGridSpec(
            num_scalar_prefetch=1,
            grid=(3,),
            in_specs=[whole(grad_out.shape)]
            + [whole(flat)] * 4
            + [
                pl.BlockSpec((columns, features), lambda k, t: (0, t[4 + k])),
                pl.BlockSpec((1, columns, features), lambda k, t: (k, 0, 0)),
            ],
            out_specs=[whole(cube)] * 2,
        ),
        compiler_params=params(),
        cost_estimate=cost(3 * piece_flops, 4 * 1024 * 1024),
    )(table, grad_out, a0, a1, b0, b1, w_out, w_theirs)
    mine, other = pl.pallas_call(
        gated_end_kernel,
        out_shape=two,
        grid_spec=pltpu.PrefetchScalarGridSpec(
            num_scalar_prefetch=1,
            grid=(1,),
            in_specs=[whole(cube)] * 2
            + [whole(flat)] * 2
            + [
                pl.BlockSpec((columns, features), lambda k, t: (0, t[7])),
                pl.BlockSpec((1, columns, features), lambda k, t: (3, 0, 0)),
            ],
            out_specs=[whole(cube)] * 2,
        ),
        compiler_params=params(),
        cost_estimate=cost(piece_flops, 3 * 1024 * 1024),
    )(table, mine, other, c0, c1, w_out, w_theirs)
    theirs = other_core(other)

    d_output, slope, query_state = pl.pallas_call(
        gate_kernel,
        out_shape=[
            jax.ShapeDtypeStruct(cube, bf16),
            jax.ShapeDtypeStruct(cube, f32),
            jax.ShapeDtypeStruct(state_shape, bf16),
        ],
        compiler_params=params(),
        cost_estimate=cost(2 * seq_count * rows * columns * HD, 3 * 1024 * 1024),
    )(mine, theirs, gate_pre, queries)
    suffix = across_seq(query_state, True)

    block = pl.BlockSpec((1, rows, HD), lambda s, h: (s, 0, h))
    d_query, d_gate, dk_part, dv_part = pl.pallas_call(
        make_inner_kernel(factor),
        out_shape=[jax.ShapeDtypeStruct(cube, kind) for kind in (bf16, bf16, f32, f32)],
        grid=(seq_count, head_count),
        in_specs=[block] * 5 + [pl.BlockSpec((1, 1, HD, HD), lambda s, h: (s, h, 0, 0))],
        out_specs=[block] * 4,
        compiler_params=params(),
        cost_estimate=cost(12 * seq_count * rows * rows * columns, 3 * 1024 * 1024),
    )(queries, keys, values, d_output, slope, prefix)

    def project(first):
        weight = pl.BlockSpec((features, columns), lambda k, t: (t[first + k], 0))
        return pl.pallas_call(
            make_project_kernel(factor),
            out_shape=jax.ShapeDtypeStruct((4, seq_count, rows, features), bf16),
            grid_spec=pltpu.PrefetchScalarGridSpec(
                num_scalar_prefetch=1,
                grid=(4,),
                in_specs=[whole(cube)] * 6 + [whole(state_shape)] + [weight] * 4,
                out_specs=pl.BlockSpec((1, seq_count, rows, features), lambda k, t: (k, 0, 0, 0)),
                scratch_shapes=[pltpu.VMEM(cube, bf16)] * 2,
            ),
            compiler_params=params(),
            cost_estimate=cost(32 * seq_count * rows * columns * features, 8 * 1024 * 1024),
        )(table, d_query, d_gate, dk_part, dv_part, keys, values, suffix, w_query, w_key, w_value, w_gate)

    theirs = other_core(project(0))
    own = project(4)

    def chip(place, s):
        return own[place, s].astype(f32) + theirs[place, s].astype(f32)

    up_far = along_y(chip(3, 0).astype(bf16), 1)
    down_far = along_y(chip(3, 1).astype(bf16), -1)
    up_near = along_y(chip(2, 1).astype(bf16), 1)
    down_near = along_y(chip(1, 0).astype(bf16), -1)
    up_last = along_y((chip(2, 0) + up_far.astype(f32)).astype(bf16), 1)
    down_last = along_y((chip(1, 1) + down_far.astype(f32)).astype(bf16), -1)
    out0 = chip(0, 0) + down_near.astype(f32) + up_last.astype(f32)
    out1 = chip(0, 1) + up_near.astype(f32) + down_last.astype(f32)
    return jnp.stack([out0, out1]).astype(bf16)


def solution(mesh):
    tokens = P(None, "seq", "head")
    return jax.shard_map(
        body,
        mesh=mesh,
        in_specs=(tokens,) * 5 + (P(None, "head"),) * 4 + (P("head", None),),
        out_specs=tokens,
        check_vma=False,
    )
```

time: 320 us -> 113 us (0.35)
  the two profiles are of different devices: /device:TPU:1 before, /device:TPU:6 now
where the time goes in v1:
time: 113 us; the launch traced here: 112 us
  waiting for transfers between devices  45 us (40%)
  starting transfers between devices  43.5 us (38%)
  Pallas kernels  16.9 us (15%)
  other arithmetic  3.98 us (4%)
  local copies, waits for them, and re-layouts  2.73 us (2%)
    ppermute x12, waiting for transfers between devices, along_y(): lax.ppermute(x, 'head', [(i, (i + 2 * by) % peers) for i in range(peers)])  28.6 us
    ppermute x12, starting transfers between devices, swap(): return lax.ppermute(x, 'seq', [(i, i ^ by) for i in range(peers)])  26.1 us
    ppermute x12, starting transfers between devices, along_y(): lax.ppermute(x, 'head', [(i, (i + 2 * by) % peers) for i in range(peers)])  17.2 us
    ppermute x12, waiting for transfers between devices, swap(): return lax.ppermute(x, 'seq', [(i, i ^ by) for i in range(peers)])  16.2 us
    pallas_call x2, Pallas kernels, project(): pl.pallas_call(make_project_kernel(factor), out_shape=jax.ShapeDtypeStruc...  7.8 us
    unnamed x20, local copies, waits for them, and re-layouts  2.7 us
    pallas_call x1, Pallas kernels, body(): pl.pallas_call(make_inner_kernel(factor), out_shape=[jax.ShapeDtypeStruct...  2.55 us
  transfers between devices with their start and end apart: 27, of which 15 were waited for; matrix products, arithmetic and copies ran while one was open for 2% of the time, Pallas kernels for 9%

profile of v1, /device:TPU:6, one launch (start us, length us, event | category | flops | bytes accessed | tf_op | source)
XLA Modules:
  0.0 112.4 jit_solution(16276668636369652204)
XLA Ops:
  0.0 1.6 %copy-done = bf16[256,4096]{1,0:T(8,128)(2,1)S(1)} copy-done((bf16[256,4096]{1,0:T(8,128)(2,1)S(1)}, bf16[256,4096]{1,0:T(8,128)(2,1)}, u32[]{:S(2)}) %copy-start) | copy-done | bytes 2097176
  1.6 0.8 shard_map.100
  2.7 1.7 %collective-permute-start = (bf16[256,512]{1,0:T(8,128)(2,1)S(1)}, bf16[256,512]{1,0:T(8,128)(2,1)S(1)}, u32[]{:S(2)}, u32[]{:S(2)}) collective-permute-start(bf16[256,512]{1,0:T(8,128)(2,1)S(1)} %get-tuple-element.34), channel_id=1, source_target_pairs={{0,2},{1,3},{2,4},{3,5},{4,6},{5,7},{6,0},{7,1},{8,10},{9,11},{10,... | collective-permute-start | bytes 786440 | tf_op jit(solution)/shard_map/ppermute | solution.py:178
  4.4 1.7 %collective-permute-start.3 = (bf16[256,512]{1,0:T(8,128)(2,1)S(1)}, bf16[256,512]{1,0:T(8,128)(2,1)S(1)}, u32[]{:S(2)}, u32[]{:S(2)}) collective-permute-start(bf16[256,512]{1,0:T(8,128)(2,1)S(1)} %get-tuple-element.33), channel_id=1, source_target_pairs={{0,6},{1,7},{2,0},{3,1},{4,2},{5,3},{6,4},{7,5},{8,14},{9,15},{10,... | collective-permute-start | bytes 786440 | tf_op jit(solution)/shard_map/ppermute | solution.py:178
  6.0 0.4 collective-permute-start.1
  6.4 2.9 %collective-permute-start.2 = (bf16[256,512]{1,0:T(8,128)(2,1)S(1)}, bf16[256,512]{1,0:T(8,128)(2,1)S(1)}, u32[]{:S(2)}, u32[]{:S(2)}) collective-permute-start(bf16[256,512]{1,0:T(8,128)(2,1)S(1)} %get-tuple-element.34), channel_id=1, source_target_pairs={{0,6},{1,7},{2,0},{3,1},{4,2},{5,3},{6,4},{7,5},{8,14},{9,15},{10,... | collective-permute-start | bytes 786440 | tf_op jit(solution)/shard_map/ppermute | solution.py:178
  9.3 3.9 %collective-permute-done.a0 = bf16[256,512]{1,0:T(8,128)(2,1)S(1)} collective-permute-done((bf16[256,512]{1,0:T(8,128)(2,1)S(1)}, bf16[256,512]{1,0:T(8,128)(2,1)S(1)}, u32[]{:S(2)}, u32[]{:S(2)}) %collective-permute-start) | collective-permute-done | bytes 262176 | tf_op jit(solution)/shard_map/ppermute | solution.py:178
  13.1 0.4 collective-permute-start.5
  13.5 2.8 %collective-permute-start.6 = (bf16[256,512]{1,0:T(8,128)(2,1)S(1)}, bf16[256,512]{1,0:T(8,128)(2,1)S(1)}, u32[]{:S(2)}, u32[]{:S(2)}) collective-permute-start(bf16[256,512]{1,0:T(8,128)(2,1)S(1)} %collective-permute-done.3.b1), channel_id=1, source_target_pairs={{0,6},{1,7},{2,0},{3,1},{4,2},{5,3},{6,4},{7,5},{8,14},{9,15},{10,... | collective-permute-start | bytes 786440 | tf_op jit(solution)/shard_map/ppermute | solution.py:178
  16.4 2.4 %collective-permute-done.1.a1 = bf16[256,512]{1,0:T(8,128)(2,1)S(1)} collective-permute-done((bf16[256,512]{1,0:T(8,128)(2,1)S(1)}, bf16[256,512]{1,0:T(8,128)(2,1)S(1)}, u32[]{:S(2)}, u32[]{:S(2)}) %collective-permute-start.1) | collective-permute-done | bytes 262176 | tf_op jit(solution)/shard_map/ppermute | solution.py:178
  18.7 0.4 collective-permute-done.2.b0
  19.1 2.1 %shard_map.101 = (f32[2,256,256]{2,1,0:T(8,128)S(1)}, f32[2,256,256]{2,1,0:T(8,128)S(1)}) custom-call(s32[8]{0:T(128)S(1)} %fusion.32.table_ref, bf16[2,256,512]{2,1,0:T(8,128)(2,1)S(1)} %copy-done.7, bf16[256,512]{1,0:T(8,128)(2,1)S(1)} %collective-permute-done.a0, bf16[256,512]{1,0:T(8,128)(2,1)S(1)} %collective-permute-done.1.a1, ...), custom_call_target="tpu_custom_call" | custom-call | flops 805306368 | bytes 4194304 | tf_op jit(solution)/shard_map/pallas_call | solution.py:216
  21.3 2.6 %collective-permute-done.5.c0 = bf16[256,512]{1,0:T(8,128)(2,1)S(1)} collective-permute-done((bf16[256,512]{1,0:T(8,128)(2,1)S(1)}, bf16[256,512]{1,0:T(8,128)(2,1)S(1)}, u32[]{:S(2)}, u32[]{:S(2)}) %collective-permute-start.5) | collective-permute-done | bytes 262176 | tf_op jit(solution)/shard_map/ppermute | solution.py:178
  23.9 1.8 %shard_map.102 = (f32[2,256,256]{2,1,0:T(8,128)S(1)}, f32[2,256,256]{2,1,0:T(8,128)}) custom-call(s32[8]{0:T(128)S(1)} %fusion.32.table_ref, f32[2,256,256]{2,1,0:T(8,128)S(1)} %get-tuple-element.16.mine_in, f32[2,256,256]{2,1,0:T(8,128)S(1)} %get-tuple-element.17.other_in, bf16[256,512]{1,0:T(8,128)(2,1)S(1)} %collective-permute-done.5.c0, ...), custom_call_target="tpu_custom_call" | custom-call | flops 268435456 | bytes 3145728 | tf_op jit(solution)/shard_map/pallas_call | solution.py:233
  26.0 2.0 %collective-permute-start.8 = (bf16[2,2,128,128]{3,2,1,0:T(8,128)(2,1)S(1)}, bf16[2,2,128,128]{3,2,1,0:T(8,128)(2,1)}, u32[]{:S(2)}, u32[]{:S(2)}) collective-permute-start(bf16[2,2,128,128]{3,2,1,0:T(8,128)(2,1)S(1)} %shard_map.104), channel_id=1, source_target_pairs={{0,8},{8,0},{16,24},{24,16},{32,40},{40,32},{48,56},{56,48},{64,72... | collective-permute-start | bytes 393224 | tf_op jit(solution)/shard_map/ppermute | solution.py:141
  28.0 0.9 copy-done.9
  29.0 1.5 %shard_map.103 = (bf16[2,256,256]{2,1,0:T(8,128)(2,1)S(1)}, f32[2,256,256]{2,1,0:T(8,128)S(1)}, bf16[2,2,128,128]{3,2,1,0:T(8,128)(2,1)S(1)}) custom-call(f32[2,256,256]{2,1,0:T(8,128)S(1)} %get-tuple-element.18.mine_ref, f32[2,256,256]{2,1,0:T(8,128)} %collective-permute-done.7.theirs_ref, bf16[2,256,256]{2,1,0:T(8,128)(2,1)S(1)} %copy-done.9, ...), custom_call_target="tpu_custom_call" | custom-call | flops 33554432 | bytes 3145728 | tf_op jit(solution)/shard_map/pallas_call | solution.py:252
  30.5 2.0 %collective-permute-start.14 = (bf16[2,2,128,128]{3,2,1,0:T(8,128)(2,1)S(1)}, bf16[2,2,128,128]{3,2,1,0:T(8,128)(2,1)S(1)}, u32[]{:S(2)}, u32[]{:S(2)}) collective-permute-start(bf16[2,2,128,128]{3,2,1,0:T(8,128)(2,1)S(1)} %get-tuple-element.26), channel_id=1, source_target_pairs={{0,8},{8,0},{16,24},{24,16},{32,40},{40,32},{48,56},{56,48},{64,72... | collective-permute-start | bytes 393224 | tf_op jit(solution)/shard_map/ppermute | solution.py:141
  32.5 0.9 fusion.12
  33.4 3.4 %collective-permute-start.9 = (bf16[2,2,128,128]{3,2,1,0:T(8,128)(2,1)S(1)}, bf16[2,2,128,128]{3,2,1,0:T(8,128)(2,1)S(1)}, u32[]{:S(2)}, u32[]{:S(2)}) collective-permute-start(bf16[2,2,128,128]{3,2,1,0:T(8,128)(2,1)S(1)} %fusion.12), channel_id=1, source_target_pairs={{0,16},{8,24},{16,0},{24,8},{32,48},{40,56},{48,32},{56,40},{64,80... | collective-permute-start | bytes 393224 | tf_op jit(solution)/shard_map/ppermute | solution.py:141
  36.8 3.4 %collective-permute-start.15 = (bf16[2,2,128,128]{3,2,1,0:T(8,128)(2,1)S(1)}, bf16[2,2,128,128]{3,2,1,0:T(8,128)(2,1)S(1)}, u32[]{:S(2)}, u32[]{:S(2)}) collective-permute-start(bf16[2,2,128,128]{3,2,1,0:T(8,128)(2,1)S(1)} %fusion.21), channel_id=1, source_target_pairs={{0,16},{8,24},{16,0},{24,8},{32,48},{40,56},{48,32},{56,40},{64,80... | collective-permute-start | bytes 393224 | tf_op jit(solution)/shard_map/ppermute | solution.py:141
  40.2 6.5 %collective-permute-done.9 = bf16[2,2,128,128]{3,2,1,0:T(8,128)(2,1)S(1)} collective-permute-done((bf16[2,2,128,128]{3,2,1,0:T(8,128)(2,1)S(1)}, bf16[2,2,128,128]{3,2,1,0:T(8,128)(2,1)S(1)}, u32[]{:S(2)}, u32[]{:S(2)}) %collective-permute-start.9) | collective-permute-done | bytes 131104 | tf_op jit(solution)/shard_map/ppermute | solution.py:141
  46.7 6.1 %collective-permute-start.10 = (bf16[2,2,128,128]{3,2,1,0:T(8,128)(2,1)S(1)}, bf16[2,2,128,128]{3,2,1,0:T(8,128)(2,1)S(1)}, u32[]{:S(2)}, u32[]{:S(2)}) collective-permute-start(bf16[2,2,128,128]{3,2,1,0:T(8,128)(2,1)S(1)} %fusion.13), channel_id=1, source_target_pairs={{0,32},{8,40},{16,48},{24,56},{32,0},{40,8},{48,16},{56,24},{64,96... | collective-permute-start | bytes 393224 | tf_op jit(solution)/shard_map/ppermute | solution.py:141
  52.9 2.1 %collective-permute-start.16 = (bf16[2,2,128,128]{3,2,1,0:T(8,128)(2,1)S(1)}, bf16[2,2,128,128]{3,2,1,0:T(8,128)(2,1)S(1)}, u32[]{:S(2)}, u32[]{:S(2)}) collective-permute-start(bf16[2,2,128,128]{3,2,1,0:T(8,128)(2,1)S(1)} %fusion.22), channel_id=1, source_target_pairs={{0,32},{8,40},{16,48},{24,56},{32,0},{40,8},{48,16},{56,24},{64,96... | collective-permute-start | bytes 393224 | tf_op jit(solution)/shard_map/ppermute | solution.py:141
  55.0 5.4 %collective-permute-done.10 = bf16[2,2,128,128]{3,2,1,0:T(8,128)(2,1)S(1)} collective-permute-done((bf16[2,2,128,128]{3,2,1,0:T(8,128)(2,1)S(1)}, bf16[2,2,128,128]{3,2,1,0:T(8,128)(2,1)S(1)}, u32[]{:S(2)}, u32[]{:S(2)}) %collective-permute-start.10) | collective-permute-done | bytes 131104 | tf_op jit(solution)/shard_map/ppermute | solution.py:141
  60.6 2.9 %collective-permute-start.12 = (bf16[2,2,128,128]{3,2,1,0:T(8,128)(2,1)S(1)}, bf16[2,2,128,128]{3,2,1,0:T(8,128)(2,1)S(1)}, u32[]{:S(2)}, u32[]{:S(2)}) collective-permute-start(bf16[2,2,128,128]{3,2,1,0:T(8,128)(2,1)S(1)} %fusion.14), channel_id=1, source_target_pairs={{0,128},{8,136},{16,144},{24,152},{32,160},{40,168},{48,176},{56,1... | collective-permute-start | bytes 393224 | tf_op jit(solution)/shard_map/ppermute | solution.py:141
  63.5 1.2 %collective-permute-start.11 = (bf16[2,2,128,128]{3,2,1,0:T(8,128)(2,1)S(1)}, bf16[2,2,128,128]{3,2,1,0:T(8,128)(2,1)S(1)}, u32[]{:S(2)}, u32[]{:S(2)}) collective-permute-start(bf16[2,2,128,128]{3,2,1,0:T(8,128)(2,1)S(1)} %fusion.14), channel_id=1, source_target_pairs={{0,64},{8,72},{16,80},{24,88},{32,96},{40,104},{48,112},{56,120},{... | collective-permute-start | bytes 393224 | tf_op jit(solution)/shard_map/ppermute | solution.py:141
  64.7 0.4 collective-permute-start.19
  65.1 2.6 %collective-permute-start.18 = (bf16[2,2,128,128]{3,2,1,0:T(8,128)(2,1)S(1)}, bf16[2,2,128,128]{3,2,1,0:T(8,128)(2,1)S(1)}, u32[]{:S(2)}, u32[]{:S(2)}) collective-permute-start(bf16[2,2,128,128]{3,2,1,0:T(8,128)(2,1)S(1)} %fusion.23), channel_id=1, source_target_pairs={{0,128},{8,136},{16,144},{24,152},{32,160},{40,168},{48,176},{56,1... | collective-permute-start | bytes 393224 | tf_op jit(solution)/shard_map/ppermute | solution.py:141
  67.7 3.0 %collective-permute-done.13 = bf16[2,2,128,128]{3,2,1,0:T(8,128)(2,1)S(1)} collective-permute-done((bf16[2,2,128,128]{3,2,1,0:T(8,128)(2,1)S(1)}, bf16[2,2,128,128]{3,2,1,0:T(8,128)(2,1)S(1)}, u32[]{:S(2)}, u32[]{:S(2)}) %collective-permute-start.13) | collective-permute-done | bytes 131104 | tf_op jit(solution)/shard_map/ppermute | solution.py:141
  70.7 1.2 %collective-permute-done.11 = bf16[2,2,128,128]{3,2,1,0:T(8,128)(2,1)S(1)} collective-permute-done((bf16[2,2,128,128]{3,2,1,0:T(8,128)(2,1)S(1)}, bf16[2,2,128,128]{3,2,1,0:T(8,128)(2,1)S(1)}, u32[]{:S(2)}, u32[]{:S(2)}) %collective-permute-start.11) | collective-permute-done | bytes 131104 | tf_op jit(solution)/shard_map/ppermute | solution.py:141
  71.8 1.1 fusion.11.prefix_ref
  72.9 2.5 %shard_map.105 = (bf16[2,256,256]{2,1,0:T(8,128)(2,1)S(1)}, bf16[2,256,256]{2,1,0:T(8,128)(2,1)S(1)}, f32[2,256,256]{2,1,0:T(8,128)S(1)}, f32[2,256,256]{2,1,0:T(8,128)S(1)}) custom-call(bf16[2,256,256]{2,1,0:T(8,128)(2,1)S(1)} %copy-done.8, bf16[2,256,256]{2,1,0:T(8,128)(2,1)S(1)} %copy-done.5, bf16[2,256,256]{2,1,0:T(8,128)(2,1)S(1)} %copy-done.6, ...), custom_call_target="tpu_custom_call" | custom-call | flops 402653184 | bytes 3145728 | tf_op jit(solution)/shard_map/pallas_call | solution.py:265
  75.8 3.9 %shard_map.107 = bf16[4,2,256,512]{3,2,1,0:T(8,128)(2,1)S(1)} custom-call(s32[8]{0:T(128)S(1)} %fusion.32.table_ref, bf16[2,256,256]{2,1,0:T(8,128)(2,1)S(1)} %get-tuple-element.22.dq_ref, bf16[2,256,256]{2,1,0:T(8,128)(2,1)S(1)} %get-tuple-element.23.dg_ref, f32[2,256,256]{2,1,0:T(8,128)S(1)} %get-tuple-element.24.dk_part, ...), custom_call_target="tpu_custom_call" | custom-call | flops 2147483648 | bytes 8388608 | tf_op jit(solution)/shard_map/pallas_call | solution.py:277
  79.8 3.9 %shard_map.106 = bf16[4,2,256,512]{3,2,1,0:T(8,128)(2,1)S(1)} custom-call(s32[8]{0:T(128)S(1)} %fusion.32.table_ref, bf16[2,256,256]{2,1,0:T(8,128)(2,1)S(1)} %get-tuple-element.22.dq_ref, bf16[2,256,256]{2,1,0:T(8,128)(2,1)S(1)} %get-tuple-element.23.dg_ref, f32[2,256,256]{2,1,0:T(8,128)S(1)} %get-tuple-element.24.dk_part, ...), custom_call_target="tpu_custom_call" | custom-call | flops 2147483648 | bytes 8388608 | tf_op jit(solution)/shard_map/pallas_call | solution.py:277
  84.0 0.3 fusion.24
  84.3 1.7 %collective-permute-start.22 = (bf16[256,512]{1,0:T(8,128)(2,1)S(1)}, bf16[256,512]{1,0:T(8,128)(2,1)S(1)}, u32[]{:S(2)}, u32[]{:S(2)}) collective-permute-start(bf16[256,512]{1,0:T(8,128)(2,1)S(1)} %get-tuple-element.32), channel_id=1, source_target_pairs={{0,2},{1,3},{2,4},{3,5},{4,6},{5,7},{6,0},{7,1},{8,10},{9,11},{10,... | collective-permute-start | bytes 786440 | tf_op jit(solution)/shard_map/ppermute | solution.py:178
  86.0 1.6 %collective-permute-start.21 = (bf16[256,512]{1,0:T(8,128)(2,1)S(1)}, bf16[256,512]{1,0:T(8,128)(2,1)S(1)}, u32[]{:S(2)}, u32[]{:S(2)}) collective-permute-start(bf16[256,512]{1,0:T(8,128)(2,1)S(1)} %get-tuple-element.29), channel_id=1, source_target_pairs={{0,6},{1,7},{2,0},{3,1},{4,2},{5,3},{6,4},{7,5},{8,14},{9,15},{10,... | collective-permute-start | bytes 786440 | tf_op jit(solution)/shard_map/ppermute | solution.py:178
  87.6 1.8 %collective-permute-start.25 = (bf16[256,512]{1,0:T(8,128)(2,1)S(1)}, bf16[256,512]{1,0:T(8,128)(2,1)S(1)}, u32[]{:S(2)}, u32[]{:S(2)}) collective-permute-start(bf16[256,512]{1,0:T(8,128)(2,1)S(1)} %get-tuple-element.30), channel_id=1, source_target_pairs={{0,6},{1,7},{2,0},{3,1},{4,2},{5,3},{6,4},{7,5},{8,14},{9,15},{10,... | collective-permute-start | bytes 786440 | tf_op jit(solution)/shard_map/ppermute | solution.py:178
  89.4 4.7 %collective-permute-done.22 = bf16[256,512]{1,0:T(8,128)(2,1)S(1)} collective-permute-done((bf16[256,512]{1,0:T(8,128)(2,1)S(1)}, bf16[256,512]{1,0:T(8,128)(2,1)S(1)}, u32[]{:S(2)}, u32[]{:S(2)}) %collective-permute-start.22) | collective-permute-done | bytes 262176 | tf_op jit(solution)/shard_map/ppermute | solution.py:178
  94.2 0.4 collective-permute-start.23
  94.6 1.3 %collective-permute-start.24 = (bf16[256,512]{1,0:T(8,128)(2,1)S(1)}, bf16[256,512]{1,0:T(8,128)(2,1)S(1)}, u32[]{:S(2)}, u32[]{:S(2)}) collective-permute-start(bf16[256,512]{1,0:T(8,128)(2,1)S(1)} %get-tuple-element.31), channel_id=1, source_target_pairs={{0,2},{1,3},{2,4},{3,5},{4,6},{5,7},{6,0},{7,1},{8,10},{9,11},{10,... | collective-permute-start | bytes 786440 | tf_op jit(solution)/shard_map/ppermute | solution.py:178
  95.9 3.9 %collective-permute-done.25 = bf16[256,512]{1,0:T(8,128)(2,1)S(1)} collective-permute-done((bf16[256,512]{1,0:T(8,128)(2,1)S(1)}, bf16[256,512]{1,0:T(8,128)(2,1)S(1)}, u32[]{:S(2)}, u32[]{:S(2)}) %collective-permute-start.25) | collective-permute-done | bytes 262176 | tf_op jit(solution)/shard_map/ppermute | solution.py:178
  99.8 4.9 %collective-permute-done.23 = bf16[256,512]{1,0:T(8,128)(2,1)S(1)} collective-permute-done((bf16[256,512]{1,0:T(8,128)(2,1)S(1)}, bf16[256,512]{1,0:T(8,128)(2,1)S(1)}, u32[]{:S(2)}, u32[]{:S(2)}) %collective-permute-start.23) | collective-permute-done | bytes 262176 | tf_op jit(solution)/shard_map/ppermute | solution.py:178
  105.0 0.6 collective-permute-start.26
  105.6 3.2 %collective-permute-done.24 = bf16[256,512]{1,0:T(8,128)(2,1)S(1)} collective-permute-done((bf16[256,512]{1,0:T(8,128)(2,1)S(1)}, bf16[256,512]{1,0:T(8,128)(2,1)S(1)}, u32[]{:S(2)}, u32[]{:S(2)}) %collective-permute-start.24) | collective-permute-done | bytes 262176 | tf_op jit(solution)/shard_map/ppermute | solution.py:178
  108.8 2.6 %collective-permute-done.26 = bf16[256,512]{1,0:T(8,128)(2,1)S(1)} collective-permute-done((bf16[256,512]{1,0:T(8,128)(2,1)S(1)}, bf16[256,512]{1,0:T(8,128)(2,1)S(1)}, u32[]{:S(2)}, u32[]{:S(2)}) %collective-permute-start.26) | collective-permute-done | bytes 262176 | tf_op jit(solution)/shard_map/ppermute | solution.py:178
  111.6 0.8 pad_maximum_fusion
  (49 shorter events, 2.1 us)
Async XLA Ops:
  0.0 1.6 %copy-start = (bf16[256,4096]{1,0:T(8,128)(2,1)S(1)}, bf16[256,4096]{1,0:T(8,128)(2,1)}, u32[]{:S(2)}) copy-start(bf16[256,4096]{1,0:T(8,128)(2,1)} %w_ref.5) | copy-start | bytes 6291460
  1.6 1.0 copy-start.7
  2.4 16.7 %collective-permute-start.4 = (bf16[4,256,512]{2,1,0:T(8,128)(2,1)S(1)}, bf16[4,256,512]{2,1,0:T(8,128)(2,1)S(1)}, u32[]{:S(2)}, u32[]{:S(2)}) collective-permute-start(bf16[4,256,512]{2,1,0:T(8,128)(2,1)S(1)} %shard_map.100), channel_id=1, source_target_pairs={{0,1},{1,0},{2,3},{3,2},{4,5},{5,4},{6,7},{7,6},{8,9},{9,8},{10,11... | collective-permute-start | bytes 3145736 | tf_op jit(solution)/shard_map/ppermute | solution.py:181
  2.7 10.4 %collective-permute-start = (bf16[256,512]{1,0:T(8,128)(2,1)S(1)}, bf16[256,512]{1,0:T(8,128)(2,1)S(1)}, u32[]{:S(2)}, u32[]{:S(2)}) collective-permute-start(bf16[256,512]{1,0:T(8,128)(2,1)S(1)} %get-tuple-element.34), channel_id=1, source_target_pairs={{0,2},{1,3},{2,4},{3,5},{4,6},{5,7},{6,0},{7,1},{8,10},{9,11},{10,... | collective-permute-start | bytes 786440 | tf_op jit(solution)/shard_map/ppermute | solution.py:178
  4.4 9.2 %collective-permute-start.3 = (bf16[256,512]{1,0:T(8,128)(2,1)S(1)}, bf16[256,512]{1,0:T(8,128)(2,1)S(1)}, u32[]{:S(2)}, u32[]{:S(2)}) collective-permute-start(bf16[256,512]{1,0:T(8,128)(2,1)S(1)} %get-tuple-element.33), channel_id=1, source_target_pairs={{0,6},{1,7},{2,0},{3,1},{4,2},{5,3},{6,4},{7,5},{8,14},{9,15},{10,... | collective-permute-start | bytes 786440 | tf_op jit(solution)/shard_map/ppermute | solution.py:178
  6.0 12.7 %collective-permute-start.1 = (bf16[256,512]{1,0:T(8,128)(2,1)S(1)}, bf16[256,512]{1,0:T(8,128)(2,1)S(1)}, u32[]{:S(2)}, u32[]{:S(2)}) collective-permute-start(bf16[256,512]{1,0:T(8,128)(2,1)S(1)} %get-tuple-element.33), channel_id=1, source_target_pairs={{0,2},{1,3},{2,4},{3,5},{4,6},{5,7},{6,0},{7,1},{8,10},{9,11},{10,... | collective-permute-start | bytes 786440 | tf_op jit(solution)/shard_map/ppermute | solution.py:178
  6.4 12.8 %collective-permute-start.2 = (bf16[256,512]{1,0:T(8,128)(2,1)S(1)}, bf16[256,512]{1,0:T(8,128)(2,1)S(1)}, u32[]{:S(2)}, u32[]{:S(2)}) collective-permute-start(bf16[256,512]{1,0:T(8,128)(2,1)S(1)} %get-tuple-element.34), channel_id=1, source_target_pairs={{0,6},{1,7},{2,0},{3,1},{4,2},{5,3},{6,4},{7,5},{8,14},{9,15},{10,... | collective-permute-start | bytes 786440 | tf_op jit(solution)/shard_map/ppermute | solution.py:178
  13.1 10.8 %collective-permute-start.5 = (bf16[256,512]{1,0:T(8,128)(2,1)S(1)}, bf16[256,512]{1,0:T(8,128)(2,1)S(1)}, u32[]{:S(2)}, u32[]{:S(2)}) collective-permute-start(bf16[256,512]{1,0:T(8,128)(2,1)S(1)} %collective-permute-done.a0), channel_id=1, source_target_pairs={{0,2},{1,3},{2,4},{3,5},{4,6},{5,7},{6,0},{7,1},{8,10},{9,11},{10,... | collective-permute-start | bytes 786440 | tf_op jit(solution)/shard_map/ppermute | solution.py:178
  13.5 10.4 %collective-permute-start.6 = (bf16[256,512]{1,0:T(8,128)(2,1)S(1)}, bf16[256,512]{1,0:T(8,128)(2,1)S(1)}, u32[]{:S(2)}, u32[]{:S(2)}) collective-permute-start(bf16[256,512]{1,0:T(8,128)(2,1)S(1)} %collective-permute-done.3.b1), channel_id=1, source_target_pairs={{0,6},{1,7},{2,0},{3,1},{4,2},{5,3},{6,4},{7,5},{8,14},{9,15},{10,... | collective-permute-start | bytes 786440 | tf_op jit(solution)/shard_map/ppermute | solution.py:178
  23.9 1.8 %copy-start.5 = (bf16[2,256,256]{2,1,0:T(8,128)(2,1)S(1)}, bf16[2,256,256]{2,1,0:T(8,128)(2,1)}, u32[]{:S(2)}) copy-start(bf16[2,256,256]{2,1,0:T(8,128)(2,1)} %k_ref.7) | copy-start | bytes 786436
  23.9 1.8 %copy-start.6 = (bf16[2,256,256]{2,1,0:T(8,128)(2,1)S(1)}, bf16[2,256,256]{2,1,0:T(8,128)(2,1)}, u32[]{:S(2)}) copy-start(bf16[2,256,256]{2,1,0:T(8,128)(2,1)} %v_ref.7) | copy-start | bytes 786436
  23.9 4.1 %copy-start.8 = (bf16[2,256,256]{2,1,0:T(8,128)(2,1)S(1)}, bf16[2,256,256]{2,1,0:T(8,128)(2,1)}, u32[]{:S(2)}) copy-start(bf16[2,256,256]{2,1,0:T(8,128)(2,1)} %q_ref.3) | copy-start | bytes 786436
  23.9 51.9 %copy-start.4 = (bf16[4096,256]{1,0:T(8,128)(2,1)S(1)}, bf16[4096,256]{1,0:T(8,128)(2,1)}, u32[]{:S(2)}) copy-start(bf16[4096,256]{1,0:T(8,128)(2,1)} %wg.3) | copy-start | bytes 6291460
  25.7 2.3 %collective-permute-start.7 = (f32[2,256,256]{2,1,0:T(8,128)}, f32[2,256,256]{2,1,0:T(8,128)}, u32[]{:S(2)}, u32[]{:S(2)}) collective-permute-start(f32[2,256,256]{2,1,0:T(8,128)} %get-tuple-element.19), channel_id=1, source_target_pairs={{0,1},{1,0},{2,3},{3,2},{4,5},{5,4},{6,7},{7,6},{8,9},{9,8},{10,11... | collective-permute-start | bytes 1572872 | tf_op jit(solution)/shard_map/ppermute | solution.py:181
  26.0 6.5 %collective-permute-start.8 = (bf16[2,2,128,128]{3,2,1,0:T(8,128)(2,1)S(1)}, bf16[2,2,128,128]{3,2,1,0:T(8,128)(2,1)}, u32[]{:S(2)}, u32[]{:S(2)}) collective-permute-start(bf16[2,2,128,128]{3,2,1,0:T(8,128)(2,1)S(1)} %shard_map.104), channel_id=1, source_target_pairs={{0,8},{8,0},{16,24},{24,16},{32,40},{40,32},{48,56},{56,48},{64,72... | collective-permute-start | bytes 393224 | tf_op jit(solution)/shard_map/ppermute | solution.py:141
  28.0 1.0 copy-start.9
  28.9 46.8 %copy-start.3 = (bf16[4096,256]{1,0:T(8,128)(2,1)S(1)}, bf16[4096,256]{1,0:T(8,128)(2,1)}, u32[]{:S(2)}) copy-start(bf16[4096,256]{1,0:T(8,128)(2,1)} %wv.3) | copy-start | bytes 6291460
  30.5 6.3 %collective-permute-start.14 = (bf16[2,2,128,128]{3,2,1,0:T(8,128)(2,1)S(1)}, bf16[2,2,128,128]{3,2,1,0:T(8,128)(2,1)S(1)}, u32[]{:S(2)}, u32[]{:S(2)}) collective-permute-start(bf16[2,2,128,128]{3,2,1,0:T(8,128)(2,1)S(1)} %get-tuple-element.26), channel_id=1, source_target_pairs={{0,8},{8,0},{16,24},{24,16},{32,40},{40,32},{48,56},{56,48},{64,72... | collective-permute-start | bytes 393224 | tf_op jit(solution)/shard_map/ppermute | solution.py:141
  33.4 13.3 %collective-permute-start.9 = (bf16[2,2,128,128]{3,2,1,0:T(8,128)(2,1)S(1)}, bf16[2,2,128,128]{3,2,1,0:T(8,128)(2,1)S(1)}, u32[]{:S(2)}, u32[]{:S(2)}) collective-permute-start(bf16[2,2,128,128]{3,2,1,0:T(8,128)(2,1)S(1)} %fusion.12), channel_id=1, source_target_pairs={{0,16},{8,24},{16,0},{24,8},{32,48},{40,56},{48,32},{56,40},{64,80... | collective-permute-start | bytes 393224 | tf_op jit(solution)/shard_map/ppermute | solution.py:141
  36.8 16.1 %collective-permute-start.15 = (bf16[2,2,128,128]{3,2,1,0:T(8,128)(2,1)S(1)}, bf16[2,2,128,128]{3,2,1,0:T(8,128)(2,1)S(1)}, u32[]{:S(2)}, u32[]{:S(2)}) collective-permute-start(bf16[2,2,128,128]{3,2,1,0:T(8,128)(2,1)S(1)} %fusion.21), channel_id=1, source_target_pairs={{0,16},{8,24},{16,0},{24,8},{32,48},{40,56},{48,32},{56,40},{64,80... | collective-permute-start | bytes 393224 | tf_op jit(solution)/shard_map/ppermute | solution.py:141
  46.7 13.7 %collective-permute-start.10 = (bf16[2,2,128,128]{3,2,1,0:T(8,128)(2,1)S(1)}, bf16[2,2,128,128]{3,2,1,0:T(8,128)(2,1)S(1)}, u32[]{:S(2)}, u32[]{:S(2)}) collective-permute-start(bf16[2,2,128,128]{3,2,1,0:T(8,128)(2,1)S(1)} %fusion.13), channel_id=1, source_target_pairs={{0,32},{8,40},{16,48},{24,56},{32,0},{40,8},{48,16},{56,24},{64,96... | collective-permute-start | bytes 393224 | tf_op jit(solution)/shard_map/ppermute | solution.py:141
  52.9 22.9 %copy-start.1 = (bf16[4096,256]{1,0:T(8,128)(2,1)S(1)}, bf16[4096,256]{1,0:T(8,128)(2,1)}, u32[]{:S(2)}) copy-start(bf16[4096,256]{1,0:T(8,128)(2,1)} %wq.3) | copy-start | bytes 6291460
  52.9 22.9 %copy-start.2 = (bf16[4096,256]{1,0:T(8,128)(2,1)S(1)}, bf16[4096,256]{1,0:T(8,128)(2,1)}, u32[]{:S(2)}) copy-start(bf16[4096,256]{1,0:T(8,128)(2,1)} %wk.3) | copy-start | bytes 6291460
  52.9 11.7 %collective-permute-start.16 = (bf16[2,2,128,128]{3,2,1,0:T(8,128)(2,1)S(1)}, bf16[2,2,128,128]{3,2,1,0:T(8,128)(2,1)S(1)}, u32[]{:S(2)}, u32[]{:S(2)}) collective-permute-start(bf16[2,2,128,128]{3,2,1,0:T(8,128)(2,1)S(1)} %fusion.22), channel_id=1, source_target_pairs={{0,32},{8,40},{16,48},{24,56},{32,0},{40,8},{48,16},{56,24},{64,96... | collective-permute-start | bytes 393224 | tf_op jit(solution)/shard_map/ppermute | solution.py:141
  60.5 10.2 %collective-permute-start.13 = (bf16[2,2,128,128]{3,2,1,0:T(8,128)(2,1)S(1)}, bf16[2,2,128,128]{3,2,1,0:T(8,128)(2,1)S(1)}, u32[]{:S(2)}, u32[]{:S(2)}) collective-permute-start(bf16[2,2,128,128]{3,2,1,0:T(8,128)(2,1)S(1)} %fusion.14), channel_id=1, source_target_pairs={{0,192},{8,200},{16,208},{24,216},{32,224},{40,232},{48,240},{56,2... | collective-permute-start | bytes 393224 | tf_op jit(solution)/shard_map/ppermute | solution.py:141
  60.6 10.1 %collective-permute-start.12 = (bf16[2,2,128,128]{3,2,1,0:T(8,128)(2,1)S(1)}, bf16[2,2,128,128]{3,2,1,0:T(8,128)(2,1)S(1)}, u32[]{:S(2)}, u32[]{:S(2)}) collective-permute-start(bf16[2,2,128,128]{3,2,1,0:T(8,128)(2,1)S(1)} %fusion.14), channel_id=1, source_target_pairs={{0,128},{8,136},{16,144},{24,152},{32,160},{40,168},{48,176},{56,1... | collective-permute-start | bytes 393224 | tf_op jit(solution)/shard_map/ppermute | solution.py:141
  63.5 8.4 %collective-permute-start.11 = (bf16[2,2,128,128]{3,2,1,0:T(8,128)(2,1)S(1)}, bf16[2,2,128,128]{3,2,1,0:T(8,128)(2,1)S(1)}, u32[]{:S(2)}, u32[]{:S(2)}) collective-permute-start(bf16[2,2,128,128]{3,2,1,0:T(8,128)(2,1)S(1)} %fusion.14), channel_id=1, source_target_pairs={{0,64},{8,72},{16,80},{24,88},{32,96},{40,104},{48,112},{56,120},{... | collective-permute-start | bytes 393224 | tf_op jit(solution)/shard_map/ppermute | solution.py:141
  64.7 10.8 %collective-permute-start.19 = (bf16[2,2,128,128]{3,2,1,0:T(8,128)(2,1)S(1)}, bf16[2,2,128,128]{3,2,1,0:T(8,128)(2,1)S(1)}, u32[]{:S(2)}, u32[]{:S(2)}) collective-permute-start(bf16[2,2,128,128]{3,2,1,0:T(8,128)(2,1)S(1)} %fusion.23), channel_id=1, source_target_pairs={{0,192},{8,200},{16,208},{24,216},{32,224},{40,232},{48,240},{56,2... | collective-permute-start | bytes 393224 | tf_op jit(solution)/shard_map/ppermute | solution.py:141
  65.1 10.4 %collective-permute-start.18 = (bf16[2,2,128,128]{3,2,1,0:T(8,128)(2,1)S(1)}, bf16[2,2,128,128]{3,2,1,0:T(8,128)(2,1)S(1)}, u32[]{:S(2)}, u32[]{:S(2)}) collective-permute-start(bf16[2,2,128,128]{3,2,1,0:T(8,128)(2,1)S(1)} %fusion.23), channel_id=1, source_target_pairs={{0,128},{8,136},{16,144},{24,152},{32,160},{40,168},{48,176},{56,1... | collective-permute-start | bytes 393224 | tf_op jit(solution)/shard_map/ppermute | solution.py:141
  70.7 5.0 %collective-permute-start.17 = (bf16[2,2,128,128]{3,2,1,0:T(8,128)(2,1)S(1)}, bf16[2,2,128,128]{3,2,1,0:T(8,128)(2,1)S(1)}, u32[]{:S(2)}, u32[]{:S(2)}) collective-permute-start(bf16[2,2,128,128]{3,2,1,0:T(8,128)(2,1)S(1)} %fusion.23), channel_id=1, source_target_pairs={{0,64},{8,72},{16,80},{24,88},{32,96},{40,104},{48,112},{56,120},{... | collective-permute-start | bytes 393224 | tf_op jit(solution)/shard_map/ppermute | solution.py:141
  79.7 4.2 %collective-permute-start.20 = (bf16[4,2,256,512]{3,2,1,0:T(8,128)(2,1)S(1)}, bf16[4,2,256,512]{3,2,1,0:T(8,128)(2,1)S(1)}, u32[]{:S(2)}, u32[]{:S(2)}) collective-permute-start(bf16[4,2,256,512]{3,2,1,0:T(8,128)(2,1)S(1)} %shard_map.107), channel_id=1, source_target_pairs={{0,1},{1,0},{2,3},{3,2},{4,5},{5,4},{6,7},{7,6},{8,9},{9,8},{10,11... | collective-permute-start | bytes 6291464 | tf_op jit(solution)/shard_map/ppermute | solution.py:181
  84.3 9.8 %collective-permute-start.22 = (bf16[256,512]{1,0:T(8,128)(2,1)S(1)}, bf16[256,512]{1,0:T(8,128)(2,1)S(1)}, u32[]{:S(2)}, u32[]{:S(2)}) collective-permute-start(bf16[256,512]{1,0:T(8,128)(2,1)S(1)} %get-tuple-element.32), channel_id=1, source_target_pairs={{0,2},{1,3},{2,4},{3,5},{4,6},{5,7},{6,0},{7,1},{8,10},{9,11},{10,... | collective-permute-start | bytes 786440 | tf_op jit(solution)/shard_map/ppermute | solution.py:178
  86.0 9.9 %collective-permute-start.21 = (bf16[256,512]{1,0:T(8,128)(2,1)S(1)}, bf16[256,512]{1,0:T(8,128)(2,1)S(1)}, u32[]{:S(2)}, u32[]{:S(2)}) collective-permute-start(bf16[256,512]{1,0:T(8,128)(2,1)S(1)} %get-tuple-element.29), channel_id=1, source_target_pairs={{0,6},{1,7},{2,0},{3,1},{4,2},{5,3},{6,4},{7,5},{8,14},{9,15},{10,... | collective-permute-start | bytes 786440 | tf_op jit(solution)/shard_map/ppermute | solution.py:178
  87.6 12.2 %collective-permute-start.25 = (bf16[256,512]{1,0:T(8,128)(2,1)S(1)}, bf16[256,512]{1,0:T(8,128)(2,1)S(1)}, u32[]{:S(2)}, u32[]{:S(2)}) collective-permute-start(bf16[256,512]{1,0:T(8,128)(2,1)S(1)} %get-tuple-element.30), channel_id=1, source_target_pairs={{0,6},{1,7},{2,0},{3,1},{4,2},{5,3},{6,4},{7,5},{8,14},{9,15},{10,... | collective-permute-start | bytes 786440 | tf_op jit(solution)/shard_map/ppermute | solution.py:178
  94.2 10.5 %collective-permute-start.23 = (bf16[256,512]{1,0:T(8,128)(2,1)S(1)}, bf16[256,512]{1,0:T(8,128)(2,1)S(1)}, u32[]{:S(2)}, u32[]{:S(2)}) collective-permute-start(bf16[256,512]{1,0:T(8,128)(2,1)S(1)} %fusion.3), channel_id=1, source_target_pairs={{0,2},{1,3},{2,4},{3,5},{4,6},{5,7},{6,0},{7,1},{8,10},{9,11},{10,... | collective-permute-start | bytes 786440 | tf_op jit(solution)/shard_map/ppermute | solution.py:178
  94.6 14.2 %collective-permute-start.24 = (bf16[256,512]{1,0:T(8,128)(2,1)S(1)}, bf16[256,512]{1,0:T(8,128)(2,1)S(1)}, u32[]{:S(2)}, u32[]{:S(2)}) collective-permute-start(bf16[256,512]{1,0:T(8,128)(2,1)S(1)} %get-tuple-element.31), channel_id=1, source_target_pairs={{0,2},{1,3},{2,4},{3,5},{4,6},{5,7},{6,0},{7,1},{8,10},{9,11},{10,... | collective-permute-start | bytes 786440 | tf_op jit(solution)/shard_map/ppermute | solution.py:178
  105.0 6.4 %collective-permute-start.26 = (bf16[256,512]{1,0:T(8,128)(2,1)S(1)}, bf16[256,512]{1,0:T(8,128)(2,1)S(1)}, u32[]{:S(2)}, u32[]{:S(2)}) collective-permute-start(bf16[256,512]{1,0:T(8,128)(2,1)S(1)} %get-tuple-element.28), channel_id=1, source_target_pairs={{0,6},{1,7},{2,0},{3,1},{4,2},{5,3},{6,4},{7,5},{8,14},{9,15},{10,... | collective-permute-start | bytes 786440 | tf_op jit(solution)/shard_map/ppermute | solution.py:178

commit v2 on v1

v2 whole, which is shorter than its diff:
```python
import jax
import jax.numpy as jnp
from jax import lax
from jax.experimental import pallas as pl
from jax.experimental.pallas import tpu as pltpu
from jax.sharding import PartitionSpec as P

HD = 128
MIB = 1024 * 1024
RELATIVE = (0, -1, 1, 2)


def params(mib=8):
    return pltpu.CompilerParams(vmem_limit_bytes=mib * MIB)


def cost(flops, moved):
    return pl.CostEstimate(flops=int(flops), bytes_accessed=int(moved), transcendentals=0)


def mm(a, b, over_a, over_b):
    return lax.dot_general(
        a, b, (((over_a,), (over_b,)), ((), ())), preferred_element_type=jnp.float32
    )


def nn(a, b):
    return mm(a, b, 1, 0)


def nt(a, b):
    return mm(a, b, 1, 1)


def tn(a, b):
    return mm(a, b, 0, 0)


def whole(shape):
    return pl.BlockSpec(shape, lambda *at: (0,) * len(shape))


def key_state_kernel(k_ref, v_ref, out_ref):
    for s in range(out_ref.shape[0]):
        for h in range(out_ref.shape[1]):
            cols = slice(h * HD, (h + 1) * HD)
            out_ref[s, h] = tn(k_ref[s, :, cols], v_ref[s, :, cols]).astype(out_ref.dtype)


def pick_kernel(table_ref, w_ref, theirs_ref, own_ref, sems):
    copies = []
    for k in range(8):
        out_ref = theirs_ref if k < 4 else own_ref
        features = out_ref.shape[2]
        cols = pl.ds(pl.multiple_of(table_ref[k] * features, features), features)
        copies.append(pltpu.make_async_copy(w_ref.at[:, cols], out_ref.at[k % 4], sems.at[k]))
        copies[-1].start()
    for copy in copies:
        copy.wait()


def gated_start_kernel(g_ref, a0, a1, b0, b1, w_ref, wo_ref, mine_ref, other_ref):
    k = pl.program_id(0)

    @pl.when(k == 0)
    def _():
        for s in range(2):
            mine_ref[s] = nt(g_ref[s], w_ref[0])
            other_ref[s] = nt(g_ref[s], wo_ref[0])

    for at, pair in ((1, (a0, a1)), (2, (b0, b1))):

        @pl.when(k == at)
        def _(pair=pair):
            for s in range(2):
                mine_ref[s] += nt(pair[s][...], w_ref[0])
                other_ref[s] += nt(pair[s][...], wo_ref[0])


def gated_end_kernel(mine_in, other_in, c0, c1, w_ref, wo_ref, mine_ref, other_ref):
    for s, piece in enumerate((c0, c1)):
        other_ref[s] = other_in[s] + nt(piece[...], wo_ref[0])
        mine_ref[s] = mine_in[s] + nt(piece[...], w_ref[0])


def gate_kernel(mine_ref, theirs_ref, gate_ref, q_ref, d_out_ref, slope_ref, state_ref):
    for s in range(2):
        d_gated = mine_ref[s] + theirs_ref[s]
        gate_open = jax.nn.sigmoid(gate_ref[s].astype(jnp.float32))
        d_output = d_gated * gate_open
        rounded = d_output.astype(jnp.bfloat16)
        d_out_ref[s] = rounded
        slope_ref[s] = d_output * (1.0 - gate_open)
        for h in range(state_ref.shape[1]):
            cols = slice(h * HD, (h + 1) * HD)
            state_ref[s, h] = tn(q_ref[s, :, cols], rounded[:, cols]).astype(state_ref.dtype)


def make_inner_kernel(factor):
    def inner_kernel(q_ref, k_ref, v_ref, d_out_ref, slope_ref, prefix_ref, dq_ref, dg_ref, dk_ref, dv_ref):
        q, k, v, d_out = q_ref[0], k_ref[0], v_ref[0], d_out_ref[0]
        prefix = prefix_ref[0, 0]
        rows = q.shape[0]
        causal = lax.broadcasted_iota(jnp.int32, (rows, rows), 0) >= lax.broadcasted_iota(
            jnp.int32, (rows, rows), 1
        )
        scores = jnp.where(causal, nt(q, k), 0.0).astype(jnp.bfloat16)
        backward = jnp.where(causal, nt(d_out, v), 0.0).astype(jnp.bfloat16)
        attended = factor * (nn(q, prefix) + nn(scores, v))
        dg_ref[0] = (slope_ref[0] * attended).astype(jnp.bfloat16)
        dq_ref[0] = (factor * (nt(d_out, prefix) + nn(backward, k))).astype(jnp.bfloat16)
        dk_ref[0] = tn(backward, q)
        dv_ref[0] = tn(scores, d_out)

    return inner_kernel


def make_project_kernel(factor, first):
    def project_kernel(
        table_ref, dq_ref, dg_ref, dk_part, dv_part, k_ref, v_ref, suffix_ref,
        wq, wk, wv, wg, out_ref, dk_sc, dv_sc, held, sems,
    ):
        seq_count, rows, columns = k_ref.shape
        features = out_ref.shape[3]
        here = pl.program_id(0)

        def copies(k):
            at = pl.ds(pl.multiple_of(table_ref[first + k] * features, features), features)
            return [
                pltpu.make_async_copy(weight.at[at, :], held.at[k, i], sems.at[k, i])
                for i, weight in enumerate((wq, wk, wv, wg))
            ]

        @pl.when(here == 0)
        def _():
            for k in range(4):
                for copy in copies(k):
                    copy.start()

        @pl.when(pl.program_id(0) == 0)
        def _():
            for s in range(seq_count):
                for h in range(columns // HD):
                    cols = slice(h * HD, (h + 1) * HD)
                    suffix = suffix_ref[s, h]
                    dk_sc[s, :, cols] = (
                        factor * (dk_part[s, :, cols] + nt(v_ref[s, :, cols], suffix))
                    ).astype(jnp.bfloat16)
                    dv_sc[s, :, cols] = (
                        factor * (dv_part[s, :, cols] + nn(k_ref[s, :, cols], suffix))
                    ).astype(jnp.bfloat16)

        for copy in copies(here):
            copy.wait()
        for s in range(seq_count):
            total = nt(dq_ref[s], held[here, 0]) + nt(dk_sc[s], held[here, 1])
            total = total + nt(dv_sc[s], held[here, 2]) + nt(dg_ref[s], held[here, 3])
            out_ref[0, s] = total.astype(jnp.bfloat16)

    return project_kernel


def together(*arrays):
    return lax.optimization_barrier(arrays)


def swap(x, by):
    return lax.ppermute(x, "seq", [(i, i ^ by) for i in range(lax.axis_size("seq"))])


def counted(x, bit, reverse):
    here = lax.axis_index("seq")
    take = (here & bit) == 0 if reverse else (here & bit) != 0
    return jnp.where(take, x.astype(jnp.float32), 0.0)


def joined(total, theirs):
    return (total.astype(jnp.float32) + theirs.astype(jnp.float32)).astype(jnp.bfloat16)


def entering(received, reverse):
    total = 0.0
    for theirs, bit in zip(received, (1, 2, 4, 8, 16, 16)):
        total = total + counted(theirs, bit, reverse)
    return total.astype(jnp.bfloat16)


def make_sum_kernel(counts):
    def sum_kernel(*refs):
        terms, outs = refs[: sum(counts)], refs[sum(counts) :]
        first = 0
        for at, count in enumerate(counts):
            total = terms[first][...].astype(jnp.float32).reshape(terms[first].shape[-2:])
            for term in terms[first + 1 : first + count]:
                total = total + term[...].astype(jnp.float32).reshape(total.shape)
            if len(outs) == len(counts):
                outs[at][...] = total.astype(jnp.bfloat16)
            else:
                outs[0][at] = total.astype(jnp.bfloat16)
            first += count

    return sum_kernel


def sums(groups, shape, stacked=False):
    arrays, specs = [], []
    for group in groups:
        for term in group:
            if isinstance(term, tuple):
                array, place, s = term
                arrays.append(array)
                specs.append(pl.BlockSpec((1, 1) + shape, lambda i, at=(place, s): at + (0, 0)))
            else:
                arrays.append(term)
                specs.append(whole(shape))
    if stacked:
        outs = jax.ShapeDtypeStruct((len(groups),) + shape, jnp.bfloat16)
        out_specs = whole(outs.shape)
    else:
        outs = [jax.ShapeDtypeStruct(shape, jnp.bfloat16)] * len(groups)
        out_specs = [whole(shape)] * len(groups)
    return pl.pallas_call(
        make_sum_kernel([len(group) for group in groups]),
        out_shape=outs,
        grid=(1,),
        in_specs=specs,
        out_specs=out_specs,
        compiler_params=params(),
        cost_estimate=cost(0, (len(arrays) + len(groups)) * shape[0] * shape[1] * 2),
    )(*arrays)


def body(queries, keys, values, gate_pre, grad_out, w_query, w_key, w_value, w_gate, w_out):
    seq_count, rows, columns = queries.shape
    head_count = columns // HD
    features = grad_out.shape[2]
    peers = lax.axis_size("head")
    ring = peers // 2
    factor = (lax.axis_size("seq") * rows) ** (-0.5)
    bf16, f32 = jnp.bfloat16, jnp.float32
    state_shape = (seq_count, head_count, HD, HD)
    cube = (seq_count, rows, columns)

    here = lax.axis_index("head")
    y, lane = here // 2, here % 2
    places = jnp.arange(8, dtype=jnp.int32)
    offset = places % 4
    offset = jnp.where(offset == 1, ring - 1, jnp.where(offset == 2, 1, jnp.where(offset == 3, 2, 0)))
    table = 2 * ((y + offset) % ring) + jnp.where(places < 4, 1 - lane, lane)
    table = table.astype(jnp.int32)

    def along_y(x, by):
        return lax.ppermute(x, "head", [(i, (i + 2 * by) % peers) for i in range(peers)])

    def other_core(x):
        return lax.ppermute(x, "head", [(i, i ^ 1) for i in range(peers)])

    g0, g1 = grad_out[0], grad_out[1]
    a0 = along_y(g0, 1)
    b1 = along_y(g1, -1)
    a1 = along_y(g1, 1)
    b0 = along_y(g0, -1)

    total = pl.pallas_call(
        key_state_kernel,
        out_shape=jax.ShapeDtypeStruct(state_shape, bf16),
        compiler_params=params(),
        cost_estimate=cost(2 * seq_count * rows * columns * HD, 4 * seq_count * rows * columns),
    )(keys, values)
    seq_peers = lax.axis_size("seq")
    rows_of = [[x * 8 + z for z in range(8)] for x in range(seq_peers // 8)]
    line = lax.all_gather(total, "seq", axis_index_groups=rows_of)
    c0 = along_y(a0, 1)
    c1 = along_y(b1, -1)

    w_pick, w_own = pl.pallas_call(
        pick_kernel,
        out_shape=[jax.ShapeDtypeStruct((4, columns, features), bf16)] * 2,
        grid_spec=pltpu.PrefetchScalarGridSpec(
            num_scalar_prefetch=1,
            grid=(1,),
            in_specs=[pl.BlockSpec(memory_space=pltpu.HBM)],
            out_specs=[whole((4, columns, features))] * 2,
            scratch_shapes=[pltpu.SemaphoreType.DMA((8,))],
        ),
        compiler_params=params(),
        cost_estimate=cost(0, 2 * 8 * columns * features * 2),
    )(table, w_out)
    w_theirs = other_core(w_pick)

    flat = (rows, features)
    two = [jax.ShapeDtypeStruct(cube, f32)] * 2
    piece_flops = 4 * seq_count * rows * features * columns
    piece = pl.BlockSpec((1, columns, features), lambda k: (k, 0, 0))
    mine, other = pl.pallas_call(
        gated_start_kernel,
        out_shape=two,
        grid=(3,),
        in_specs=[whole(grad_out.shape)] + [whole(flat)] * 4 + [piece] * 2,
        out_specs=[whole(cube)] * 2,
        compiler_params=params(),
        cost_estimate=cost(3 * piece_flops, 4 * MIB),
    )(grad_out, a0, a1, b0, b1, w_own, w_theirs)
    piece = pl.BlockSpec((1, columns, features), lambda k: (3, 0, 0))
    mine, other = pl.pallas_call(
        gated_end_kernel,
        out_shape=two,
        grid=(1,),
        in_specs=[whole(cube)] * 2 + [whole(flat)] * 2 + [piece] * 2,
        out_specs=[whole(cube)] * 2,
        compiler_params=params(),
        cost_estimate=cost(piece_flops, 3 * MIB),
    )(mine, other, c0, c1, w_own, w_theirs)
    theirs = other_core(other)

    d_output, slope, query_state = pl.pallas_call(
        gate_kernel,
        out_shape=[
            jax.ShapeDtypeStruct(cube, bf16),
            jax.ShapeDtypeStruct(cube, f32),
            jax.ShapeDtypeStruct(state_shape, bf16),
        ],
        compiler_params=params(),
        cost_estimate=cost(2 * seq_count * rows * columns * HD, 3 * 1024 * 1024),
    )(mine, theirs, gate_pre, queries)
    after = [swap(query_state, 1)]
    line, after[0] = together(line, after[0])
    z = lax.axis_index("seq") % 8
    earlier = (jnp.arange(8) < z).reshape(8, 1, 1, 1, 1)
    line = line.astype(f32)
    prefix = jnp.where(earlier, line, 0.0).sum(0)
    row_total = line.sum(0).astype(bf16)
    for by, bit in ((8, 8), (16, 16), (24, 16)):
        prefix = prefix + counted(swap(row_total, by), bit, False)
    prefix = prefix.astype(bf16)
    total = joined(query_state, after[0])
    after.append(swap(total, 2))

    block = pl.BlockSpec((1, rows, HD), lambda s, h: (s, 0, h))
    d_query, d_gate, dk_part, dv_part = pl.pallas_call(
        make_inner_kernel(factor),
        out_shape=[jax.ShapeDtypeStruct(cube, kind) for kind in (bf16, bf16, f32, f32)],
        grid=(seq_count, head_count),
        in_specs=[block] * 5 + [pl.BlockSpec((1, 1, HD, HD), lambda s, h: (s, h, 0, 0))],
        out_specs=[block] * 4,
        compiler_params=params(),
        cost_estimate=cost(12 * seq_count * rows * rows * columns, 3 * 1024 * 1024),
    )(queries, keys, values, d_output, slope, prefix)

    after[1], d_query = together(after[1], d_query)
    total = joined(total, after[1])
    after.append(swap(total, 4))
    total = joined(total, after[2])
    after += [swap(total, by) for by in (8, 16, 24)]
    suffix = entering(after, True)

    def project(first):
        weight = pl.BlockSpec(memory_space=pltpu.HBM)
        return pl.pallas_call(
            make_project_kernel(factor, first),
            out_shape=jax.ShapeDtypeStruct((4, seq_count, rows, features), bf16),
            grid_spec=pltpu.PrefetchScalarGridSpec(
                num_scalar_prefetch=1,
                grid=(4,),
                in_specs=[whole(cube)] * 6 + [whole(state_shape)] + [weight] * 4,
                out_specs=pl.BlockSpec((1, seq_count, rows, features), lambda k, t: (k, 0, 0, 0)),
                scratch_shapes=[pltpu.VMEM(cube, bf16)] * 2
                + [pltpu.VMEM((4, 4, features, columns), bf16), pltpu.SemaphoreType.DMA((4, 4))],
            ),
            compiler_params=params(16),
            cost_estimate=cost(32 * seq_count * rows * columns * features, 8 * 1024 * 1024),
        )(table, d_query, d_gate, dk_part, dv_part, keys, values, suffix, w_query, w_key, w_value, w_gate)

    theirs = other_core(project(0))
    own = project(4)

    def chip(place, s):
        return [(own, place, s), (theirs, place, s)]

    far0, far1 = sums([chip(3, 0), chip(3, 1)], flat)
    up_far = along_y(far0, 1)
    down_far = along_y(far1, -1)
    near1, near0 = sums([chip(2, 1), chip(1, 0)], flat)
    up_near = along_y(near1, 1)
    down_near = along_y(near0, -1)
    (last0,) = sums([chip(2, 0) + [up_far]], flat)
    (last1,) = sums([chip(1, 1) + [down_far]], flat)
    up_last = along_y(last0, 1)
    down_last = along_y(last1, -1)
    return sums([chip(0, 0) + [down_near, up_last], chip(0, 1) + [up_near, down_last]], flat, stacked=True)


def solution(mesh):
    tokens = P(None, "seq", "head")
    return jax.shard_map(
        body,
        mesh=mesh,
        in_specs=(tokens,) * 5 + (P(None, "head"),) * 4 + (P("head", None),),
        out_specs=tokens,
        check_vma=False,
    )
```

time: 113 us -> 139 us (1.23)
  the two profiles are of different devices: /device:TPU:6 before, /device:TPU:1 now
where the time goes in v2:
time: 139 us
  starting transfers between devices  44.4 us (32%)
  waiting for transfers between devices  44.3 us (32%)
  Pallas kernels  16.7 us (12%)
  local copies, waits for them, and re-layouts  15.5 us (11%)
  between operations  13.7 us (10%)
  other arithmetic  3.93 us (3%)
    ppermute x12, waiting for transfers between devices, along_y(): lax.ppermute(x, 'head', [(i, (i + 2 * by) % peers) for i in range(peers)])  24.3 us
    ppermute x9, waiting for transfers between devices, swap(): lax.ppermute(x, 'seq', [(i, i ^ by) for i in range(lax.axis_size('seq'))])  17.2 us
    ppermute x12, starting transfers between devices, along_y(): lax.ppermute(x, 'head', [(i, (i + 2 * by) % peers) for i in range(peers)])  16.6 us
    unnamed x48, local copies, waits for them, and re-layouts  15.5 us
    ppermute x3, starting transfers between devices, other_core(): return lax.ppermute(x, 'head', [(i, i ^ 1) for i in range(peers)])  14.4 us
    ppermute x9, starting transfers between devices, swap(): lax.ppermute(x, 'seq', [(i, i ^ by) for i in range(lax.axis_size('seq'))])  13.4 us
    pallas_call x2, Pallas kernels, project(): pl.pallas_call(make_project_kernel(factor, first), out_shape=jax.ShapeDty...  8.66 us
  transfers between devices with their start and end apart: 25, of which 17 were waited for; matrix products, arithmetic and copies ran while one was open for 0% of the time, Pallas kernels for 7%

profile of v2, /device:TPU:1, one launch (start us, length us, event | category | flops | bytes accessed | tf_op | source)
XLA Modules:
  0.0 138.6 jit_solution(18283467888446720919)
XLA Ops:
  6.5 0.9 copy-done.4
  7.5 0.9 copy-done.6
  8.4 0.9 shard_map.104
  9.4 1.6 %copy-done.11 = bf16[256,4096]{1,0:T(8,128)(2,1)S(1)} copy-done((bf16[256,4096]{1,0:T(8,128)(2,1)S(1)}, bf16[256,4096]{1,0:T(8,128)(2,1)}, u32[]{:S(2)}) %copy-start.11) | copy-done | bytes 2097176
  11.8 3.3 %collective-permute-start.4 = (bf16[4,256,512]{2,1,0:T(8,128)(2,1)S(1)}, bf16[4,256,512]{2,1,0:T(8,128)(2,1)S(1)}, u32[]{:S(2)}, u32[]{:S(2)}) collective-permute-start(bf16[4,256,512]{2,1,0:T(8,128)(2,1)S(1)} %get-tuple-element.27), channel_id=1, source_target_pairs={{0,1},{1,0},{2,3},{3,2},{4,5},{5,4},{6,7},{7,6},{8,9},{9,8},{10,11... | collective-permute-start | bytes 3145736 | tf_op jit(solution)/shard_map/ppermute | solution.py:256
  15.3 2.7 %collective-permute-start.3 = (bf16[256,512]{1,0:T(8,128)(2,1)S(1)}, bf16[256,512]{1,0:T(8,128)(2,1)S(1)}, u32[]{:S(2)}, u32[]{:S(2)}) collective-permute-start(bf16[256,512]{1,0:T(8,128)(2,1)S(1)} %get-tuple-element.47), channel_id=1, source_target_pairs={{0,6},{1,7},{2,0},{3,1},{4,2},{5,3},{6,4},{7,5},{8,14},{9,15},{10,... | collective-permute-start | bytes 786440 | tf_op jit(solution)/shard_map/ppermute | solution.py:253
  18.0 2.7 %collective-permute-start.2 = (bf16[256,512]{1,0:T(8,128)(2,1)S(1)}, bf16[256,512]{1,0:T(8,128)(2,1)S(1)}, u32[]{:S(2)}, u32[]{:S(2)}) collective-permute-start(bf16[256,512]{1,0:T(8,128)(2,1)S(1)} %get-tuple-element.48), channel_id=1, source_target_pairs={{0,6},{1,7},{2,0},{3,1},{4,2},{5,3},{6,4},{7,5},{8,14},{9,15},{10,... | collective-permute-start | bytes 786440 | tf_op jit(solution)/shard_map/ppermute | solution.py:253
  20.6 3.8 %collective-permute-done.a0 = bf16[256,512]{1,0:T(8,128)(2,1)S(1)} collective-permute-done((bf16[256,512]{1,0:T(8,128)(2,1)S(1)}, bf16[256,512]{1,0:T(8,128)(2,1)S(1)}, u32[]{:S(2)}, u32[]{:S(2)}) %collective-permute-start) | collective-permute-done | bytes 262176 | tf_op jit(solution)/shard_map/ppermute | solution.py:253
  24.4 2.7 %collective-permute-start.6 = (bf16[256,512]{1,0:T(8,128)(2,1)S(1)}, bf16[256,512]{1,0:T(8,128)(2,1)S(1)}, u32[]{:S(2)}, u32[]{:S(2)}) collective-permute-start(bf16[256,512]{1,0:T(8,128)(2,1)S(1)} %collective-permute-done.3.b1), channel_id=1, source_target_pairs={{0,6},{1,7},{2,0},{3,1},{4,2},{5,3},{6,4},{7,5},{8,14},{9,15},{10,... | collective-permute-start | bytes 786440 | tf_op jit(solution)/shard_map/ppermute | solution.py:253
  27.1 3.0 %collective-permute-done.1.a1 = bf16[256,512]{1,0:T(8,128)(2,1)S(1)} collective-permute-done((bf16[256,512]{1,0:T(8,128)(2,1)S(1)}, bf16[256,512]{1,0:T(8,128)(2,1)S(1)}, u32[]{:S(2)}, u32[]{:S(2)}) %collective-permute-start.1) | collective-permute-done | bytes 262176 | tf_op jit(solution)/shard_map/ppermute | solution.py:253
  30.1 1.5 %shard_map.101 = (f32[2,256,256]{2,1,0:T(8,128)S(1)}, f32[2,256,256]{2,1,0:T(8,128)S(1)}) custom-call(bf16[2,256,512]{2,1,0:T(8,128)(2,1)S(1)} %copy-done.10, bf16[256,512]{1,0:T(8,128)(2,1)S(1)} %collective-permute-done.a0, bf16[256,512]{1,0:T(8,128)(2,1)S(1)} %collective-permute-done.1.a1, bf16[256,512]{1,0:T(8,128)(2,1)S(1)} %collective-permute-done.2.b0, ...), custom_call_target="tpu_custom_call" | custom-call | flops 805306368 | bytes 4194304 | tf_op jit(solution)/shard_map/pallas_call | solution.py:295
  31.6 4.1 %collective-permute-done.5.c0 = bf16[256,512]{1,0:T(8,128)(2,1)S(1)} collective-permute-done((bf16[256,512]{1,0:T(8,128)(2,1)S(1)}, bf16[256,512]{1,0:T(8,128)(2,1)S(1)}, u32[]{:S(2)}, u32[]{:S(2)}) %collective-permute-start.5) | collective-permute-done | bytes 262176 | tf_op jit(solution)/shard_map/ppermute | solution.py:253
  36.1 0.9 collective-permute-start.7
  37.0 1.5 %collective-permute-done.7.theirs_ref = f32[2,256,256]{2,1,0:T(8,128)S(1)} collective-permute-done((f32[2,256,256]{2,1,0:T(8,128)S(1)}, f32[2,256,256]{2,1,0:T(8,128)S(1)}, u32[]{:S(2)}, u32[]{:S(2)}) %collective-permute-start.7) | collective-permute-done | bytes 524320 | tf_op jit(solution)/shard_map/ppermute | solution.py:256
  40.4 6.6 %collective-permute-done.8 = bf16[2,2,128,128]{3,2,1,0:T(8,128)(2,1)S(1)} collective-permute-done((bf16[2,2,128,128]{3,2,1,0:T(8,128)(2,1)S(1)}, bf16[2,2,128,128]{3,2,1,0:T(8,128)(2,1)S(1)}, u32[]{:S(2)}, u32[]{:S(2)}) %collective-permute-start.8) | collective-permute-done | bytes 131104 | tf_op jit(solution)/shard_map/ppermute | solution.py:168
  47.0 1.3 all-gather.3.cloned.1.call-done
  48.3 1.5 %reduce_sum.22 = bf16[2,2,128,128]{3,2,1,0:T(8,128)(2,1)S(1)} reduce(bf16[8,2,2,128,128]{4,3,2,1,0:T(8,128)(2,1)} %bitcast.5, bf16[]{:T(256)} %constant.74.clone.1), dimensions={0}, to_apply=%region_1.2 | reduce | flops 458752 | bytes 1179650 | tf_op jit(solution)/shard_map/reduce_sum | solution.py:332
  49.8 1.1 collective-permute-start.10
  50.9 2.2 %collective-permute-start.11 = (bf16[2,2,128,128]{3,2,1,0:T(8,128)(2,1)S(1)}, bf16[2,2,128,128]{3,2,1,0:T(8,128)(2,1)S(1)}, u32[]{:S(2)}, u32[]{:S(2)}) collective-permute-start(bf16[2,2,128,128]{3,2,1,0:T(8,128)(2,1)S(1)} %reduce_sum.22), channel_id=1, source_target_pairs={{0,128},{8,136},{16,144},{24,152},{32,160},{40,168},{48,176},{56,1... | collective-permute-start | bytes 393224 | tf_op jit(solution)/shard_map/ppermute | solution.py:168
  53.8 1.2 collective-permute-start.9
  55.3 1.5 %collective-permute-done.11 = bf16[2,2,128,128]{3,2,1,0:T(8,128)(2,1)S(1)} collective-permute-done((bf16[2,2,128,128]{3,2,1,0:T(8,128)(2,1)S(1)}, bf16[2,2,128,128]{3,2,1,0:T(8,128)(2,1)S(1)}, u32[]{:S(2)}, u32[]{:S(2)}) %collective-permute-start.11) | collective-permute-done | bytes 131104 | tf_op jit(solution)/shard_map/ppermute | solution.py:168
  56.8 1.4 %collective-permute-done.12 = bf16[2,2,128,128]{3,2,1,0:T(8,128)(2,1)S(1)} collective-permute-done((bf16[2,2,128,128]{3,2,1,0:T(8,128)(2,1)S(1)}, bf16[2,2,128,128]{3,2,1,0:T(8,128)(2,1)S(1)}, u32[]{:S(2)}, u32[]{:S(2)}) %collective-permute-start.12) | collective-permute-done | bytes 131104 | tf_op jit(solution)/shard_map/ppermute | solution.py:168
  58.4 0.9 copy-done.15
  59.3 2.5 %shard_map.105 = (bf16[2,256,256]{2,1,0:T(8,128)(2,1)S(1)}, bf16[2,256,256]{2,1,0:T(8,128)(2,1)S(1)}, f32[2,256,256]{2,1,0:T(8,128)S(1)}, f32[2,256,256]{2,1,0:T(8,128)S(1)}) custom-call(bf16[2,256,256]{2,1,0:T(8,128)(2,1)S(1)} %copy-done.15, bf16[2,256,256]{2,1,0:T(8,128)(2,1)S(1)} %copy-done.5, bf16[2,256,256]{2,1,0:T(8,128)(2,1)S(1)} %copy-done.7, ...), custom_call_target="tpu_custom_call" | custom-call | flops 402653184 | bytes 3145728 | tf_op jit(solution)/shard_map/pallas_call | solution.py:340
  64.0 4.4 %collective-permute-start.13 = (bf16[2,2,128,128]{3,2,1,0:T(8,128)(2,1)S(1)}, bf16[2,2,128,128]{3,2,1,0:T(8,128)(2,1)S(1)}, u32[]{:S(2)}, u32[]{:S(2)}) collective-permute-start(bf16[2,2,128,128]{3,2,1,0:T(8,128)(2,1)S(1)} %fusion.7), channel_id=1, source_target_pairs={{0,32},{8,40},{16,48},{24,56},{32,0},{40,8},{48,16},{56,24},{64,96... | collective-permute-start | bytes 393224 | tf_op jit(solution)/shard_map/ppermute | solution.py:168
  68.4 3.7 %collective-permute-done.13 = bf16[2,2,128,128]{3,2,1,0:T(8,128)(2,1)S(1)} collective-permute-done((bf16[2,2,128,128]{3,2,1,0:T(8,128)(2,1)S(1)}, bf16[2,2,128,128]{3,2,1,0:T(8,128)(2,1)S(1)}, u32[]{:S(2)}, u32[]{:S(2)}) %collective-permute-start.13) | collective-permute-done | bytes 131104 | tf_op jit(solution)/shard_map/ppermute | solution.py:168
  74.0 1.9 %collective-permute-start.15 = (bf16[2,2,128,128]{3,2,1,0:T(8,128)(2,1)}, bf16[2,2,128,128]{3,2,1,0:T(8,128)(2,1)}, u32[]{:S(2)}, u32[]{:S(2)}) collective-permute-start(bf16[2,2,128,128]{3,2,1,0:T(8,128)(2,1)} %fusion.8), channel_id=1, source_target_pairs={{0,128},{8,136},{16,144},{24,152},{32,160},{40,168},{48,176},{56,1... | collective-permute-start | bytes 393224 | tf_op jit(solution)/shard_map/ppermute | solution.py:168
  75.8 1.5 %collective-permute-start.16 = (bf16[2,2,128,128]{3,2,1,0:T(8,128)(2,1)}, bf16[2,2,128,128]{3,2,1,0:T(8,128)(2,1)}, u32[]{:S(2)}, u32[]{:S(2)}) collective-permute-start(bf16[2,2,128,128]{3,2,1,0:T(8,128)(2,1)} %fusion.8), channel_id=1, source_target_pairs={{0,192},{8,200},{16,208},{24,216},{32,224},{40,232},{48,240},{56,2... | collective-permute-start | bytes 393224 | tf_op jit(solution)/shard_map/ppermute | solution.py:168
  77.6 2.5 %collective-permute-done.15 = bf16[2,2,128,128]{3,2,1,0:T(8,128)(2,1)} collective-permute-done((bf16[2,2,128,128]{3,2,1,0:T(8,128)(2,1)}, bf16[2,2,128,128]{3,2,1,0:T(8,128)(2,1)}, u32[]{:S(2)}, u32[]{:S(2)}) %collective-permute-start.15) | collective-permute-done | bytes 131104 | tf_op jit(solution)/shard_map/ppermute | solution.py:168
  80.1 1.2 collective-permute-done.16
  81.3 1.3 fusion.6.suffix_ref
  82.7 1.6 %copy-done.1 = bf16[4096,256]{1,0:T(8,128)(2,1)S(1)} copy-done((bf16[4096,256]{1,0:T(8,128)(2,1)S(1)}, bf16[4096,256]{1,0:T(8,128)(2,1)}, u32[]{:S(2)}) %copy-start.1) | copy-done | bytes 2097176
  84.3 1.6 %copy-done.2 = bf16[4096,256]{1,0:T(8,128)(2,1)S(1)} copy-done((bf16[4096,256]{1,0:T(8,128)(2,1)S(1)}, bf16[4096,256]{1,0:T(8,128)(2,1)}, u32[]{:S(2)}) %copy-start.2) | copy-done | bytes 2097176
  85.8 1.6 %copy-done.3 = bf16[4096,256]{1,0:T(8,128)(2,1)S(1)} copy-done((bf16[4096,256]{1,0:T(8,128)(2,1)S(1)}, bf16[4096,256]{1,0:T(8,128)(2,1)}, u32[]{:S(2)}) %copy-start.3) | copy-done | bytes 2097176
  87.4 1.0 copy-done.9
  88.5 0.9 copy-done.13
  89.4 4.3 %shard_map.107 = bf16[4,2,256,512]{3,2,1,0:T(8,128)(2,1)S(1)} custom-call(s32[8]{0:T(128)S(1)} %fusion.11.table_ref, bf16[2,256,256]{2,1,0:T(8,128)(2,1)S(1)} %get-tuple-element.38.dq_ref, bf16[2,256,256]{2,1,0:T(8,128)(2,1)S(1)} %copy-done.13, f32[2,256,256]{2,1,0:T(8,128)S(1)} %get-tuple-element.40.dk_part, f32[2,256,256]{2,1,0:T(8,128)S(1)} %copy-done.9, ...), custom_call_target="tpu_custom_call" | custom-call | flops 2147483648 | bytes 8388608 | tf_op jit(solution)/shard_map/pallas_call | solution.py:359
  93.8 10.2 %collective-permute-start.17 = (bf16[4,2,256,512]{3,2,1,0:T(8,128)(2,1)S(1)}, bf16[4,2,256,512]{3,2,1,0:T(8,128)(2,1)S(1)}, u32[]{:S(2)}, u32[]{:S(2)}) collective-permute-start(bf16[4,2,256,512]{3,2,1,0:T(8,128)(2,1)S(1)} %shard_map.107), channel_id=1, source_target_pairs={{0,1},{1,0},{2,3},{3,2},{4,5},{5,4},{6,7},{7,6},{8,9},{9,8},{10,11... | collective-permute-start | bytes 6291464 | tf_op jit(solution)/shard_map/ppermute | solution.py:256
  104.0 4.3 %shard_map.106.refs_0_.refs_2_.refs_4_ = bf16[4,2,256,512]{3,2,1,0:T(8,128)(2,1)S(1)} custom-call(s32[8]{0:T(128)S(1)} %fusion.11.table_ref, bf16[2,256,256]{2,1,0:T(8,128)(2,1)S(1)} %get-tuple-element.38.dq_ref, bf16[2,256,256]{2,1,0:T(8,128)(2,1)S(1)} %copy-done.13, f32[2,256,256]{2,1,0:T(8,128)S(1)} %get-tuple-element.40.dk_part, ...), custom_call_target="tpu_custom_call" | custom-call | flops 2147483648 | bytes 8388608 | tf_op jit(solution)/shard_map/pallas_call | solution.py:359
  108.4 2.2 %collective-permute-start.22 = (bf16[256,512]{1,0:T(8,128)(2,1)S(1)}, bf16[256,512]{1,0:T(8,128)(2,1)S(1)}, u32[]{:S(2)}, u32[]{:S(2)}) collective-permute-start(bf16[256,512]{1,0:T(8,128)(2,1)S(1)} %get-tuple-element.46), channel_id=1, source_target_pairs={{0,6},{1,7},{2,0},{3,1},{4,2},{5,3},{6,4},{7,5},{8,14},{9,15},{10,... | collective-permute-start | bytes 786440 | tf_op jit(solution)/shard_map/ppermute | solution.py:253
  110.8 2.8 %collective-permute-start.18 = (bf16[256,512]{1,0:T(8,128)(2,1)S(1)}, bf16[256,512]{1,0:T(8,128)(2,1)S(1)}, u32[]{:S(2)}, u32[]{:S(2)}) collective-permute-start(bf16[256,512]{1,0:T(8,128)(2,1)S(1)} %get-tuple-element.43), channel_id=1, source_target_pairs={{0,6},{1,7},{2,0},{3,1},{4,2},{5,3},{6,4},{7,5},{8,14},{9,15},{10,... | collective-permute-start | bytes 786440 | tf_op jit(solution)/shard_map/ppermute | solution.py:253
  113.5 2.9 %collective-permute-done.22.refs_2_ = bf16[256,512]{1,0:T(8,128)(2,1)S(1)} collective-permute-done((bf16[256,512]{1,0:T(8,128)(2,1)S(1)}, bf16[256,512]{1,0:T(8,128)(2,1)S(1)}, u32[]{:S(2)}, u32[]{:S(2)}) %collective-permute-start.22) | collective-permute-done | bytes 262176 | tf_op jit(solution)/shard_map/ppermute | solution.py:253
  116.5 3.4 %collective-permute-start.23 = (bf16[256,512]{1,0:T(8,128)(2,1)S(1)}, bf16[256,512]{1,0:T(8,128)(2,1)S(1)}, u32[]{:S(2)}, u32[]{:S(2)}) collective-permute-start(bf16[256,512]{1,0:T(8,128)(2,1)S(1)} %shard_map.111), channel_id=1, source_target_pairs={{0,6},{1,7},{2,0},{3,1},{4,2},{5,3},{6,4},{7,5},{8,14},{9,15},{10,... | collective-permute-start | bytes 786440 | tf_op jit(solution)/shard_map/ppermute | solution.py:253
  120.2 1.9 %collective-permute-done.18.refs_2_ = bf16[256,512]{1,0:T(8,128)(2,1)S(1)} collective-permute-done((bf16[256,512]{1,0:T(8,128)(2,1)S(1)}, bf16[256,512]{1,0:T(8,128)(2,1)S(1)}, u32[]{:S(2)}, u32[]{:S(2)}) %collective-permute-start.18) | collective-permute-done | bytes 262176 | tf_op jit(solution)/shard_map/ppermute | solution.py:253
  122.1 3.0 %collective-permute-done.21.refs_6_ = bf16[256,512]{1,0:T(8,128)(2,1)S(1)} collective-permute-done((bf16[256,512]{1,0:T(8,128)(2,1)S(1)}, bf16[256,512]{1,0:T(8,128)(2,1)S(1)}, u32[]{:S(2)}, u32[]{:S(2)}) %collective-permute-start.21) | collective-permute-done | bytes 262176 | tf_op jit(solution)/shard_map/ppermute | solution.py:253
  125.1 2.6 %collective-permute-done.23.refs_7_ = bf16[256,512]{1,0:T(8,128)(2,1)S(1)} collective-permute-done((bf16[256,512]{1,0:T(8,128)(2,1)S(1)}, bf16[256,512]{1,0:T(8,128)(2,1)S(1)}, u32[]{:S(2)}, u32[]{:S(2)}) %collective-permute-start.23) | collective-permute-done | bytes 262176 | tf_op jit(solution)/shard_map/ppermute | solution.py:253
  127.7 3.0 %collective-permute-done.20.refs_3_ = bf16[256,512]{1,0:T(8,128)(2,1)S(1)} collective-permute-done((bf16[256,512]{1,0:T(8,128)(2,1)S(1)}, bf16[256,512]{1,0:T(8,128)(2,1)S(1)}, u32[]{:S(2)}, u32[]{:S(2)}) %collective-permute-start.20) | collective-permute-done | bytes 262176 | tf_op jit(solution)/shard_map/ppermute | solution.py:253
  130.7 1.0 shard_map.112
  (74 shorter events, 9.3 us)
Async XLA Ops:
  6.5 41.8 %all-gather.3.cloned.1.call-start = ((), (), s32[]{:S(2)}) async-start(), calls=%async_computation | async-start | bytes 1179648 | tf_op jit(solution)/shard_map/all_gather | solution.py:272
  6.5 0.9 copy-start.4
  7.5 0.9 copy-start.6
  8.4 6.7 %copy-start.10 = (bf16[2,256,512]{2,1,0:T(8,128)(2,1)S(1)}, bf16[2,256,512]{2,1,0:T(8,128)(2,1)}, u32[]{:S(2)}) copy-start(bf16[2,256,512]{2,1,0:T(8,128)(2,1)} %g_ref.1) | copy-start | bytes 1572868
  9.4 1.6 %copy-start.11 = (bf16[256,4096]{1,0:T(8,128)(2,1)S(1)}, bf16[256,4096]{1,0:T(8,128)(2,1)}, u32[]{:S(2)}) copy-start(bf16[256,4096]{1,0:T(8,128)(2,1)} %w_ref.1) | copy-start | bytes 6291460
  11.8 18.2 %collective-permute-start.4 = (bf16[4,256,512]{2,1,0:T(8,128)(2,1)S(1)}, bf16[4,256,512]{2,1,0:T(8,128)(2,1)S(1)}, u32[]{:S(2)}, u32[]{:S(2)}) collective-permute-start(bf16[4,256,512]{2,1,0:T(8,128)(2,1)S(1)} %get-tuple-element.27), channel_id=1, source_target_pairs={{0,1},{1,0},{2,3},{3,2},{4,5},{5,4},{6,7},{7,6},{8,9},{9,8},{10,11... | collective-permute-start | bytes 3145736 | tf_op jit(solution)/shard_map/ppermute | solution.py:256
  15.2 9.2 %collective-permute-start = (bf16[256,512]{1,0:T(8,128)(2,1)S(1)}, bf16[256,512]{1,0:T(8,128)(2,1)S(1)}, u32[]{:S(2)}, u32[]{:S(2)}) collective-permute-start(bf16[256,512]{1,0:T(8,128)(2,1)S(1)} %get-tuple-element.48), channel_id=1, source_target_pairs={{0,2},{1,3},{2,4},{3,5},{4,6},{5,7},{6,0},{7,1},{8,10},{9,11},{10,... | collective-permute-start | bytes 786440 | tf_op jit(solution)/shard_map/ppermute | solution.py:253
  15.3 9.1 %collective-permute-start.3 = (bf16[256,512]{1,0:T(8,128)(2,1)S(1)}, bf16[256,512]{1,0:T(8,128)(2,1)S(1)}, u32[]{:S(2)}, u32[]{:S(2)}) collective-permute-start(bf16[256,512]{1,0:T(8,128)(2,1)S(1)} %get-tuple-element.47), channel_id=1, source_target_pairs={{0,6},{1,7},{2,0},{3,1},{4,2},{5,3},{6,4},{7,5},{8,14},{9,15},{10,... | collective-permute-start | bytes 786440 | tf_op jit(solution)/shard_map/ppermute | solution.py:253
  18.0 12.1 %collective-permute-start.1 = (bf16[256,512]{1,0:T(8,128)(2,1)S(1)}, bf16[256,512]{1,0:T(8,128)(2,1)S(1)}, u32[]{:S(2)}, u32[]{:S(2)}) collective-permute-start(bf16[256,512]{1,0:T(8,128)(2,1)S(1)} %get-tuple-element.47), channel_id=1, source_target_pairs={{0,2},{1,3},{2,4},{3,5},{4,6},{5,7},{6,0},{7,1},{8,10},{9,11},{10,... | collective-permute-start | bytes 786440 | tf_op jit(solution)/shard_map/ppermute | solution.py:253
  18.0 12.1 %collective-permute-start.2 = (bf16[256,512]{1,0:T(8,128)(2,1)S(1)}, bf16[256,512]{1,0:T(8,128)(2,1)S(1)}, u32[]{:S(2)}, u32[]{:S(2)}) collective-permute-start(bf16[256,512]{1,0:T(8,128)(2,1)S(1)} %get-tuple-element.48), channel_id=1, source_target_pairs={{0,6},{1,7},{2,0},{3,1},{4,2},{5,3},{6,4},{7,5},{8,14},{9,15},{10,... | collective-permute-start | bytes 786440 | tf_op jit(solution)/shard_map/ppermute | solution.py:253
  24.4 11.2 %collective-permute-start.5 = (bf16[256,512]{1,0:T(8,128)(2,1)S(1)}, bf16[256,512]{1,0:T(8,128)(2,1)S(1)}, u32[]{:S(2)}, u32[]{:S(2)}) collective-permute-start(bf16[256,512]{1,0:T(8,128)(2,1)S(1)} %collective-permute-done.a0), channel_id=1, source_target_pairs={{0,2},{1,3},{2,4},{3,5},{4,6},{5,7},{6,0},{7,1},{8,10},{9,11},{10,... | collective-permute-start | bytes 786440 | tf_op jit(solution)/shard_map/ppermute | solution.py:253
  24.4 11.2 %collective-permute-start.6 = (bf16[256,512]{1,0:T(8,128)(2,1)S(1)}, bf16[256,512]{1,0:T(8,128)(2,1)S(1)}, u32[]{:S(2)}, u32[]{:S(2)}) collective-permute-start(bf16[256,512]{1,0:T(8,128)(2,1)S(1)} %collective-permute-done.3.b1), channel_id=1, source_target_pairs={{0,6},{1,7},{2,0},{3,1},{4,2},{5,3},{6,4},{7,5},{8,14},{9,15},{10,... | collective-permute-start | bytes 786440 | tf_op jit(solution)/shard_map/ppermute | solution.py:253
  31.6 7.0 %copy-start.14 = (bf16[2,256,256]{2,1,0:T(8,128)(2,1)S(1)}, bf16[2,256,256]{2,1,0:T(8,128)(2,1)}, u32[]{:S(2)}) copy-start(bf16[2,256,256]{2,1,0:T(8,128)(2,1)} %q_ref.3) | copy-start | bytes 786436
  31.6 7.0 %copy-start.18 = (bf16[2,256,256]{2,1,0:T(8,128)(2,1)S(1)}, bf16[2,256,256]{2,1,0:T(8,128)(2,1)}, u32[]{:S(2)}) copy-start(bf16[2,256,256]{2,1,0:T(8,128)(2,1)} %gate_ref.1) | copy-start | bytes 786436
  36.1 2.4 %collective-permute-start.7 = (f32[2,256,256]{2,1,0:T(8,128)S(1)}, f32[2,256,256]{2,1,0:T(8,128)S(1)}, u32[]{:S(2)}, u32[]{:S(2)}) collective-permute-start(f32[2,256,256]{2,1,0:T(8,128)S(1)} %get-tuple-element.31), channel_id=1, source_target_pairs={{0,1},{1,0},{2,3},{3,2},{4,5},{5,4},{6,7},{7,6},{8,9},{9,8},{10,11... | collective-permute-start | bytes 1572872 | tf_op jit(solution)/shard_map/ppermute | solution.py:256
  38.9 0.8 copy-start.16
  39.7 0.7 copy-start.19
  40.4 17.9 %copy-start.5 = (bf16[2,256,256]{2,1,0:T(8,128)(2,1)S(1)}, bf16[2,256,256]{2,1,0:T(8,128)(2,1)}, u32[]{:S(2)}) copy-start(bf16[2,256,256]{2,1,0:T(8,128)(2,1)} %k_ref.7) | copy-start | bytes 786436
  40.4 17.9 %copy-start.7 = (bf16[2,256,256]{2,1,0:T(8,128)(2,1)S(1)}, bf16[2,256,256]{2,1,0:T(8,128)(2,1)}, u32[]{:S(2)}) copy-start(bf16[2,256,256]{2,1,0:T(8,128)(2,1)} %v_ref.7) | copy-start | bytes 786436
  40.4 6.6 %collective-permute-start.8 = (bf16[2,2,128,128]{3,2,1,0:T(8,128)(2,1)S(1)}, bf16[2,2,128,128]{3,2,1,0:T(8,128)(2,1)S(1)}, u32[]{:S(2)}, u32[]{:S(2)}) collective-permute-start(bf16[2,2,128,128]{3,2,1,0:T(8,128)(2,1)S(1)} %get-tuple-element.32), channel_id=1, source_target_pairs={{0,8},{8,0},{16,24},{24,16},{32,40},{40,32},{48,56},{56,48},{64,72... | collective-permute-start | bytes 393224 | tf_op jit(solution)/shard_map/ppermute | solution.py:168
  48.3 6.7 %copy-start.21 = (bf16[16,2,128,128]{3,2,1,0:T(8,128)(2,1)S(1)}, bf16[16,2,128,128]{3,2,1,0:T(8,128)(2,1)}, u32[]{:S(2)}) copy-start(bf16[16,2,128,128]{3,2,1,0:T(8,128)(2,1)} %all-gather.3.cloned.1.call-done) | copy-start | bytes 3145732
  49.8 8.5 %copy-start.17 = (f32[2,256,256]{2,1,0:T(8,128)S(1)}, f32[2,256,256]{2,1,0:T(8,128)}, u32[]{:S(2)}) copy-start(f32[2,256,256]{2,1,0:T(8,128)} %copy-done.16) | copy-start | bytes 1572868
  49.8 8.5 %copy-start.20 = (bf16[2,256,256]{2,1,0:T(8,128)(2,1)S(1)}, bf16[2,256,256]{2,1,0:T(8,128)(2,1)}, u32[]{:S(2)}) copy-start(bf16[2,256,256]{2,1,0:T(8,128)(2,1)} %copy-done.19) | copy-start | bytes 786436
  49.8 5.5 %collective-permute-start.10 = (bf16[2,2,128,128]{3,2,1,0:T(8,128)(2,1)S(1)}, bf16[2,2,128,128]{3,2,1,0:T(8,128)(2,1)S(1)}, u32[]{:S(2)}, u32[]{:S(2)}) collective-permute-start(bf16[2,2,128,128]{3,2,1,0:T(8,128)(2,1)S(1)} %reduce_sum.22), channel_id=1, source_target_pairs={{0,64},{8,72},{16,80},{24,88},{32,96},{40,104},{48,112},{56,120},{... | collective-permute-start | bytes 393224 | tf_op jit(solution)/shard_map/ppermute | solution.py:168
  50.9 5.9 %collective-permute-start.11 = (bf16[2,2,128,128]{3,2,1,0:T(8,128)(2,1)S(1)}, bf16[2,2,128,128]{3,2,1,0:T(8,128)(2,1)S(1)}, u32[]{:S(2)}, u32[]{:S(2)}) collective-permute-start(bf16[2,2,128,128]{3,2,1,0:T(8,128)(2,1)S(1)} %reduce_sum.22), channel_id=1, source_target_pairs={{0,128},{8,136},{16,144},{24,152},{32,160},{40,168},{48,176},{56,1... | collective-permute-start | bytes 393224 | tf_op jit(solution)/shard_map/ppermute | solution.py:168
  53.1 5.2 %collective-permute-start.12 = (bf16[2,2,128,128]{3,2,1,0:T(8,128)(2,1)S(1)}, bf16[2,2,128,128]{3,2,1,0:T(8,128)(2,1)S(1)}, u32[]{:S(2)}, u32[]{:S(2)}) collective-permute-start(bf16[2,2,128,128]{3,2,1,0:T(8,128)(2,1)S(1)} %reduce_sum.22), channel_id=1, source_target_pairs={{0,192},{8,200},{16,208},{24,216},{32,224},{40,232},{48,240},{56,2... | collective-permute-start | bytes 393224 | tf_op jit(solution)/shard_map/ppermute | solution.py:168
  53.8 9.5 %collective-permute-start.9 = (bf16[2,2,128,128]{3,2,1,0:T(8,128)(2,1)S(1)}, bf16[2,2,128,128]{3,2,1,0:T(8,128)(2,1)S(1)}, u32[]{:S(2)}, u32[]{:S(2)}) collective-permute-start(bf16[2,2,128,128]{3,2,1,0:T(8,128)(2,1)S(1)} %fusion), channel_id=1, source_target_pairs={{0,16},{8,24},{16,0},{24,8},{32,48},{40,56},{48,32},{56,40},{64,80... | collective-permute-start | bytes 393224 | tf_op jit(solution)/shard_map/ppermute | solution.py:168
  55.3 27.3 %copy-start = (bf16[4096,256]{1,0:T(8,128)(2,1)S(1)}, bf16[4096,256]{1,0:T(8,128)(2,1)}, u32[]{:S(2)}) copy-start(bf16[4096,256]{1,0:T(8,128)(2,1)} %wq.3) | copy-start | bytes 6291460
  58.4 1.0 copy-start.15
  61.8 0.8 copy-start.8
  62.6 0.7 copy-start.12
  64.0 8.1 %collective-permute-start.13 = (bf16[2,2,128,128]{3,2,1,0:T(8,128)(2,1)S(1)}, bf16[2,2,128,128]{3,2,1,0:T(8,128)(2,1)S(1)}, u32[]{:S(2)}, u32[]{:S(2)}) collective-permute-start(bf16[2,2,128,128]{3,2,1,0:T(8,128)(2,1)S(1)} %fusion.7), channel_id=1, source_target_pairs={{0,32},{8,40},{16,48},{24,56},{32,0},{40,8},{48,16},{56,24},{64,96... | collective-permute-start | bytes 393224 | tf_op jit(solution)/shard_map/ppermute | solution.py:168
  72.1 0.6 copy-start.23
  73.5 4.1 %collective-permute-start.14 = (bf16[2,2,128,128]{3,2,1,0:T(8,128)(2,1)}, bf16[2,2,128,128]{3,2,1,0:T(8,128)(2,1)}, u32[]{:S(2)}, u32[]{:S(2)}) collective-permute-start(bf16[2,2,128,128]{3,2,1,0:T(8,128)(2,1)} %fusion.8), channel_id=1, source_target_pairs={{0,64},{8,72},{16,80},{24,88},{32,96},{40,104},{48,112},{56,120},{... | collective-permute-start | bytes 393224 | tf_op jit(solution)/shard_map/ppermute | solution.py:168
  74.0 6.1 %collective-permute-start.15 = (bf16[2,2,128,128]{3,2,1,0:T(8,128)(2,1)}, bf16[2,2,128,128]{3,2,1,0:T(8,128)(2,1)}, u32[]{:S(2)}, u32[]{:S(2)}) collective-permute-start(bf16[2,2,128,128]{3,2,1,0:T(8,128)(2,1)} %fusion.8), channel_id=1, source_target_pairs={{0,128},{8,136},{16,144},{24,152},{32,160},{40,168},{48,176},{56,1... | collective-permute-start | bytes 393224 | tf_op jit(solution)/shard_map/ppermute | solution.py:168
  75.8 5.5 %collective-permute-start.16 = (bf16[2,2,128,128]{3,2,1,0:T(8,128)(2,1)}, bf16[2,2,128,128]{3,2,1,0:T(8,128)(2,1)}, u32[]{:S(2)}, u32[]{:S(2)}) collective-permute-start(bf16[2,2,128,128]{3,2,1,0:T(8,128)(2,1)} %fusion.8), channel_id=1, source_target_pairs={{0,192},{8,200},{16,208},{24,216},{32,224},{40,232},{48,240},{56,2... | collective-permute-start | bytes 393224 | tf_op jit(solution)/shard_map/ppermute | solution.py:168
  82.7 1.6 %copy-start.1 = (bf16[4096,256]{1,0:T(8,128)(2,1)S(1)}, bf16[4096,256]{1,0:T(8,128)(2,1)}, u32[]{:S(2)}) copy-start(bf16[4096,256]{1,0:T(8,128)(2,1)} %wk.3) | copy-start | bytes 6291460
  84.3 1.6 %copy-start.2 = (bf16[4096,256]{1,0:T(8,128)(2,1)S(1)}, bf16[4096,256]{1,0:T(8,128)(2,1)}, u32[]{:S(2)}) copy-start(bf16[4096,256]{1,0:T(8,128)(2,1)} %wv.3) | copy-start | bytes 6291460
  85.8 1.6 %copy-start.3 = (bf16[4096,256]{1,0:T(8,128)(2,1)S(1)}, bf16[4096,256]{1,0:T(8,128)(2,1)}, u32[]{:S(2)}) copy-start(bf16[4096,256]{1,0:T(8,128)(2,1)} %wg.3) | copy-start | bytes 6291460
  87.4 1.0 copy-start.9
  88.5 0.9 copy-start.13
  93.8 14.5 %collective-permute-start.17 = (bf16[4,2,256,512]{3,2,1,0:T(8,128)(2,1)S(1)}, bf16[4,2,256,512]{3,2,1,0:T(8,128)(2,1)S(1)}, u32[]{:S(2)}, u32[]{:S(2)}) collective-permute-start(bf16[4,2,256,512]{3,2,1,0:T(8,128)(2,1)S(1)} %shard_map.107), channel_id=1, source_target_pairs={{0,1},{1,0},{2,3},{3,2},{4,5},{5,4},{6,7},{7,6},{8,9},{9,8},{10,11... | collective-permute-start | bytes 6291464 | tf_op jit(solution)/shard_map/ppermute | solution.py:256
  108.4 8.0 %collective-permute-start.22 = (bf16[256,512]{1,0:T(8,128)(2,1)S(1)}, bf16[256,512]{1,0:T(8,128)(2,1)S(1)}, u32[]{:S(2)}, u32[]{:S(2)}) collective-permute-start(bf16[256,512]{1,0:T(8,128)(2,1)S(1)} %get-tuple-element.46), channel_id=1, source_target_pairs={{0,6},{1,7},{2,0},{3,1},{4,2},{5,3},{6,4},{7,5},{8,14},{9,15},{10,... | collective-permute-start | bytes 786440 | tf_op jit(solution)/shard_map/ppermute | solution.py:253
  110.7 9.3 %collective-permute-start.19 = (bf16[256,512]{1,0:T(8,128)(2,1)S(1)}, bf16[256,512]{1,0:T(8,128)(2,1)S(1)}, u32[]{:S(2)}, u32[]{:S(2)}) collective-permute-start(bf16[256,512]{1,0:T(8,128)(2,1)S(1)} %get-tuple-element.44), channel_id=1, source_target_pairs={{0,2},{1,3},{2,4},{3,5},{4,6},{5,7},{6,0},{7,1},{8,10},{9,11},{10,... | collective-permute-start | bytes 786440 | tf_op jit(solution)/shard_map/ppermute | solution.py:253
  110.8 11.3 %collective-permute-start.18 = (bf16[256,512]{1,0:T(8,128)(2,1)S(1)}, bf16[256,512]{1,0:T(8,128)(2,1)S(1)}, u32[]{:S(2)}, u32[]{:S(2)}) collective-permute-start(bf16[256,512]{1,0:T(8,128)(2,1)S(1)} %get-tuple-element.43), channel_id=1, source_target_pairs={{0,6},{1,7},{2,0},{3,1},{4,2},{5,3},{6,4},{7,5},{8,14},{9,15},{10,... | collective-permute-start | bytes 786440 | tf_op jit(solution)/shard_map/ppermute | solution.py:253
  113.5 11.5 %collective-permute-start.21 = (bf16[256,512]{1,0:T(8,128)(2,1)S(1)}, bf16[256,512]{1,0:T(8,128)(2,1)S(1)}, u32[]{:S(2)}, u32[]{:S(2)}) collective-permute-start(bf16[256,512]{1,0:T(8,128)(2,1)S(1)} %get-tuple-element.45), channel_id=1, source_target_pairs={{0,2},{1,3},{2,4},{3,5},{4,6},{5,7},{6,0},{7,1},{8,10},{9,11},{10,... | collective-permute-start | bytes 786440 | tf_op jit(solution)/shard_map/ppermute | solution.py:253
  116.5 11.1 %collective-permute-start.23 = (bf16[256,512]{1,0:T(8,128)(2,1)S(1)}, bf16[256,512]{1,0:T(8,128)(2,1)S(1)}, u32[]{:S(2)}, u32[]{:S(2)}) collective-permute-start(bf16[256,512]{1,0:T(8,128)(2,1)S(1)} %shard_map.111), channel_id=1, source_target_pairs={{0,6},{1,7},{2,0},{3,1},{4,2},{5,3},{6,4},{7,5},{8,14},{9,15},{10,... | collective-permute-start | bytes 786440 | tf_op jit(solution)/shard_map/ppermute | solution.py:253
  120.1 10.6 %collective-permute-start.20 = (bf16[256,512]{1,0:T(8,128)(2,1)S(1)}, bf16[256,512]{1,0:T(8,128)(2,1)S(1)}, u32[]{:S(2)}, u32[]{:S(2)}) collective-permute-start(bf16[256,512]{1,0:T(8,128)(2,1)S(1)} %shard_map.110), channel_id=1, source_target_pairs={{0,2},{1,3},{2,4},{3,5},{4,6},{5,7},{6,0},{7,1},{8,10},{9,11},{10,... | collective-permute-start | bytes 786440 | tf_op jit(solution)/shard_map/ppermute | solution.py:253
  (1 other events, 0.6 us)
Sparse Core Ops, SparseCore 0:
  9.5 38.7 all-gather.2

commit v3 on v2

--- a/solution.py
+++ b/solution.py
@@ -6,6 +6,11 @@
 from jax.sharding import PartitionSpec as P
 
 HD = 128
+PROJ = 48
+PICK = 54
+INNER = 48
+SUM = 8
+GATE = 8
 MIB = 1024 * 1024
 RELATIVE = (0, -1, 1, 2)
 
@@ -59,7 +64,7 @@
         copy.wait()
 
 
-def gated_start_kernel(g_ref, a0, a1, b0, b1, w_ref, wo_ref, mine_ref, other_ref):
+def gated_start_kernel(g_ref, a_ref, b_ref, w_ref, wo_ref, mine_ref, other_ref):
     k = pl.program_id(0)
 
     @pl.when(k == 0)
@@ -68,13 +73,13 @@
             mine_ref[s] = nt(g_ref[s], w_ref[0])
             other_ref[s] = nt(g_ref[s], wo_ref[0])
 
-    for at, pair in ((1, (a0, a1)), (2, (b0, b1))):
+    for at, piece in ((1, a_ref), (2, b_ref)):
 
         @pl.when(k == at)
-        def _(pair=pair):
+        def _(piece=piece):
             for s in range(2):
-                mine_ref[s] += nt(pair[s][...], w_ref[0])
-                other_ref[s] += nt(pair[s][...], wo_ref[0])
+                mine_ref[s] += nt(piece[s], w_ref[0])
+                other_ref[s] += nt(piece[s], wo_ref[0])
 
 
 def gated_end_kernel(mine_in, other_in, c0, c1, w_ref, wo_ref, mine_ref, other_ref):
@@ -225,7 +230,7 @@
         grid=(1,),
         in_specs=specs,
         out_specs=out_specs,
-        compiler_params=params(),
+        compiler_params=params(SUM),
         cost_estimate=cost(0, (len(arrays) + len(groups)) * shape[0] * shape[1] * 2),
     )(*arrays)
 
@@ -255,11 +260,10 @@
     def other_core(x):
         return lax.ppermute(x, "head", [(i, i ^ 1) for i in range(peers)])
 
-    g0, g1 = grad_out[0], grad_out[1]
-    a0 = along_y(g0, 1)
-    b1 = along_y(g1, -1)
-    a1 = along_y(g1, 1)
-    b0 = along_y(g0, -1)
+    a = along_y(grad_out, 1)
+    b = along_y(grad_out, -1)
+    c0 = along_y(a[0], 1)
+    c1 = along_y(b[1], -1)
 
     total = pl.pallas_call(
         key_state_kernel,
@@ -267,11 +271,10 @@
         compiler_params=params(),
         cost_estimate=cost(2 * seq_count * rows * columns * HD, 4 * seq_count * rows * columns),
     )(keys, values)
-    seq_peers = lax.axis_size("seq")
-    rows_of = [[x * 8 + z for z in range(8)] for x in range(seq_peers // 8)]
-    line = lax.all_gather(total, "seq", axis_index_groups=rows_of)
-    c0 = along_y(a0, 1)
-    c1 = along_y(b1, -1)
+    before = [swap(total, 1)]
+    total = joined(total, before[0])
+    a, total = together(a, total)
+    before.append(swap(total, 2))
 
     w_pick, w_own = pl.pallas_call(
         pick_kernel,
@@ -283,7 +286,7 @@
             out_specs=[whole((4, columns, features))] * 2,
             scratch_shapes=[pltpu.SemaphoreType.DMA((8,))],
         ),
-        compiler_params=params(),
+        compiler_params=params(PICK),
         cost_estimate=cost(0, 2 * 8 * columns * features * 2),
     )(table, w_out)
     w_theirs = other_core(w_pick)
@@ -296,11 +299,11 @@
         gated_start_kernel,
         out_shape=two,
         grid=(3,),
-        in_specs=[whole(grad_out.shape)] + [whole(flat)] * 4 + [piece] * 2,
+        in_specs=[whole(grad_out.shape)] * 3 + [piece] * 2,
         out_specs=[whole(cube)] * 2,
         compiler_params=params(),
         cost_estimate=cost(3 * piece_flops, 4 * MIB),
-    )(grad_out, a0, a1, b0, b1, w_own, w_theirs)
+    )(grad_out, a, b, w_own, w_theirs)
     piece = pl.BlockSpec((1, columns, features), lambda k: (3, 0, 0))
     mine, other = pl.pallas_call(
         gated_end_kernel,
@@ -311,7 +314,10 @@
         compiler_params=params(),
         cost_estimate=cost(piece_flops, 3 * MIB),
     )(mine, other, c0, c1, w_own, w_theirs)
+    other, before[1] = together(other, before[1])
     theirs = other_core(other)
+    total = joined(total, before[1])
+    before.append(swap(total, 4))
 
     d_output, slope, query_state = pl.pallas_call(
         gate_kernel,
@@ -320,19 +326,14 @@
             jax.ShapeDtypeStruct(cube, f32),
             jax.ShapeDtypeStruct(state_shape, bf16),
         ],
-        compiler_params=params(),
+        compiler_params=params(GATE),
         cost_estimate=cost(2 * seq_count * rows * columns * HD, 3 * 1024 * 1024),
     )(mine, theirs, gate_pre, queries)
     after = [swap(query_state, 1)]
-    line, after[0] = together(line, after[0])
-    z = lax.axis_index("seq") % 8
-    earlier = (jnp.arange(8) < z).reshape(8, 1, 1, 1, 1)
-    line = line.astype(f32)
-    prefix = jnp.where(earlier, line, 0.0).sum(0)
-    row_total = line.sum(0).astype(bf16)
-    for by, bit in ((8, 8), (16, 16), (24, 16)):
-        prefix = prefix + counted(swap(row_total, by), bit, False)
-    prefix = prefix.astype(bf16)
+    after[0], before[2] = together(after[0], before[2])
+    total = joined(total, before[2])
+    before += [swap(total, by) for by in (8, 16, 24)]
+    prefix = entering(before, False)
     total = joined(query_state, after[0])
     after.append(swap(total, 2))
 
@@ -343,7 +344,7 @@
         grid=(seq_count, head_count),
         in_specs=[block] * 5 + [pl.BlockSpec((1, 1, HD, HD), lambda s, h: (s, h, 0, 0))],
         out_specs=[block] * 4,
-        compiler_params=params(),
+        compiler_params=params(INNER),
         cost_estimate=cost(12 * seq_count * rows * rows * columns, 3 * 1024 * 1024),
     )(queries, keys, values, d_output, slope, prefix)
 
@@ -367,7 +368,7 @@
                 scratch_shapes=[pltpu.VMEM(cube, bf16)] * 2
                 + [pltpu.VMEM((4, 4, features, columns), bf16), pltpu.SemaphoreType.DMA((4, 4))],
             ),
-            compiler_params=params(16),
+            compiler_params=params(PROJ),
             cost_estimate=cost(32 * seq_count * rows * columns * features, 8 * 1024 * 1024),
         )(table, d_query, d_gate, dk_part, dv_part, keys, values, suffix, w_query, w_key, w_value, w_gate)
 

time: 139 us -> 121 us (0.87)
  local copies, waits for them, and re-layouts: 15.5 us -> 0.07 us
  between operations: 13.7 us -> 0.26 us
  waiting for transfers between devices: 44.3 us -> 55.1 us
  Pallas kernels: 16.7 us -> 20.1 us
  starting transfers between devices: 44.4 us -> 42.5 us
    unnamed x48 -> x14, local copies, waits for them, and re-layouts: 15.5 us -> 0.03 us
    ppermute x9 -> x12, waiting for transfers between devices: 17.2 us -> 30.6 us  [swap(): lax.ppermute(x, 'seq', [(i, i ^ by) for i in range(lax.axis_size('seq'))])]
    ppermute x3, starting transfers between devices: 14.4 us -> 7.27 us  [other_core(): return lax.ppermute(x, 'head', [(i, i ^ 1) for i in range(peers)])]
    pallas_call x1, Pallas kernels: 0.81 us -> 3.62 us  [body(): pl.pallas_call(pick_kernel, out_shape=[jax.ShapeDtypeStruct((4, columns,...]
    ppermute x12 -> x10, starting transfers between devices: 16.6 us -> 19.4 us  [along_y(): lax.ppermute(x, 'head', [(i, (i + 2 * by) % peers) for i in range(peers)])]
    ppermute x9 -> x12, starting transfers between devices: 13.4 us -> 15.8 us  [swap(): lax.ppermute(x, 'seq', [(i, i ^ by) for i in range(lax.axis_size('seq'))])]
    reduce_sum x2 -> x0, other arithmetic: 1.73 us -> none  [the longest x1 1.47 us: body(): row_total = line.sum(0).astype(bf16)]
    ppermute x3, waiting for transfers between devices: 1.54 us -> 0.01 us  [other_core(): return lax.ppermute(x, 'head', [(i, i ^ 1) for i in range(peers)])]
  transfers between devices with their start and end apart: 25 -> 25, of which waited for: 17 -> 16; matrix products, arithmetic and copies ran while one was open for 0% -> 1% of each run, Pallas kernels for 7% -> 12%
where the time goes in v3:
time: 121 us
  waiting for transfers between devices  55.1 us (46%)
  starting transfers between devices  42.5 us (35%)
  Pallas kernels  20.1 us (17%)
  other arithmetic  2.88 us (2%)
    ppermute x12, waiting for transfers between devices, swap(): lax.ppermute(x, 'seq', [(i, i ^ by) for i in range(lax.axis_size('seq'))])  30.6 us
    ppermute x10, waiting for transfers between devices, along_y(): lax.ppermute(x, 'head', [(i, (i + 2 * by) % peers) for i in range(peers)])  24.5 us
    ppermute x10, starting transfers between devices, along_y(): lax.ppermute(x, 'head', [(i, (i + 2 * by) % peers) for i in range(peers)])  19.4 us
    ppermute x12, starting transfers between devices, swap(): lax.ppermute(x, 'seq', [(i, i ^ by) for i in range(lax.axis_size('seq'))])  15.8 us
    pallas_call x2, Pallas kernels, project(): pl.pallas_call(make_project_kernel(factor, first), out_shape=jax.ShapeDty...  9.84 us
    ppermute x3, starting transfers between devices, other_core(): return lax.ppermute(x, 'head', [(i, i ^ 1) for i in range(peers)])  7.27 us
    pallas_call x1, Pallas kernels, body(): pl.pallas_call(pick_kernel, out_shape=[jax.ShapeDtypeStruct((4, columns,...  3.62 us
    pallas_call x1, Pallas kernels, body(): pl.pallas_call(make_inner_kernel(factor), out_shape=[jax.ShapeDtypeStruct...  2.54 us
  transfers between devices with their start and end apart: 25, of which 16 were waited for; matrix products, arithmetic and copies ran while one was open for 1% of the time, Pallas kernels for 12%

profile of v3, /device:TPU:1, one launch (start us, length us, event | category | flops | bytes accessed | tf_op | source)
XLA Modules:
  0.0 120.8 jit_solution(3783075465018190696)
XLA Ops:
  0.0 2.2 %collective-permute-start = (bf16[2,256,512]{2,1,0:T(8,128)(2,1)}, bf16[2,256,512]{2,1,0:T(8,128)(2,1)S(1)}, u32[]{:S(2)}, u32[]{:S(2)}) collective-permute-start(bf16[2,256,512]{2,1,0:T(8,128)(2,1)} %g_ref.1), channel_id=1, source_target_pairs={{0,2},{1,3},{2,4},{3,5},{4,6},{5,7},{6,0},{7,1},{8,10},{9,11},{10,... | collective-permute-start | bytes 1572872 | tf_op jit(solution)/shard_map/ppermute | solution.py:258
  2.2 0.5 fusion.20.table_ref
  2.7 3.6 %shard_map.101 = (bf16[4,256,512]{2,1,0:T(8,128)(2,1)}, bf16[4,256,512]{2,1,0:T(8,128)(2,1)}) custom-call(s32[8]{0:T(128)} %fusion.20.table_ref, bf16[256,4096]{1,0:T(8,128)(2,1)} %w_ref.1), custom_call_target="tpu_custom_call" | custom-call | bytes 4194304 | tf_op jit(solution)/shard_map/pallas_call | solution.py:279
  6.4 1.1 collective-permute-start.3
  7.5 2.9 %collective-permute-start.2 = (bf16[2,256,512]{2,1,0:T(8,128)(2,1)S(1)}, bf16[2,256,512]{2,1,0:T(8,128)(2,1)S(1)}, u32[]{:S(2)}, u32[]{:S(2)}) collective-permute-start(bf16[2,256,512]{2,1,0:T(8,128)(2,1)S(1)} %copy-done.4), channel_id=1, source_target_pairs={{0,6},{1,7},{2,0},{3,1},{4,2},{5,3},{6,4},{7,5},{8,14},{9,15},{10,... | collective-permute-start | bytes 1572872 | tf_op jit(solution)/shard_map/ppermute | solution.py:258
  10.5 0.3 shard_map.100
  10.9 2.7 %collective-permute-done.a_ref = bf16[2,256,512]{2,1,0:T(8,128)(2,1)S(1)} collective-permute-done((bf16[2,256,512]{2,1,0:T(8,128)(2,1)}, bf16[2,256,512]{2,1,0:T(8,128)(2,1)S(1)}, u32[]{:S(2)}, u32[]{:S(2)}) %collective-permute-start) | collective-permute-done | bytes 524320 | tf_op jit(solution)/shard_map/ppermute | solution.py:258
  13.6 1.6 %collective-permute-start.4 = (bf16[256,512]{1,0:T(8,128)(2,1)S(1)}, bf16[256,512]{1,0:T(8,128)(2,1)S(1)}, u32[]{:S(2)}, u32[]{:S(2)}) collective-permute-start(bf16[256,512]{1,0:T(8,128)(2,1)S(1)} %slice_bitcast_fusion.1), channel_id=1, source_target_pairs={{0,2},{1,3},{2,4},{3,5},{4,6},{5,7},{6,0},{7,1},{8,10},{9,11},{10,... | collective-permute-start | bytes 786440 | tf_op jit(solution)/shard_map/ppermute | solution.py:258
  15.1 6.6 %collective-permute-done.2.b_ref = bf16[2,256,512]{2,1,0:T(8,128)(2,1)S(1)} collective-permute-done((bf16[2,256,512]{2,1,0:T(8,128)(2,1)S(1)}, bf16[2,256,512]{2,1,0:T(8,128)(2,1)S(1)}, u32[]{:S(2)}, u32[]{:S(2)}) %collective-permute-start.2) | collective-permute-done | bytes 524320 | tf_op jit(solution)/shard_map/ppermute | solution.py:258
  21.8 3.5 %collective-permute-start.5 = (bf16[256,512]{1,0:T(8,128)(2,1)S(1)}, bf16[256,512]{1,0:T(8,128)(2,1)S(1)}, u32[]{:S(2)}, u32[]{:S(2)}) collective-permute-start(bf16[256,512]{1,0:T(8,128)(2,1)S(1)} %slice_bitcast_fusion), channel_id=1, source_target_pairs={{0,6},{1,7},{2,0},{3,1},{4,2},{5,3},{6,4},{7,5},{8,14},{9,15},{10,... | collective-permute-start | bytes 786440 | tf_op jit(solution)/shard_map/ppermute | solution.py:258
  25.3 1.4 %collective-permute-start.6 = (bf16[2,2,128,128]{3,2,1,0:T(8,128)(2,1)S(1)}, bf16[2,2,128,128]{3,2,1,0:T(8,128)(2,1)S(1)}, u32[]{:S(2)}, u32[]{:S(2)}) collective-permute-start(bf16[2,2,128,128]{3,2,1,0:T(8,128)(2,1)S(1)} %fusion), channel_id=1, source_target_pairs={{0,16},{8,24},{16,0},{24,8},{32,48},{40,56},{48,32},{56,40},{64,80... | collective-permute-start | bytes 393224 | tf_op jit(solution)/shard_map/ppermute | solution.py:173
  26.7 1.5 %shard_map.102 = (f32[2,256,256]{2,1,0:T(8,128)S(1)}, f32[2,256,256]{2,1,0:T(8,128)S(1)}) custom-call(bf16[2,256,512]{2,1,0:T(8,128)(2,1)S(1)} %copy-done.4, bf16[2,256,512]{2,1,0:T(8,128)(2,1)S(1)} %collective-permute-done.a_ref, bf16[2,256,512]{2,1,0:T(8,128)(2,1)S(1)} %collective-permute-done.2.b_ref, bf16[4,256,512]{2,1,0:T(8,128)(2,1)S(1)} %copy-done, ...), custom_call_target="tpu_custom_call" | custom-call | flops 805306368 | bytes 4194304 | tf_op jit(solution)/shard_map/pallas_call | solution.py:298
  28.2 1.8 %collective-permute-done.5.c1 = bf16[256,512]{1,0:T(8,128)(2,1)S(1)} collective-permute-done((bf16[256,512]{1,0:T(8,128)(2,1)S(1)}, bf16[256,512]{1,0:T(8,128)(2,1)S(1)}, u32[]{:S(2)}, u32[]{:S(2)}) %collective-permute-start.5) | collective-permute-done | bytes 262176 | tf_op jit(solution)/shard_map/ppermute | solution.py:258
  30.0 0.5 shard_map.103
  30.5 3.6 %collective-permute-done.6 = bf16[2,2,128,128]{3,2,1,0:T(8,128)(2,1)S(1)} collective-permute-done((bf16[2,2,128,128]{3,2,1,0:T(8,128)(2,1)S(1)}, bf16[2,2,128,128]{3,2,1,0:T(8,128)(2,1)S(1)}, u32[]{:S(2)}, u32[]{:S(2)}) %collective-permute-start.6) | collective-permute-done | bytes 131104 | tf_op jit(solution)/shard_map/ppermute | solution.py:173
  34.1 0.9 collective-permute-start.7
  35.0 5.3 %collective-permute-start.9 = (bf16[2,2,128,128]{3,2,1,0:T(8,128)(2,1)S(1)}, bf16[2,2,128,128]{3,2,1,0:T(8,128)(2,1)S(1)}, u32[]{:S(2)}, u32[]{:S(2)}) collective-permute-start(bf16[2,2,128,128]{3,2,1,0:T(8,128)(2,1)S(1)} %fusion.7), channel_id=1, source_target_pairs={{0,32},{8,40},{16,48},{24,56},{32,0},{40,8},{48,16},{56,24},{64,96... | collective-permute-start | bytes 393224 | tf_op jit(solution)/shard_map/ppermute | solution.py:173
  40.4 0.4 shard_map.104
  40.9 6.1 %collective-permute-done.9 = bf16[2,2,128,128]{3,2,1,0:T(8,128)(2,1)S(1)} collective-permute-done((bf16[2,2,128,128]{3,2,1,0:T(8,128)(2,1)S(1)}, bf16[2,2,128,128]{3,2,1,0:T(8,128)(2,1)S(1)}, u32[]{:S(2)}, u32[]{:S(2)}) %collective-permute-start.9) | collective-permute-done | bytes 131104 | tf_op jit(solution)/shard_map/ppermute | solution.py:173
  47.0 1.9 %collective-permute-done.8 = bf16[2,2,128,128]{3,2,1,0:T(8,128)(2,1)S(1)} collective-permute-done((bf16[2,2,128,128]{3,2,1,0:T(8,128)(2,1)S(1)}, bf16[2,2,128,128]{3,2,1,0:T(8,128)(2,1)S(1)}, u32[]{:S(2)}, u32[]{:S(2)}) %collective-permute-start.8) | collective-permute-done | bytes 131104 | tf_op jit(solution)/shard_map/ppermute | solution.py:173
  48.9 1.3 %collective-permute-start.11 = (bf16[2,2,128,128]{3,2,1,0:T(8,128)(2,1)S(1)}, bf16[2,2,128,128]{3,2,1,0:T(8,128)(2,1)S(1)}, u32[]{:S(2)}, u32[]{:S(2)}) collective-permute-start(bf16[2,2,128,128]{3,2,1,0:T(8,128)(2,1)S(1)} %fusion.15), channel_id=1, source_target_pairs={{0,64},{8,72},{16,80},{24,88},{32,96},{40,104},{48,112},{56,120},{... | collective-permute-start | bytes 393224 | tf_op jit(solution)/shard_map/ppermute | solution.py:173
  50.2 2.5 %collective-permute-start.12 = (bf16[2,2,128,128]{3,2,1,0:T(8,128)(2,1)S(1)}, bf16[2,2,128,128]{3,2,1,0:T(8,128)(2,1)S(1)}, u32[]{:S(2)}, u32[]{:S(2)}) collective-permute-start(bf16[2,2,128,128]{3,2,1,0:T(8,128)(2,1)S(1)} %fusion.15), channel_id=1, source_target_pairs={{0,128},{8,136},{16,144},{24,152},{32,160},{40,168},{48,176},{56,1... | collective-permute-start | bytes 393224 | tf_op jit(solution)/shard_map/ppermute | solution.py:173
  52.7 0.2 collective-permute-start.13
  52.9 0.7 collective-permute-start.10
  53.7 4.8 %collective-permute-done.12 = bf16[2,2,128,128]{3,2,1,0:T(8,128)(2,1)S(1)} collective-permute-done((bf16[2,2,128,128]{3,2,1,0:T(8,128)(2,1)S(1)}, bf16[2,2,128,128]{3,2,1,0:T(8,128)(2,1)S(1)}, u32[]{:S(2)}, u32[]{:S(2)}) %collective-permute-start.12) | collective-permute-done | bytes 131104 | tf_op jit(solution)/shard_map/ppermute | solution.py:173
  58.4 2.5 %collective-permute-done.13 = bf16[2,2,128,128]{3,2,1,0:T(8,128)(2,1)S(1)} collective-permute-done((bf16[2,2,128,128]{3,2,1,0:T(8,128)(2,1)S(1)}, bf16[2,2,128,128]{3,2,1,0:T(8,128)(2,1)S(1)}, u32[]{:S(2)}, u32[]{:S(2)}) %collective-permute-start.13) | collective-permute-done | bytes 131104 | tf_op jit(solution)/shard_map/ppermute | solution.py:173
  60.9 0.2 fusion.6.prefix_ref
  61.1 2.5 %shard_map.105 = (bf16[2,256,256]{2,1,0:T(8,128)(2,1)S(1)}, bf16[2,256,256]{2,1,0:T(8,128)(2,1)S(1)}, f32[2,256,256]{2,1,0:T(8,128)S(1)}, f32[2,256,256]{2,1,0:T(8,128)S(1)}) custom-call(bf16[2,256,256]{2,1,0:T(8,128)(2,1)S(1)} %copy-done.3, bf16[2,256,256]{2,1,0:T(8,128)(2,1)S(1)} %copy-done.1, bf16[2,256,256]{2,1,0:T(8,128)(2,1)S(1)} %copy-done.2, ...), custom_call_target="tpu_custom_call" | custom-call | flops 402653184 | bytes 3145728 | tf_op jit(solution)/shard_map/pallas_call | solution.py:341
  63.7 0.9 fusion.16
  64.7 8.7 %collective-permute-done.14 = bf16[2,2,128,128]{3,2,1,0:T(8,128)(2,1)S(1)} collective-permute-done((bf16[2,2,128,128]{3,2,1,0:T(8,128)(2,1)S(1)}, bf16[2,2,128,128]{3,2,1,0:T(8,128)(2,1)S(1)}, u32[]{:S(2)}, u32[]{:S(2)}) %collective-permute-start.14) | collective-permute-done | bytes 131104 | tf_op jit(solution)/shard_map/ppermute | solution.py:173
  73.5 0.3 collective-permute-start.15
  73.7 1.0 collective-permute-start.16
  74.7 2.9 %collective-permute-start.17 = (bf16[2,2,128,128]{3,2,1,0:T(8,128)(2,1)S(1)}, bf16[2,2,128,128]{3,2,1,0:T(8,128)(2,1)S(1)}, u32[]{:S(2)}, u32[]{:S(2)}) collective-permute-start(bf16[2,2,128,128]{3,2,1,0:T(8,128)(2,1)S(1)} %fusion.17), channel_id=1, source_target_pairs={{0,192},{8,200},{16,208},{24,216},{32,224},{40,232},{48,240},{56,2... | collective-permute-start | bytes 393224 | tf_op jit(solution)/shard_map/ppermute | solution.py:173
  77.6 1.6 %collective-permute-done.16 = bf16[2,2,128,128]{3,2,1,0:T(8,128)(2,1)S(1)} collective-permute-done((bf16[2,2,128,128]{3,2,1,0:T(8,128)(2,1)S(1)}, bf16[2,2,128,128]{3,2,1,0:T(8,128)(2,1)S(1)}, u32[]{:S(2)}, u32[]{:S(2)}) %collective-permute-start.16) | collective-permute-done | bytes 131104 | tf_op jit(solution)/shard_map/ppermute | solution.py:173
  79.2 1.3 %collective-permute-done.17 = bf16[2,2,128,128]{3,2,1,0:T(8,128)(2,1)S(1)} collective-permute-done((bf16[2,2,128,128]{3,2,1,0:T(8,128)(2,1)S(1)}, bf16[2,2,128,128]{3,2,1,0:T(8,128)(2,1)S(1)}, u32[]{:S(2)}, u32[]{:S(2)}) %collective-permute-start.17) | collective-permute-done | bytes 131104 | tf_op jit(solution)/shard_map/ppermute | solution.py:173
  80.5 1.1 fusion.14.suffix_ref
  81.6 4.9 %shard_map.107 = bf16[4,2,256,512]{3,2,1,0:T(8,128)(2,1)S(1)} custom-call(s32[8]{0:T(128)S(1)} %copy-done.6, bf16[2,256,256]{2,1,0:T(8,128)(2,1)S(1)} %get-tuple-element.46.dq_ref, bf16[2,256,256]{2,1,0:T(8,128)(2,1)S(1)} %get-tuple-element.47.dg_ref, f32[2,256,256]{2,1,0:T(8,128)S(1)} %get-tuple-element.48.dk_part, ...), custom_call_target="tpu_custom_call" | custom-call | flops 2147483648 | bytes 8388608 | tf_op jit(solution)/shard_map/pallas_call | solution.py:360
  86.6 5.2 %collective-permute-start.18 = (bf16[4,2,256,512]{3,2,1,0:T(8,128)(2,1)S(1)}, bf16[4,2,256,512]{3,2,1,0:T(8,128)(2,1)S(1)}, u32[]{:S(2)}, u32[]{:S(2)}) collective-permute-start(bf16[4,2,256,512]{3,2,1,0:T(8,128)(2,1)S(1)} %shard_map.107), channel_id=1, source_target_pairs={{0,1},{1,0},{2,3},{3,2},{4,5},{5,4},{6,7},{7,6},{8,9},{9,8},{10,11... | collective-permute-start | bytes 6291464 | tf_op jit(solution)/shard_map/ppermute | solution.py:261
  91.8 4.9 %shard_map.106.refs_0_.refs_2_.refs_4_ = bf16[4,2,256,512]{3,2,1,0:T(8,128)(2,1)S(1)} custom-call(s32[8]{0:T(128)S(1)} %copy-done.6, bf16[2,256,256]{2,1,0:T(8,128)(2,1)S(1)} %get-tuple-element.46.dq_ref, bf16[2,256,256]{2,1,0:T(8,128)(2,1)S(1)} %get-tuple-element.47.dg_ref, f32[2,256,256]{2,1,0:T(8,128)S(1)} %get-tuple-element.48.dk_part, ...), custom_call_target="tpu_custom_call" | custom-call | flops 2147483648 | bytes 8388608 | tf_op jit(solution)/shard_map/pallas_call | solution.py:360
  96.9 2.9 %collective-permute-start.23 = (bf16[256,512]{1,0:T(8,128)(2,1)S(1)}, bf16[256,512]{1,0:T(8,128)(2,1)S(1)}, u32[]{:S(2)}, u32[]{:S(2)}) collective-permute-start(bf16[256,512]{1,0:T(8,128)(2,1)S(1)} %get-tuple-element.54), channel_id=1, source_target_pairs={{0,6},{1,7},{2,0},{3,1},{4,2},{5,3},{6,4},{7,5},{8,14},{9,15},{10,... | collective-permute-start | bytes 786440 | tf_op jit(solution)/shard_map/ppermute | solution.py:258
  99.8 2.8 %collective-permute-start.19 = (bf16[256,512]{1,0:T(8,128)(2,1)S(1)}, bf16[256,512]{1,0:T(8,128)(2,1)S(1)}, u32[]{:S(2)}, u32[]{:S(2)}) collective-permute-start(bf16[256,512]{1,0:T(8,128)(2,1)S(1)} %get-tuple-element.51), channel_id=1, source_target_pairs={{0,6},{1,7},{2,0},{3,1},{4,2},{5,3},{6,4},{7,5},{8,14},{9,15},{10,... | collective-permute-start | bytes 786440 | tf_op jit(solution)/shard_map/ppermute | solution.py:258
  102.6 2.8 %collective-permute-done.23.refs_2_ = bf16[256,512]{1,0:T(8,128)(2,1)S(1)} collective-permute-done((bf16[256,512]{1,0:T(8,128)(2,1)S(1)}, bf16[256,512]{1,0:T(8,128)(2,1)S(1)}, u32[]{:S(2)}, u32[]{:S(2)}) %collective-permute-start.23) | collective-permute-done | bytes 262176 | tf_op jit(solution)/shard_map/ppermute | solution.py:258
  105.5 3.5 %collective-permute-start.24 = (bf16[256,512]{1,0:T(8,128)(2,1)S(1)}, bf16[256,512]{1,0:T(8,128)(2,1)S(1)}, u32[]{:S(2)}, u32[]{:S(2)}) collective-permute-start(bf16[256,512]{1,0:T(8,128)(2,1)S(1)} %shard_map.111), channel_id=1, source_target_pairs={{0,6},{1,7},{2,0},{3,1},{4,2},{5,3},{6,4},{7,5},{8,14},{9,15},{10,... | collective-permute-start | bytes 786440 | tf_op jit(solution)/shard_map/ppermute | solution.py:258
  109.2 1.8 %collective-permute-done.19.refs_2_ = bf16[256,512]{1,0:T(8,128)(2,1)S(1)} collective-permute-done((bf16[256,512]{1,0:T(8,128)(2,1)S(1)}, bf16[256,512]{1,0:T(8,128)(2,1)S(1)}, u32[]{:S(2)}, u32[]{:S(2)}) %collective-permute-start.19) | collective-permute-done | bytes 262176 | tf_op jit(solution)/shard_map/ppermute | solution.py:258
  111.1 3.1 %collective-permute-done.22.refs_6_ = bf16[256,512]{1,0:T(8,128)(2,1)S(1)} collective-permute-done((bf16[256,512]{1,0:T(8,128)(2,1)S(1)}, bf16[256,512]{1,0:T(8,128)(2,1)S(1)}, u32[]{:S(2)}, u32[]{:S(2)}) %collective-permute-start.22) | collective-permute-done | bytes 262176 | tf_op jit(solution)/shard_map/ppermute | solution.py:258
  114.2 2.5 %collective-permute-done.24.refs_7_ = bf16[256,512]{1,0:T(8,128)(2,1)S(1)} collective-permute-done((bf16[256,512]{1,0:T(8,128)(2,1)S(1)}, bf16[256,512]{1,0:T(8,128)(2,1)S(1)}, u32[]{:S(2)}, u32[]{:S(2)}) %collective-permute-start.24) | collective-permute-done | bytes 262176 | tf_op jit(solution)/shard_map/ppermute | solution.py:258
  116.7 3.1 %collective-permute-done.21.refs_3_ = bf16[256,512]{1,0:T(8,128)(2,1)S(1)} collective-permute-done((bf16[256,512]{1,0:T(8,128)(2,1)S(1)}, bf16[256,512]{1,0:T(8,128)(2,1)S(1)}, u32[]{:S(2)}, u32[]{:S(2)}) %collective-permute-start.21) | collective-permute-done | bytes 262176 | tf_op jit(solution)/shard_map/ppermute | solution.py:258
  119.8 1.0 shard_map.112
  (40 shorter events, 1.1 us)
Async XLA Ops:
  0.0 7.5 %copy-start.4 = (bf16[2,256,512]{2,1,0:T(8,128)(2,1)S(1)}, bf16[2,256,512]{2,1,0:T(8,128)(2,1)}, u32[]{:S(2)}) copy-start(bf16[2,256,512]{2,1,0:T(8,128)(2,1)} %g_ref.1) | copy-start | bytes 1572868
  0.0 10.5 %copy-start.1 = (bf16[2,256,256]{2,1,0:T(8,128)(2,1)S(1)}, bf16[2,256,256]{2,1,0:T(8,128)(2,1)}, u32[]{:S(2)}) copy-start(bf16[2,256,256]{2,1,0:T(8,128)(2,1)} %k_ref.7) | copy-start | bytes 786436
  0.0 10.5 %copy-start.2 = (bf16[2,256,256]{2,1,0:T(8,128)(2,1)S(1)}, bf16[2,256,256]{2,1,0:T(8,128)(2,1)}, u32[]{:S(2)}) copy-start(bf16[2,256,256]{2,1,0:T(8,128)(2,1)} %v_ref.7) | copy-start | bytes 786436
  0.0 13.5 %collective-permute-start = (bf16[2,256,512]{2,1,0:T(8,128)(2,1)}, bf16[2,256,512]{2,1,0:T(8,128)(2,1)S(1)}, u32[]{:S(2)}, u32[]{:S(2)}) collective-permute-start(bf16[2,256,512]{2,1,0:T(8,128)(2,1)} %g_ref.1), channel_id=1, source_target_pairs={{0,2},{1,3},{2,4},{3,5},{4,6},{5,7},{6,0},{7,1},{8,10},{9,11},{10,... | collective-permute-start | bytes 1572872 | tf_op jit(solution)/shard_map/ppermute | solution.py:258
  6.4 20.4 %copy-start = (bf16[4,256,512]{2,1,0:T(8,128)(2,1)S(1)}, bf16[4,256,512]{2,1,0:T(8,128)(2,1)}, u32[]{:S(2)}) copy-start(bf16[4,256,512]{2,1,0:T(8,128)(2,1)} %get-tuple-element.31.w_ref) | copy-start | bytes 3145732
  6.4 20.3 %collective-permute-start.3 = (bf16[4,256,512]{2,1,0:T(8,128)(2,1)}, bf16[4,256,512]{2,1,0:T(8,128)(2,1)S(1)}, u32[]{:S(2)}, u32[]{:S(2)}) collective-permute-start(bf16[4,256,512]{2,1,0:T(8,128)(2,1)} %get-tuple-element.32), channel_id=1, source_target_pairs={{0,1},{1,0},{2,3},{3,2},{4,5},{5,4},{6,7},{7,6},{8,9},{9,8},{10,11... | collective-permute-start | bytes 3145736 | tf_op jit(solution)/shard_map/ppermute | solution.py:261
  7.5 14.2 %collective-permute-start.2 = (bf16[2,256,512]{2,1,0:T(8,128)(2,1)S(1)}, bf16[2,256,512]{2,1,0:T(8,128)(2,1)S(1)}, u32[]{:S(2)}, u32[]{:S(2)}) collective-permute-start(bf16[2,256,512]{2,1,0:T(8,128)(2,1)S(1)} %copy-done.4), channel_id=1, source_target_pairs={{0,6},{1,7},{2,0},{3,1},{4,2},{5,3},{6,4},{7,5},{8,14},{9,15},{10,... | collective-permute-start | bytes 1572872 | tf_op jit(solution)/shard_map/ppermute | solution.py:258
  10.8 14.5 %collective-permute-start.1 = (bf16[2,2,128,128]{3,2,1,0:T(8,128)(2,1)S(1)}, bf16[2,2,128,128]{3,2,1,0:T(8,128)(2,1)S(1)}, u32[]{:S(2)}, u32[]{:S(2)}) collective-permute-start(bf16[2,2,128,128]{3,2,1,0:T(8,128)(2,1)S(1)} %shard_map.100), channel_id=1, source_target_pairs={{0,8},{8,0},{16,24},{24,16},{32,40},{40,32},{48,56},{56,48},{64,72... | collective-permute-start | bytes 393224 | tf_op jit(solution)/shard_map/ppermute | solution.py:173
  13.6 14.7 %collective-permute-start.4 = (bf16[256,512]{1,0:T(8,128)(2,1)S(1)}, bf16[256,512]{1,0:T(8,128)(2,1)S(1)}, u32[]{:S(2)}, u32[]{:S(2)}) collective-permute-start(bf16[256,512]{1,0:T(8,128)(2,1)S(1)} %slice_bitcast_fusion.1), channel_id=1, source_target_pairs={{0,2},{1,3},{2,4},{3,5},{4,6},{5,7},{6,0},{7,1},{8,10},{9,11},{10,... | collective-permute-start | bytes 786440 | tf_op jit(solution)/shard_map/ppermute | solution.py:258
  21.8 8.2 %collective-permute-start.5 = (bf16[256,512]{1,0:T(8,128)(2,1)S(1)}, bf16[256,512]{1,0:T(8,128)(2,1)S(1)}, u32[]{:S(2)}, u32[]{:S(2)}) collective-permute-start(bf16[256,512]{1,0:T(8,128)(2,1)S(1)} %slice_bitcast_fusion), channel_id=1, source_target_pairs={{0,6},{1,7},{2,0},{3,1},{4,2},{5,3},{6,4},{7,5},{8,14},{9,15},{10,... | collective-permute-start | bytes 786440 | tf_op jit(solution)/shard_map/ppermute | solution.py:258
  25.3 8.8 %collective-permute-start.6 = (bf16[2,2,128,128]{3,2,1,0:T(8,128)(2,1)S(1)}, bf16[2,2,128,128]{3,2,1,0:T(8,128)(2,1)S(1)}, u32[]{:S(2)}, u32[]{:S(2)}) collective-permute-start(bf16[2,2,128,128]{3,2,1,0:T(8,128)(2,1)S(1)} %fusion), channel_id=1, source_target_pairs={{0,16},{8,24},{16,0},{24,8},{32,48},{40,56},{48,32},{56,40},{64,80... | collective-permute-start | bytes 393224 | tf_op jit(solution)/shard_map/ppermute | solution.py:173
  28.2 12.2 %copy-start.3 = (bf16[2,256,256]{2,1,0:T(8,128)(2,1)S(1)}, bf16[2,256,256]{2,1,0:T(8,128)(2,1)}, u32[]{:S(2)}) copy-start(bf16[2,256,256]{2,1,0:T(8,128)(2,1)} %q_ref.3) | copy-start | bytes 786436
  28.2 12.2 %copy-start.5 = (bf16[2,256,256]{2,1,0:T(8,128)(2,1)S(1)}, bf16[2,256,256]{2,1,0:T(8,128)(2,1)}, u32[]{:S(2)}) copy-start(bf16[2,256,256]{2,1,0:T(8,128)(2,1)} %gate_ref.1) | copy-start | bytes 786436
  34.1 6.3 %collective-permute-start.7 = (f32[2,256,256]{2,1,0:T(8,128)S(1)}, f32[2,256,256]{2,1,0:T(8,128)S(1)}, u32[]{:S(2)}, u32[]{:S(2)}) collective-permute-start(f32[2,256,256]{2,1,0:T(8,128)S(1)} %get-tuple-element.38), channel_id=1, source_target_pairs={{0,1},{1,0},{2,3},{3,2},{4,5},{5,4},{6,7},{7,6},{8,9},{9,8},{10,11... | collective-permute-start | bytes 1572872 | tf_op jit(solution)/shard_map/ppermute | solution.py:261
  35.0 11.9 %collective-permute-start.9 = (bf16[2,2,128,128]{3,2,1,0:T(8,128)(2,1)S(1)}, bf16[2,2,128,128]{3,2,1,0:T(8,128)(2,1)S(1)}, u32[]{:S(2)}, u32[]{:S(2)}) collective-permute-start(bf16[2,2,128,128]{3,2,1,0:T(8,128)(2,1)S(1)} %fusion.7), channel_id=1, source_target_pairs={{0,32},{8,40},{16,48},{24,56},{32,0},{40,8},{48,16},{56,24},{64,96... | collective-permute-start | bytes 393224 | tf_op jit(solution)/shard_map/ppermute | solution.py:173
  40.8 8.1 %collective-permute-start.8 = (bf16[2,2,128,128]{3,2,1,0:T(8,128)(2,1)S(1)}, bf16[2,2,128,128]{3,2,1,0:T(8,128)(2,1)S(1)}, u32[]{:S(2)}, u32[]{:S(2)}) collective-permute-start(bf16[2,2,128,128]{3,2,1,0:T(8,128)(2,1)S(1)} %get-tuple-element.39), channel_id=1, source_target_pairs={{0,8},{8,0},{16,24},{24,16},{32,40},{40,32},{48,56},{56,48},{64,72... | collective-permute-start | bytes 393224 | tf_op jit(solution)/shard_map/ppermute | solution.py:173
  48.9 4.7 %collective-permute-start.11 = (bf16[2,2,128,128]{3,2,1,0:T(8,128)(2,1)S(1)}, bf16[2,2,128,128]{3,2,1,0:T(8,128)(2,1)S(1)}, u32[]{:S(2)}, u32[]{:S(2)}) collective-permute-start(bf16[2,2,128,128]{3,2,1,0:T(8,128)(2,1)S(1)} %fusion.15), channel_id=1, source_target_pairs={{0,64},{8,72},{16,80},{24,88},{32,96},{40,104},{48,112},{56,120},{... | collective-permute-start | bytes 393224 | tf_op jit(solution)/shard_map/ppermute | solution.py:173
  50.2 8.2 %collective-permute-start.12 = (bf16[2,2,128,128]{3,2,1,0:T(8,128)(2,1)S(1)}, bf16[2,2,128,128]{3,2,1,0:T(8,128)(2,1)S(1)}, u32[]{:S(2)}, u32[]{:S(2)}) collective-permute-start(bf16[2,2,128,128]{3,2,1,0:T(8,128)(2,1)S(1)} %fusion.15), channel_id=1, source_target_pairs={{0,128},{8,136},{16,144},{24,152},{32,160},{40,168},{48,176},{56,1... | collective-permute-start | bytes 393224 | tf_op jit(solution)/shard_map/ppermute | solution.py:173
  52.7 8.3 %collective-permute-start.13 = (bf16[2,2,128,128]{3,2,1,0:T(8,128)(2,1)S(1)}, bf16[2,2,128,128]{3,2,1,0:T(8,128)(2,1)S(1)}, u32[]{:S(2)}, u32[]{:S(2)}) collective-permute-start(bf16[2,2,128,128]{3,2,1,0:T(8,128)(2,1)S(1)} %fusion.15), channel_id=1, source_target_pairs={{0,192},{8,200},{16,208},{24,216},{32,224},{40,232},{48,240},{56,2... | collective-permute-start | bytes 393224 | tf_op jit(solution)/shard_map/ppermute | solution.py:173
  52.9 28.7 %copy-start.6 = (s32[8]{0:T(128)S(1)}, s32[8]{0:T(128)}, u32[]{:S(2)}) copy-start(s32[8]{0:T(128)} %fusion.20.table_ref) | copy-start | bytes 100
  52.9 10.7 %collective-permute-start.10 = (bf16[2,2,128,128]{3,2,1,0:T(8,128)(2,1)S(1)}, bf16[2,2,128,128]{3,2,1,0:T(8,128)(2,1)}, u32[]{:S(2)}, u32[]{:S(2)}) collective-permute-start(bf16[2,2,128,128]{3,2,1,0:T(8,128)(2,1)S(1)} %fusion.8), channel_id=1, source_target_pairs={{0,16},{8,24},{16,0},{24,8},{32,48},{40,56},{48,32},{56,40},{64,80... | collective-permute-start | bytes 393224 | tf_op jit(solution)/shard_map/ppermute | solution.py:173
  64.6 8.8 %collective-permute-start.14 = (bf16[2,2,128,128]{3,2,1,0:T(8,128)(2,1)S(1)}, bf16[2,2,128,128]{3,2,1,0:T(8,128)(2,1)S(1)}, u32[]{:S(2)}, u32[]{:S(2)}) collective-permute-start(bf16[2,2,128,128]{3,2,1,0:T(8,128)(2,1)S(1)} %fusion.16), channel_id=1, source_target_pairs={{0,32},{8,40},{16,48},{24,56},{32,0},{40,8},{48,16},{56,24},{64,96... | collective-permute-start | bytes 393224 | tf_op jit(solution)/shard_map/ppermute | solution.py:173
  73.5 4.1 %collective-permute-start.15 = (bf16[2,2,128,128]{3,2,1,0:T(8,128)(2,1)S(1)}, bf16[2,2,128,128]{3,2,1,0:T(8,128)(2,1)S(1)}, u32[]{:S(2)}, u32[]{:S(2)}) collective-permute-start(bf16[2,2,128,128]{3,2,1,0:T(8,128)(2,1)S(1)} %fusion.17), channel_id=1, source_target_pairs={{0,64},{8,72},{16,80},{24,88},{32,96},{40,104},{48,112},{56,120},{... | collective-permute-start | bytes 393224 | tf_op jit(solution)/shard_map/ppermute | solution.py:173
  73.7 5.5 %collective-permute-start.16 = (bf16[2,2,128,128]{3,2,1,0:T(8,128)(2,1)S(1)}, bf16[2,2,128,128]{3,2,1,0:T(8,128)(2,1)S(1)}, u32[]{:S(2)}, u32[]{:S(2)}) collective-permute-start(bf16[2,2,128,128]{3,2,1,0:T(8,128)(2,1)S(1)} %fusion.17), channel_id=1, source_target_pairs={{0,128},{8,136},{16,144},{24,152},{32,160},{40,168},{48,176},{56,1... | collective-permute-start | bytes 393224 | tf_op jit(solution)/shard_map/ppermute | solution.py:173
  74.7 5.9 %collective-permute-start.17 = (bf16[2,2,128,128]{3,2,1,0:T(8,128)(2,1)S(1)}, bf16[2,2,128,128]{3,2,1,0:T(8,128)(2,1)S(1)}, u32[]{:S(2)}, u32[]{:S(2)}) collective-permute-start(bf16[2,2,128,128]{3,2,1,0:T(8,128)(2,1)S(1)} %fusion.17), channel_id=1, source_target_pairs={{0,192},{8,200},{16,208},{24,216},{32,224},{40,232},{48,240},{56,2... | collective-permute-start | bytes 393224 | tf_op jit(solution)/shard_map/ppermute | solution.py:173
  86.6 10.2 %collective-permute-start.18 = (bf16[4,2,256,512]{3,2,1,0:T(8,128)(2,1)S(1)}, bf16[4,2,256,512]{3,2,1,0:T(8,128)(2,1)S(1)}, u32[]{:S(2)}, u32[]{:S(2)}) collective-permute-start(bf16[4,2,256,512]{3,2,1,0:T(8,128)(2,1)S(1)} %shard_map.107), channel_id=1, source_target_pairs={{0,1},{1,0},{2,3},{3,2},{4,5},{5,4},{6,7},{7,6},{8,9},{9,8},{10,11... | collective-permute-start | bytes 6291464 | tf_op jit(solution)/shard_map/ppermute | solution.py:261
  96.9 8.6 %collective-permute-start.23 = (bf16[256,512]{1,0:T(8,128)(2,1)S(1)}, bf16[256,512]{1,0:T(8,128)(2,1)S(1)}, u32[]{:S(2)}, u32[]{:S(2)}) collective-permute-start(bf16[256,512]{1,0:T(8,128)(2,1)S(1)} %get-tuple-element.54), channel_id=1, source_target_pairs={{0,6},{1,7},{2,0},{3,1},{4,2},{5,3},{6,4},{7,5},{8,14},{9,15},{10,... | collective-permute-start | bytes 786440 | tf_op jit(solution)/shard_map/ppermute | solution.py:258
  99.7 9.3 %collective-permute-start.20 = (bf16[256,512]{1,0:T(8,128)(2,1)S(1)}, bf16[256,512]{1,0:T(8,128)(2,1)S(1)}, u32[]{:S(2)}, u32[]{:S(2)}) collective-permute-start(bf16[256,512]{1,0:T(8,128)(2,1)S(1)} %get-tuple-element.52), channel_id=1, source_target_pairs={{0,2},{1,3},{2,4},{3,5},{4,6},{5,7},{6,0},{7,1},{8,10},{9,11},{10,... | collective-permute-start | bytes 786440 | tf_op jit(solution)/shard_map/ppermute | solution.py:258
  99.8 11.2 %collective-permute-start.19 = (bf16[256,512]{1,0:T(8,128)(2,1)S(1)}, bf16[256,512]{1,0:T(8,128)(2,1)S(1)}, u32[]{:S(2)}, u32[]{:S(2)}) collective-permute-start(bf16[256,512]{1,0:T(8,128)(2,1)S(1)} %get-tuple-element.51), channel_id=1, source_target_pairs={{0,6},{1,7},{2,0},{3,1},{4,2},{5,3},{6,4},{7,5},{8,14},{9,15},{10,... | collective-permute-start | bytes 786440 | tf_op jit(solution)/shard_map/ppermute | solution.py:258
  102.6 11.6 %collective-permute-start.22 = (bf16[256,512]{1,0:T(8,128)(2,1)S(1)}, bf16[256,512]{1,0:T(8,128)(2,1)S(1)}, u32[]{:S(2)}, u32[]{:S(2)}) collective-permute-start(bf16[256,512]{1,0:T(8,128)(2,1)S(1)} %get-tuple-element.53), channel_id=1, source_target_pairs={{0,2},{1,3},{2,4},{3,5},{4,6},{5,7},{6,0},{7,1},{8,10},{9,11},{10,... | collective-permute-start | bytes 786440 | tf_op jit(solution)/shard_map/ppermute | solution.py:258
  105.5 11.1 %collective-permute-start.24 = (bf16[256,512]{1,0:T(8,128)(2,1)S(1)}, bf16[256,512]{1,0:T(8,128)(2,1)S(1)}, u32[]{:S(2)}, u32[]{:S(2)}) collective-permute-start(bf16[256,512]{1,0:T(8,128)(2,1)S(1)} %shard_map.111), channel_id=1, source_target_pairs={{0,6},{1,7},{2,0},{3,1},{4,2},{5,3},{6,4},{7,5},{8,14},{9,15},{10,... | collective-permute-start | bytes 786440 | tf_op jit(solution)/shard_map/ppermute | solution.py:258
  109.1 10.6 %collective-permute-start.21 = (bf16[256,512]{1,0:T(8,128)(2,1)S(1)}, bf16[256,512]{1,0:T(8,128)(2,1)S(1)}, u32[]{:S(2)}, u32[]{:S(2)}) collective-permute-start(bf16[256,512]{1,0:T(8,128)(2,1)S(1)} %shard_map.110), channel_id=1, source_target_pairs={{0,2},{1,3},{2,4},{3,5},{4,6},{5,7},{6,0},{7,1},{8,10},{9,11},{10,... | collective-permute-start | bytes 786440 | tf_op jit(solution)/shard_map/ppermute | solution.py:258

commit v4 on v1

--- a/solution.py
+++ b/solution.py
@@ -6,12 +6,12 @@
 from jax.sharding import PartitionSpec as P
 
 HD = 128
-VMEM_LIMIT = 32 * 1024 * 1024
+MIB = 1024 * 1024
 RELATIVE = (0, -1, 1, 2)
 
 
-def params():
-    return pltpu.CompilerParams(vmem_limit_bytes=VMEM_LIMIT)
+def params(mib=32):
+    return pltpu.CompilerParams(vmem_limit_bytes=mib * MIB)
 
 
 def cost(flops, moved):
@@ -145,14 +145,59 @@
         return jnp.where(take, x.astype(jnp.float32), 0.0)
 
     total, entering = state, jnp.zeros(state.shape, jnp.float32)
-    for bit in (1, 2, 4):
-        theirs = swap(total, bit)
+    for bit, by in ((1, 1), (2, 2), (4, 7)):
+        theirs = swap(total, by)
         entering = entering + counted(theirs, bit)
         total = (total.astype(jnp.float32) + theirs.astype(jnp.float32)).astype(jnp.bfloat16)
     swapped = [swap(total, by) for by in (8, 16, 24)]
     for theirs, bit in zip(swapped, (8, 16, 16)):
         entering = entering + counted(theirs, bit)
     return entering.astype(jnp.bfloat16)
+
+
+def make_sum_kernel(counts):
+    def sum_kernel(*refs):
+        terms, outs = refs[: sum(counts)], refs[sum(counts) :]
+        first = 0
+        for at, count in enumerate(counts):
+            total = terms[first][...].astype(jnp.float32).reshape(terms[first].shape[-2:])
+            for term in terms[first + 1 : first + count]:
+                total = total + term[...].astype(jnp.float32).reshape(total.shape)
+            if len(outs) == len(counts):
+                outs[at][...] = total.astype(jnp.bfloat16)
+            else:
+                outs[0][at] = total.astype(jnp.bfloat16)
+            first += count
+
+    return sum_kernel
+
+
+def sums(groups, shape, stacked=False):
+    arrays, specs = [], []
+    for group in groups:
+        for term in group:
+            if isinstance(term, tuple):
+                array, place, s = term
+                arrays.append(array)
+                specs.append(pl.BlockSpec((1, 1) + shape, lambda i, at=(place, s): at + (0, 0)))
+            else:
+                arrays.append(term)
+                specs.append(whole(shape))
+    if stacked:
+        outs = jax.ShapeDtypeStruct((len(groups),) + shape, jnp.bfloat16)
+        out_specs = whole(outs.shape)
+    else:
+        outs = [jax.ShapeDtypeStruct(shape, jnp.bfloat16)] * len(groups)
+        out_specs = [whole(shape)] * len(groups)
+    return pl.pallas_call(
+        make_sum_kernel([len(group) for group in groups]),
+        out_shape=outs,
+        grid=(1,),
+        in_specs=specs,
+        out_specs=out_specs,
+        compiler_params=params(8),
+        cost_estimate=cost(0, (len(arrays) + len(groups)) * shape[0] * shape[1] * 2),
+    )(*arrays)
 
 
 def body(queries, keys, values, gate_pre, grad_out, w_query, w_key, w_value, w_gate, w_out):
@@ -292,17 +337,19 @@
     own = project(4)
 
     def chip(place, s):
-        return own[place, s].astype(f32) + theirs[place, s].astype(f32)
-
-    up_far = along_y(chip(3, 0).astype(bf16), 1)
-    down_far = along_y(chip(3, 1).astype(bf16), -1)
-    up_near = along_y(chip(2, 1).astype(bf16), 1)
-    down_near = along_y(chip(1, 0).astype(bf16), -1)
-    up_last = along_y((chip(2, 0) + up_far.astype(f32)).astype(bf16), 1)
-    down_last = along_y((chip(1, 1) + down_far.astype(f32)).astype(bf16), -1)
-    out0 = chip(0, 0) + down_near.astype(f32) + up_last.astype(f32)
-    out1 = chip(0, 1) + up_near.astype(f32) + down_last.astype(f32)
-    return jnp.stack([out0, out1]).astype(bf16)
+        return [(own, place, s), (theirs, place, s)]
+
+    far0, far1 = sums([chip(3, 0), chip(3, 1)], flat)
+    up_far = along_y(far0, 1)
+    down_far = along_y(far1, -1)
+    near1, near0 = sums([chip(2, 1), chip(1, 0)], flat)
+    up_near = along_y(near1, 1)
+    down_near = along_y(near0, -1)
+    (last0,) = sums([chip(2, 0) + [up_far]], flat)
+    (last1,) = sums([chip(1, 1) + [down_far]], flat)
+    up_last = along_y(last0, 1)
+    down_last = along_y(last1, -1)
+    return sums([chip(0, 0) + [down_near, up_last], chip(0, 1) + [up_near, down_last]], flat, stacked=True)
 
 
 def solution(mesh):

time: 113 us -> 113 us (level)
  the two profiles are of different devices: /device:TPU:6 before, /device:TPU:1 now
where the time goes in v4:
time: 113 us
  starting transfers between devices  44.8 us (40%)
  waiting for transfers between devices  44.4 us (39%)
  Pallas kernels  18.4 us (16%)
  local copies, waits for them, and re-layouts  2.61 us (2%)
  other arithmetic  2.37 us (2%)
    ppermute x12, waiting for transfers between devices, along_y(): lax.ppermute(x, 'head', [(i, (i + 2 * by) % peers) for i in range(peers)])  23.2 us
    ppermute x12, waiting for transfers between devices, swap(): return lax.ppermute(x, 'seq', [(i, i ^ by) for i in range(peers)])  19.8 us
    ppermute x12, starting transfers between devices, swap(): return lax.ppermute(x, 'seq', [(i, i ^ by) for i in range(peers)])  18.6 us
    ppermute x12, starting transfers between devices, along_y(): lax.ppermute(x, 'head', [(i, (i + 2 * by) % peers) for i in range(peers)])  17.2 us
    ppermute x3, starting transfers between devices, other_core(): return lax.ppermute(x, 'head', [(i, i ^ 1) for i in range(peers)])  8.96 us
    pallas_call x2, Pallas kernels, project(): pl.pallas_call(make_project_kernel(factor), out_shape=jax.ShapeDtypeStruc...  7.8 us
    unnamed x20, local copies, waits for them, and re-layouts  2.57 us
    pallas_call x1, Pallas kernels, body(): pl.pallas_call(make_inner_kernel(factor), out_shape=[jax.ShapeDtypeStruct...  2.54 us
  transfers between devices with their start and end apart: 27, of which 17 were waited for; matrix products, arithmetic and copies ran while one was open for 2% of the time, Pallas kernels for 9%

profile of v4, /device:TPU:1, one launch (start us, length us, event | category | flops | bytes accessed | tf_op | source)
XLA Modules:
  0.0 112.9 jit_solution(5691349225729402517)
XLA Ops:
  0.0 1.6 %copy-done = bf16[256,4096]{1,0:T(8,128)(2,1)S(1)} copy-done((bf16[256,4096]{1,0:T(8,128)(2,1)S(1)}, bf16[256,4096]{1,0:T(8,128)(2,1)}, u32[]{:S(2)}) %copy-start) | copy-done | bytes 2097176
  1.6 0.8 shard_map.100
  2.4 3.3 %collective-permute-start.4 = (bf16[4,256,512]{2,1,0:T(8,128)(2,1)S(1)}, bf16[4,256,512]{2,1,0:T(8,128)(2,1)S(1)}, u32[]{:S(2)}, u32[]{:S(2)}) collective-permute-start(bf16[4,256,512]{2,1,0:T(8,128)(2,1)S(1)} %shard_map.100), channel_id=1, source_target_pairs={{0,1},{1,0},{2,3},{3,2},{4,5},{5,4},{6,7},{7,6},{8,9},{9,8},{10,11... | collective-permute-start | bytes 3145736 | tf_op jit(solution)/shard_map/ppermute | solution.py:226
  5.9 2.7 %collective-permute-start.3 = (bf16[256,512]{1,0:T(8,128)(2,1)S(1)}, bf16[256,512]{1,0:T(8,128)(2,1)S(1)}, u32[]{:S(2)}, u32[]{:S(2)}) collective-permute-start(bf16[256,512]{1,0:T(8,128)(2,1)S(1)} %get-tuple-element.35), channel_id=1, source_target_pairs={{0,6},{1,7},{2,0},{3,1},{4,2},{5,3},{6,4},{7,5},{8,14},{9,15},{10,... | collective-permute-start | bytes 786440 | tf_op jit(solution)/shard_map/ppermute | solution.py:223
  8.5 2.7 %collective-permute-start.2 = (bf16[256,512]{1,0:T(8,128)(2,1)S(1)}, bf16[256,512]{1,0:T(8,128)(2,1)S(1)}, u32[]{:S(2)}, u32[]{:S(2)}) collective-permute-start(bf16[256,512]{1,0:T(8,128)(2,1)S(1)} %get-tuple-element.36), channel_id=1, source_target_pairs={{0,6},{1,7},{2,0},{3,1},{4,2},{5,3},{6,4},{7,5},{8,14},{9,15},{10,... | collective-permute-start | bytes 786440 | tf_op jit(solution)/shard_map/ppermute | solution.py:223
  11.2 3.6 %collective-permute-done.a0 = bf16[256,512]{1,0:T(8,128)(2,1)S(1)} collective-permute-done((bf16[256,512]{1,0:T(8,128)(2,1)S(1)}, bf16[256,512]{1,0:T(8,128)(2,1)S(1)}, u32[]{:S(2)}, u32[]{:S(2)}) %collective-permute-start) | collective-permute-done | bytes 262176 | tf_op jit(solution)/shard_map/ppermute | solution.py:223
  14.9 2.7 %collective-permute-start.6 = (bf16[256,512]{1,0:T(8,128)(2,1)S(1)}, bf16[256,512]{1,0:T(8,128)(2,1)S(1)}, u32[]{:S(2)}, u32[]{:S(2)}) collective-permute-start(bf16[256,512]{1,0:T(8,128)(2,1)S(1)} %collective-permute-done.3.b1), channel_id=1, source_target_pairs={{0,6},{1,7},{2,0},{3,1},{4,2},{5,3},{6,4},{7,5},{8,14},{9,15},{10,... | collective-permute-start | bytes 786440 | tf_op jit(solution)/shard_map/ppermute | solution.py:223
  17.5 2.9 %collective-permute-done.1.a1 = bf16[256,512]{1,0:T(8,128)(2,1)S(1)} collective-permute-done((bf16[256,512]{1,0:T(8,128)(2,1)S(1)}, bf16[256,512]{1,0:T(8,128)(2,1)S(1)}, u32[]{:S(2)}, u32[]{:S(2)}) %collective-permute-start.1) | collective-permute-done | bytes 262176 | tf_op jit(solution)/shard_map/ppermute | solution.py:223
  20.5 2.1 %shard_map.101 = (f32[2,256,256]{2,1,0:T(8,128)S(1)}, f32[2,256,256]{2,1,0:T(8,128)S(1)}) custom-call(s32[8]{0:T(128)S(1)} %fusion.20.table_ref, bf16[2,256,512]{2,1,0:T(8,128)(2,1)S(1)} %copy-done.7, bf16[256,512]{1,0:T(8,128)(2,1)S(1)} %collective-permute-done.a0, bf16[256,512]{1,0:T(8,128)(2,1)S(1)} %collective-permute-done.1.a1, ...), custom_call_target="tpu_custom_call" | custom-call | flops 805306368 | bytes 4194304 | tf_op jit(solution)/shard_map/pallas_call | solution.py:261
  22.6 3.5 %collective-permute-done.5.c0 = bf16[256,512]{1,0:T(8,128)(2,1)S(1)} collective-permute-done((bf16[256,512]{1,0:T(8,128)(2,1)S(1)}, bf16[256,512]{1,0:T(8,128)(2,1)S(1)}, u32[]{:S(2)}, u32[]{:S(2)}) %collective-permute-start.5) | collective-permute-done | bytes 262176 | tf_op jit(solution)/shard_map/ppermute | solution.py:223
  26.1 1.8 %shard_map.102 = (f32[2,256,256]{2,1,0:T(8,128)S(1)}, f32[2,256,256]{2,1,0:T(8,128)}) custom-call(s32[8]{0:T(128)S(1)} %fusion.20.table_ref, f32[2,256,256]{2,1,0:T(8,128)S(1)} %get-tuple-element.20.mine_in, f32[2,256,256]{2,1,0:T(8,128)S(1)} %get-tuple-element.21.other_in, bf16[256,512]{1,0:T(8,128)(2,1)S(1)} %collective-permute-done.5.c0, ...), custom_call_target="tpu_custom_call" | custom-call | flops 268435456 | bytes 3145728 | tf_op jit(solution)/shard_map/pallas_call | solution.py:278
  27.9 1.0 collective-permute-start.7
  28.9 0.3 shard_map.104
  29.3 1.5 %collective-permute-done.7.theirs_ref = f32[2,256,256]{2,1,0:T(8,128)} collective-permute-done((f32[2,256,256]{2,1,0:T(8,128)}, f32[2,256,256]{2,1,0:T(8,128)}, u32[]{:S(2)}, u32[]{:S(2)}) %collective-permute-start.7) | collective-permute-done | bytes 524320 | tf_op jit(solution)/shard_map/ppermute | solution.py:226
  30.8 0.9 copy-done.9
  31.7 1.5 %shard_map.103 = (bf16[2,256,256]{2,1,0:T(8,128)(2,1)S(1)}, f32[2,256,256]{2,1,0:T(8,128)S(1)}, bf16[2,2,128,128]{3,2,1,0:T(8,128)(2,1)S(1)}) custom-call(f32[2,256,256]{2,1,0:T(8,128)S(1)} %get-tuple-element.22.mine_ref, f32[2,256,256]{2,1,0:T(8,128)} %collective-permute-done.7.theirs_ref, bf16[2,256,256]{2,1,0:T(8,128)(2,1)S(1)} %copy-done.9, ...), custom_call_target="tpu_custom_call" | custom-call | flops 33554432 | bytes 3145728 | tf_op jit(solution)/shard_map/pallas_call | solution.py:297
  33.3 1.1 collective-permute-done.8
  34.5 0.9 fusion.6
  35.4 1.9 %collective-permute-start.9 = (bf16[2,2,128,128]{3,2,1,0:T(8,128)(2,1)S(1)}, bf16[2,2,128,128]{3,2,1,0:T(8,128)(2,1)S(1)}, u32[]{:S(2)}, u32[]{:S(2)}) collective-permute-start(bf16[2,2,128,128]{3,2,1,0:T(8,128)(2,1)S(1)} %fusion.6), channel_id=1, source_target_pairs={{0,16},{8,24},{16,0},{24,8},{32,48},{40,56},{48,32},{56,40},{64,80... | collective-permute-start | bytes 393224 | tf_op jit(solution)/shard_map/ppermute | solution.py:141
  37.3 0.7 collective-permute-done.14
  38.1 1.7 %collective-permute-start.15 = (bf16[2,2,128,128]{3,2,1,0:T(8,128)(2,1)S(1)}, bf16[2,2,128,128]{3,2,1,0:T(8,128)(2,1)S(1)}, u32[]{:S(2)}, u32[]{:S(2)}) collective-permute-start(bf16[2,2,128,128]{3,2,1,0:T(8,128)(2,1)S(1)} %fusion.15), channel_id=1, source_target_pairs={{0,16},{8,24},{16,0},{24,8},{32,48},{40,56},{48,32},{56,40},{64,80... | collective-permute-start | bytes 393224 | tf_op jit(solution)/shard_map/ppermute | solution.py:141
  39.8 6.8 %collective-permute-done.9 = bf16[2,2,128,128]{3,2,1,0:T(8,128)(2,1)S(1)} collective-permute-done((bf16[2,2,128,128]{3,2,1,0:T(8,128)(2,1)S(1)}, bf16[2,2,128,128]{3,2,1,0:T(8,128)(2,1)S(1)}, u32[]{:S(2)}, u32[]{:S(2)}) %collective-permute-start.9) | collective-permute-done | bytes 131104 | tf_op jit(solution)/shard_map/ppermute | solution.py:141
  46.7 4.1 %collective-permute-start.10 = (bf16[2,2,128,128]{3,2,1,0:T(8,128)(2,1)S(1)}, bf16[2,2,128,128]{3,2,1,0:T(8,128)(2,1)S(1)}, u32[]{:S(2)}, u32[]{:S(2)}) collective-permute-start(bf16[2,2,128,128]{3,2,1,0:T(8,128)(2,1)S(1)} %fusion.7), channel_id=1, source_target_pairs={{0,56},{8,48},{16,40},{24,32},{32,24},{40,16},{48,8},{56,0},{64,12... | collective-permute-start | bytes 393224 | tf_op jit(solution)/shard_map/ppermute | solution.py:141
  50.9 2.8 %collective-permute-start.16 = (bf16[2,2,128,128]{3,2,1,0:T(8,128)(2,1)S(1)}, bf16[2,2,128,128]{3,2,1,0:T(8,128)(2,1)S(1)}, u32[]{:S(2)}, u32[]{:S(2)}) collective-permute-start(bf16[2,2,128,128]{3,2,1,0:T(8,128)(2,1)S(1)} %fusion.16), channel_id=1, source_target_pairs={{0,56},{8,48},{16,40},{24,32},{32,24},{40,16},{48,8},{56,0},{64,12... | collective-permute-start | bytes 393224 | tf_op jit(solution)/shard_map/ppermute | solution.py:141
  53.6 4.2 %collective-permute-done.10 = bf16[2,2,128,128]{3,2,1,0:T(8,128)(2,1)S(1)} collective-permute-done((bf16[2,2,128,128]{3,2,1,0:T(8,128)(2,1)S(1)}, bf16[2,2,128,128]{3,2,1,0:T(8,128)(2,1)S(1)}, u32[]{:S(2)}, u32[]{:S(2)}) %collective-permute-start.10) | collective-permute-done | bytes 131104 | tf_op jit(solution)/shard_map/ppermute | solution.py:141
  57.9 1.3 %collective-permute-start.11 = (bf16[2,2,128,128]{3,2,1,0:T(8,128)(2,1)S(1)}, bf16[2,2,128,128]{3,2,1,0:T(8,128)(2,1)S(1)}, u32[]{:S(2)}, u32[]{:S(2)}) collective-permute-start(bf16[2,2,128,128]{3,2,1,0:T(8,128)(2,1)S(1)} %fusion.8), channel_id=1, source_target_pairs={{0,64},{8,72},{16,80},{24,88},{32,96},{40,104},{48,112},{56,120},{... | collective-permute-start | bytes 393224 | tf_op jit(solution)/shard_map/ppermute | solution.py:141
  59.2 2.5 %collective-permute-start.12 = (bf16[2,2,128,128]{3,2,1,0:T(8,128)(2,1)S(1)}, bf16[2,2,128,128]{3,2,1,0:T(8,128)(2,1)S(1)}, u32[]{:S(2)}, u32[]{:S(2)}) collective-permute-start(bf16[2,2,128,128]{3,2,1,0:T(8,128)(2,1)S(1)} %fusion.8), channel_id=1, source_target_pairs={{0,128},{8,136},{16,144},{24,152},{32,160},{40,168},{48,176},{56,1... | collective-permute-start | bytes 393224 | tf_op jit(solution)/shard_map/ppermute | solution.py:141
  61.7 0.2 collective-permute-start.13
  61.9 0.6 collective-permute-done.16
  62.5 1.3 %collective-permute-start.17 = (bf16[2,2,128,128]{3,2,1,0:T(8,128)(2,1)S(1)}, bf16[2,2,128,128]{3,2,1,0:T(8,128)(2,1)S(1)}, u32[]{:S(2)}, u32[]{:S(2)}) collective-permute-start(bf16[2,2,128,128]{3,2,1,0:T(8,128)(2,1)S(1)} %fusion.17), channel_id=1, source_target_pairs={{0,64},{8,72},{16,80},{24,88},{32,96},{40,104},{48,112},{56,120},{... | collective-permute-start | bytes 393224 | tf_op jit(solution)/shard_map/ppermute | solution.py:141
  63.8 2.5 %collective-permute-start.18 = (bf16[2,2,128,128]{3,2,1,0:T(8,128)(2,1)S(1)}, bf16[2,2,128,128]{3,2,1,0:T(8,128)(2,1)S(1)}, u32[]{:S(2)}, u32[]{:S(2)}) collective-permute-start(bf16[2,2,128,128]{3,2,1,0:T(8,128)(2,1)S(1)} %fusion.17), channel_id=1, source_target_pairs={{0,128},{8,136},{16,144},{24,152},{32,160},{40,168},{48,176},{56,1... | collective-permute-start | bytes 393224 | tf_op jit(solution)/shard_map/ppermute | solution.py:141
  66.5 0.4 collective-permute-done.13
  66.8 1.1 fusion.5.prefix_ref
  67.9 2.5 %shard_map.105 = (bf16[2,256,256]{2,1,0:T(8,128)(2,1)S(1)}, bf16[2,256,256]{2,1,0:T(8,128)(2,1)S(1)}, f32[2,256,256]{2,1,0:T(8,128)S(1)}, f32[2,256,256]{2,1,0:T(8,128)S(1)}) custom-call(bf16[2,256,256]{2,1,0:T(8,128)(2,1)S(1)} %copy-done.8, bf16[2,256,256]{2,1,0:T(8,128)(2,1)S(1)} %copy-done.5, bf16[2,256,256]{2,1,0:T(8,128)(2,1)S(1)} %copy-done.6, ...), custom_call_target="tpu_custom_call" | custom-call | flops 402653184 | bytes 3145728 | tf_op jit(solution)/shard_map/pallas_call | solution.py:310
  70.4 2.0 %collective-permute-done.18 = bf16[2,2,128,128]{3,2,1,0:T(8,128)(2,1)S(1)} collective-permute-done((bf16[2,2,128,128]{3,2,1,0:T(8,128)(2,1)S(1)}, bf16[2,2,128,128]{3,2,1,0:T(8,128)(2,1)S(1)}, u32[]{:S(2)}, u32[]{:S(2)}) %collective-permute-start.18) | collective-permute-done | bytes 131104 | tf_op jit(solution)/shard_map/ppermute | solution.py:141
  72.5 3.9 %collective-permute-done.19 = bf16[2,2,128,128]{3,2,1,0:T(8,128)(2,1)S(1)} collective-permute-done((bf16[2,2,128,128]{3,2,1,0:T(8,128)(2,1)S(1)}, bf16[2,2,128,128]{3,2,1,0:T(8,128)(2,1)S(1)}, u32[]{:S(2)}, u32[]{:S(2)}) %collective-permute-start.19) | collective-permute-done | bytes 131104 | tf_op jit(solution)/shard_map/ppermute | solution.py:141
  76.6 3.9 %shard_map.107 = bf16[4,2,256,512]{3,2,1,0:T(8,128)(2,1)S(1)} custom-call(s32[8]{0:T(128)S(1)} %fusion.20.table_ref, bf16[2,256,256]{2,1,0:T(8,128)(2,1)S(1)} %get-tuple-element.26.dq_ref, bf16[2,256,256]{2,1,0:T(8,128)(2,1)S(1)} %get-tuple-element.27.dg_ref, f32[2,256,256]{2,1,0:T(8,128)S(1)} %get-tuple-element.28.dk_part, ...), custom_call_target="tpu_custom_call" | custom-call | flops 2147483648 | bytes 8388608 | tf_op jit(solution)/shard_map/pallas_call | solution.py:322
  80.5 4.7 %collective-permute-start.20 = (bf16[4,2,256,512]{3,2,1,0:T(8,128)(2,1)S(1)}, bf16[4,2,256,512]{3,2,1,0:T(8,128)(2,1)S(1)}, u32[]{:S(2)}, u32[]{:S(2)}) collective-permute-start(bf16[4,2,256,512]{3,2,1,0:T(8,128)(2,1)S(1)} %shard_map.107), channel_id=1, source_target_pairs={{0,1},{1,0},{2,3},{3,2},{4,5},{5,4},{6,7},{7,6},{8,9},{9,8},{10,11... | collective-permute-start | bytes 6291464 | tf_op jit(solution)/shard_map/ppermute | solution.py:226
  85.2 3.9 %shard_map.106.refs_0_.refs_2_.refs_4_ = bf16[4,2,256,512]{3,2,1,0:T(8,128)(2,1)S(1)} custom-call(s32[8]{0:T(128)S(1)} %fusion.20.table_ref, bf16[2,256,256]{2,1,0:T(8,128)(2,1)S(1)} %get-tuple-element.26.dq_ref, bf16[2,256,256]{2,1,0:T(8,128)(2,1)S(1)} %get-tuple-element.27.dg_ref, f32[2,256,256]{2,1,0:T(8,128)S(1)} %get-tuple-element.28.dk_part, ...), custom_call_target="tpu_custom_call" | custom-call | flops 2147483648 | bytes 8388608 | tf_op jit(solution)/shard_map/pallas_call | solution.py:322
  89.2 2.8 %collective-permute-start.25 = (bf16[256,512]{1,0:T(8,128)(2,1)S(1)}, bf16[256,512]{1,0:T(8,128)(2,1)S(1)}, u32[]{:S(2)}, u32[]{:S(2)}) collective-permute-start(bf16[256,512]{1,0:T(8,128)(2,1)S(1)} %get-tuple-element.34), channel_id=1, source_target_pairs={{0,6},{1,7},{2,0},{3,1},{4,2},{5,3},{6,4},{7,5},{8,14},{9,15},{10,... | collective-permute-start | bytes 786440 | tf_op jit(solution)/shard_map/ppermute | solution.py:223
  92.2 2.8 %collective-permute-start.21 = (bf16[256,512]{1,0:T(8,128)(2,1)S(1)}, bf16[256,512]{1,0:T(8,128)(2,1)S(1)}, u32[]{:S(2)}, u32[]{:S(2)}) collective-permute-start(bf16[256,512]{1,0:T(8,128)(2,1)S(1)} %get-tuple-element.31), channel_id=1, source_target_pairs={{0,6},{1,7},{2,0},{3,1},{4,2},{5,3},{6,4},{7,5},{8,14},{9,15},{10,... | collective-permute-start | bytes 786440 | tf_op jit(solution)/shard_map/ppermute | solution.py:223
  94.9 2.6 %collective-permute-done.25.refs_2_ = bf16[256,512]{1,0:T(8,128)(2,1)S(1)} collective-permute-done((bf16[256,512]{1,0:T(8,128)(2,1)S(1)}, bf16[256,512]{1,0:T(8,128)(2,1)S(1)}, u32[]{:S(2)}, u32[]{:S(2)}) %collective-permute-start.25) | collective-permute-done | bytes 262176 | tf_op jit(solution)/shard_map/ppermute | solution.py:223
  97.6 3.5 %collective-permute-start.26 = (bf16[256,512]{1,0:T(8,128)(2,1)S(1)}, bf16[256,512]{1,0:T(8,128)(2,1)S(1)}, u32[]{:S(2)}, u32[]{:S(2)}) collective-permute-start(bf16[256,512]{1,0:T(8,128)(2,1)S(1)} %shard_map.111), channel_id=1, source_target_pairs={{0,6},{1,7},{2,0},{3,1},{4,2},{5,3},{6,4},{7,5},{8,14},{9,15},{10,... | collective-permute-start | bytes 786440 | tf_op jit(solution)/shard_map/ppermute | solution.py:223
  101.3 1.8 %collective-permute-done.21.refs_2_ = bf16[256,512]{1,0:T(8,128)(2,1)S(1)} collective-permute-done((bf16[256,512]{1,0:T(8,128)(2,1)S(1)}, bf16[256,512]{1,0:T(8,128)(2,1)S(1)}, u32[]{:S(2)}, u32[]{:S(2)}) %collective-permute-start.21) | collective-permute-done | bytes 262176 | tf_op jit(solution)/shard_map/ppermute | solution.py:223
  103.1 3.1 %collective-permute-done.24.refs_6_ = bf16[256,512]{1,0:T(8,128)(2,1)S(1)} collective-permute-done((bf16[256,512]{1,0:T(8,128)(2,1)S(1)}, bf16[256,512]{1,0:T(8,128)(2,1)S(1)}, u32[]{:S(2)}, u32[]{:S(2)}) %collective-permute-start.24) | collective-permute-done | bytes 262176 | tf_op jit(solution)/shard_map/ppermute | solution.py:223
  106.2 2.5 %collective-permute-done.26.refs_7_ = bf16[256,512]{1,0:T(8,128)(2,1)S(1)} collective-permute-done((bf16[256,512]{1,0:T(8,128)(2,1)S(1)}, bf16[256,512]{1,0:T(8,128)(2,1)S(1)}, u32[]{:S(2)}, u32[]{:S(2)}) %collective-permute-start.26) | collective-permute-done | bytes 262176 | tf_op jit(solution)/shard_map/ppermute | solution.py:223
  108.7 3.1 %collective-permute-done.23.refs_3_ = bf16[256,512]{1,0:T(8,128)(2,1)S(1)} collective-permute-done((bf16[256,512]{1,0:T(8,128)(2,1)S(1)}, bf16[256,512]{1,0:T(8,128)(2,1)S(1)}, u32[]{:S(2)}, u32[]{:S(2)}) %collective-permute-start.23) | collective-permute-done | bytes 262176 | tf_op jit(solution)/shard_map/ppermute | solution.py:223
  111.8 1.0 shard_map.112
  (49 shorter events, 1.5 us)
Async XLA Ops:
  0.0 1.6 %copy-start = (bf16[256,4096]{1,0:T(8,128)(2,1)S(1)}, bf16[256,4096]{1,0:T(8,128)(2,1)}, u32[]{:S(2)}) copy-start(bf16[256,4096]{1,0:T(8,128)(2,1)} %w_ref.5) | copy-start | bytes 6291460
  1.6 4.1 %copy-start.7 = (bf16[2,256,512]{2,1,0:T(8,128)(2,1)S(1)}, bf16[2,256,512]{2,1,0:T(8,128)(2,1)}, u32[]{:S(2)}) copy-start(bf16[2,256,512]{2,1,0:T(8,128)(2,1)} %g_ref.1) | copy-start | bytes 1572868
  2.4 18.0 %collective-permute-start.4 = (bf16[4,256,512]{2,1,0:T(8,128)(2,1)S(1)}, bf16[4,256,512]{2,1,0:T(8,128)(2,1)S(1)}, u32[]{:S(2)}, u32[]{:S(2)}) collective-permute-start(bf16[4,256,512]{2,1,0:T(8,128)(2,1)S(1)} %shard_map.100), channel_id=1, source_target_pairs={{0,1},{1,0},{2,3},{3,2},{4,5},{5,4},{6,7},{7,6},{8,9},{9,8},{10,11... | collective-permute-start | bytes 3145736 | tf_op jit(solution)/shard_map/ppermute | solution.py:226
  5.8 9.1 %collective-permute-start = (bf16[256,512]{1,0:T(8,128)(2,1)S(1)}, bf16[256,512]{1,0:T(8,128)(2,1)S(1)}, u32[]{:S(2)}, u32[]{:S(2)}) collective-permute-start(bf16[256,512]{1,0:T(8,128)(2,1)S(1)} %get-tuple-element.36), channel_id=1, source_target_pairs={{0,2},{1,3},{2,4},{3,5},{4,6},{5,7},{6,0},{7,1},{8,10},{9,11},{10,... | collective-permute-start | bytes 786440 | tf_op jit(solution)/shard_map/ppermute | solution.py:223
  5.9 9.0 %collective-permute-start.3 = (bf16[256,512]{1,0:T(8,128)(2,1)S(1)}, bf16[256,512]{1,0:T(8,128)(2,1)S(1)}, u32[]{:S(2)}, u32[]{:S(2)}) collective-permute-start(bf16[256,512]{1,0:T(8,128)(2,1)S(1)} %get-tuple-element.35), channel_id=1, source_target_pairs={{0,6},{1,7},{2,0},{3,1},{4,2},{5,3},{6,4},{7,5},{8,14},{9,15},{10,... | collective-permute-start | bytes 786440 | tf_op jit(solution)/shard_map/ppermute | solution.py:223
  8.5 11.9 %collective-permute-start.1 = (bf16[256,512]{1,0:T(8,128)(2,1)S(1)}, bf16[256,512]{1,0:T(8,128)(2,1)S(1)}, u32[]{:S(2)}, u32[]{:S(2)}) collective-permute-start(bf16[256,512]{1,0:T(8,128)(2,1)S(1)} %get-tuple-element.35), channel_id=1, source_target_pairs={{0,2},{1,3},{2,4},{3,5},{4,6},{5,7},{6,0},{7,1},{8,10},{9,11},{10,... | collective-permute-start | bytes 786440 | tf_op jit(solution)/shard_map/ppermute | solution.py:223
  8.5 11.9 %collective-permute-start.2 = (bf16[256,512]{1,0:T(8,128)(2,1)S(1)}, bf16[256,512]{1,0:T(8,128)(2,1)S(1)}, u32[]{:S(2)}, u32[]{:S(2)}) collective-permute-start(bf16[256,512]{1,0:T(8,128)(2,1)S(1)} %get-tuple-element.36), channel_id=1, source_target_pairs={{0,6},{1,7},{2,0},{3,1},{4,2},{5,3},{6,4},{7,5},{8,14},{9,15},{10,... | collective-permute-start | bytes 786440 | tf_op jit(solution)/shard_map/ppermute | solution.py:223
  14.8 11.2 %collective-permute-start.5 = (bf16[256,512]{1,0:T(8,128)(2,1)S(1)}, bf16[256,512]{1,0:T(8,128)(2,1)S(1)}, u32[]{:S(2)}, u32[]{:S(2)}) collective-permute-start(bf16[256,512]{1,0:T(8,128)(2,1)S(1)} %collective-permute-done.a0), channel_id=1, source_target_pairs={{0,2},{1,3},{2,4},{3,5},{4,6},{5,7},{6,0},{7,1},{8,10},{9,11},{10,... | collective-permute-start | bytes 786440 | tf_op jit(solution)/shard_map/ppermute | solution.py:223
  14.9 11.2 %collective-permute-start.6 = (bf16[256,512]{1,0:T(8,128)(2,1)S(1)}, bf16[256,512]{1,0:T(8,128)(2,1)S(1)}, u32[]{:S(2)}, u32[]{:S(2)}) collective-permute-start(bf16[256,512]{1,0:T(8,128)(2,1)S(1)} %collective-permute-done.3.b1), channel_id=1, source_target_pairs={{0,6},{1,7},{2,0},{3,1},{4,2},{5,3},{6,4},{7,5},{8,14},{9,15},{10,... | collective-permute-start | bytes 786440 | tf_op jit(solution)/shard_map/ppermute | solution.py:223
  26.1 2.8 %copy-start.5 = (bf16[2,256,256]{2,1,0:T(8,128)(2,1)S(1)}, bf16[2,256,256]{2,1,0:T(8,128)(2,1)}, u32[]{:S(2)}) copy-start(bf16[2,256,256]{2,1,0:T(8,128)(2,1)} %k_ref.7) | copy-start | bytes 786436
  26.1 2.8 %copy-start.6 = (bf16[2,256,256]{2,1,0:T(8,128)(2,1)S(1)}, bf16[2,256,256]{2,1,0:T(8,128)(2,1)}, u32[]{:S(2)}) copy-start(bf16[2,256,256]{2,1,0:T(8,128)(2,1)} %v_ref.7) | copy-start | bytes 786436
  26.1 4.7 %copy-start.8 = (bf16[2,256,256]{2,1,0:T(8,128)(2,1)S(1)}, bf16[2,256,256]{2,1,0:T(8,128)(2,1)}, u32[]{:S(2)}) copy-start(bf16[2,256,256]{2,1,0:T(8,128)(2,1)} %q_ref.3) | copy-start | bytes 786436
  26.1 50.5 %copy-start.4 = (bf16[4096,256]{1,0:T(8,128)(2,1)S(1)}, bf16[4096,256]{1,0:T(8,128)(2,1)}, u32[]{:S(2)}) copy-start(bf16[4096,256]{1,0:T(8,128)(2,1)} %wg.3) | copy-start | bytes 6291460
  27.9 2.8 %collective-permute-start.7 = (f32[2,256,256]{2,1,0:T(8,128)}, f32[2,256,256]{2,1,0:T(8,128)}, u32[]{:S(2)}, u32[]{:S(2)}) collective-permute-start(f32[2,256,256]{2,1,0:T(8,128)} %get-tuple-element.23), channel_id=1, source_target_pairs={{0,1},{1,0},{2,3},{3,2},{4,5},{5,4},{6,7},{7,6},{8,9},{9,8},{10,11... | collective-permute-start | bytes 1572872 | tf_op jit(solution)/shard_map/ppermute | solution.py:226
  29.1 5.3 %collective-permute-start.8 = (bf16[2,2,128,128]{3,2,1,0:T(8,128)(2,1)S(1)}, bf16[2,2,128,128]{3,2,1,0:T(8,128)(2,1)}, u32[]{:S(2)}, u32[]{:S(2)}) collective-permute-start(bf16[2,2,128,128]{3,2,1,0:T(8,128)(2,1)S(1)} %shard_map.104), channel_id=1, source_target_pairs={{0,8},{8,0},{16,24},{24,16},{32,40},{40,32},{48,56},{56,48},{64,72... | collective-permute-start | bytes 393224 | tf_op jit(solution)/shard_map/ppermute | solution.py:141
  30.8 1.0 copy-start.9
  31.7 44.9 %copy-start.3 = (bf16[4096,256]{1,0:T(8,128)(2,1)S(1)}, bf16[4096,256]{1,0:T(8,128)(2,1)}, u32[]{:S(2)}) copy-start(bf16[4096,256]{1,0:T(8,128)(2,1)} %wv.3) | copy-start | bytes 6291460
  33.2 4.8 %collective-permute-start.14 = (bf16[2,2,128,128]{3,2,1,0:T(8,128)(2,1)S(1)}, bf16[2,2,128,128]{3,2,1,0:T(8,128)(2,1)S(1)}, u32[]{:S(2)}, u32[]{:S(2)}) collective-permute-start(bf16[2,2,128,128]{3,2,1,0:T(8,128)(2,1)S(1)} %get-tuple-element.30), channel_id=1, source_target_pairs={{0,8},{8,0},{16,24},{24,16},{32,40},{40,32},{48,56},{56,48},{64,72... | collective-permute-start | bytes 393224 | tf_op jit(solution)/shard_map/ppermute | solution.py:141
  35.4 11.3 %collective-permute-start.9 = (bf16[2,2,128,128]{3,2,1,0:T(8,128)(2,1)S(1)}, bf16[2,2,128,128]{3,2,1,0:T(8,128)(2,1)S(1)}, u32[]{:S(2)}, u32[]{:S(2)}) collective-permute-start(bf16[2,2,128,128]{3,2,1,0:T(8,128)(2,1)S(1)} %fusion.6), channel_id=1, source_target_pairs={{0,16},{8,24},{16,0},{24,8},{32,48},{40,56},{48,32},{56,40},{64,80... | collective-permute-start | bytes 393224 | tf_op jit(solution)/shard_map/ppermute | solution.py:141
  38.1 12.7 %collective-permute-start.15 = (bf16[2,2,128,128]{3,2,1,0:T(8,128)(2,1)S(1)}, bf16[2,2,128,128]{3,2,1,0:T(8,128)(2,1)S(1)}, u32[]{:S(2)}, u32[]{:S(2)}) collective-permute-start(bf16[2,2,128,128]{3,2,1,0:T(8,128)(2,1)S(1)} %fusion.15), channel_id=1, source_target_pairs={{0,16},{8,24},{16,0},{24,8},{32,48},{40,56},{48,32},{56,40},{64,80... | collective-permute-start | bytes 393224 | tf_op jit(solution)/shard_map/ppermute | solution.py:141
  46.7 11.1 %collective-permute-start.10 = (bf16[2,2,128,128]{3,2,1,0:T(8,128)(2,1)S(1)}, bf16[2,2,128,128]{3,2,1,0:T(8,128)(2,1)S(1)}, u32[]{:S(2)}, u32[]{:S(2)}) collective-permute-start(bf16[2,2,128,128]{3,2,1,0:T(8,128)(2,1)S(1)} %fusion.7), channel_id=1, source_target_pairs={{0,56},{8,48},{16,40},{24,32},{32,24},{40,16},{48,8},{56,0},{64,12... | collective-permute-start | bytes 393224 | tf_op jit(solution)/shard_map/ppermute | solution.py:141
  50.9 25.7 %copy-start.1 = (bf16[4096,256]{1,0:T(8,128)(2,1)S(1)}, bf16[4096,256]{1,0:T(8,128)(2,1)}, u32[]{:S(2)}) copy-start(bf16[4096,256]{1,0:T(8,128)(2,1)} %wq.3) | copy-start | bytes 6291460
  50.9 25.7 %copy-start.2 = (bf16[4096,256]{1,0:T(8,128)(2,1)S(1)}, bf16[4096,256]{1,0:T(8,128)(2,1)}, u32[]{:S(2)}) copy-start(bf16[4096,256]{1,0:T(8,128)(2,1)} %wk.3) | copy-start | bytes 6291460
  50.9 11.6 %collective-permute-start.16 = (bf16[2,2,128,128]{3,2,1,0:T(8,128)(2,1)S(1)}, bf16[2,2,128,128]{3,2,1,0:T(8,128)(2,1)S(1)}, u32[]{:S(2)}, u32[]{:S(2)}) collective-permute-start(bf16[2,2,128,128]{3,2,1,0:T(8,128)(2,1)S(1)} %fusion.16), channel_id=1, source_target_pairs={{0,56},{8,48},{16,40},{24,32},{32,24},{40,16},{48,8},{56,0},{64,12... | collective-permute-start | bytes 393224 | tf_op jit(solution)/shard_map/ppermute | solution.py:141
  57.9 8.3 %collective-permute-start.11 = (bf16[2,2,128,128]{3,2,1,0:T(8,128)(2,1)S(1)}, bf16[2,2,128,128]{3,2,1,0:T(8,128)(2,1)S(1)}, u32[]{:S(2)}, u32[]{:S(2)}) collective-permute-start(bf16[2,2,128,128]{3,2,1,0:T(8,128)(2,1)S(1)} %fusion.8), channel_id=1, source_target_pairs={{0,64},{8,72},{16,80},{24,88},{32,96},{40,104},{48,112},{56,120},{... | collective-permute-start | bytes 393224 | tf_op jit(solution)/shard_map/ppermute | solution.py:141
  59.2 7.3 %collective-permute-start.12 = (bf16[2,2,128,128]{3,2,1,0:T(8,128)(2,1)S(1)}, bf16[2,2,128,128]{3,2,1,0:T(8,128)(2,1)S(1)}, u32[]{:S(2)}, u32[]{:S(2)}) collective-permute-start(bf16[2,2,128,128]{3,2,1,0:T(8,128)(2,1)S(1)} %fusion.8), channel_id=1, source_target_pairs={{0,128},{8,136},{16,144},{24,152},{32,160},{40,168},{48,176},{56,1... | collective-permute-start | bytes 393224 | tf_op jit(solution)/shard_map/ppermute | solution.py:141
  61.7 5.2 %collective-permute-start.13 = (bf16[2,2,128,128]{3,2,1,0:T(8,128)(2,1)S(1)}, bf16[2,2,128,128]{3,2,1,0:T(8,128)(2,1)S(1)}, u32[]{:S(2)}, u32[]{:S(2)}) collective-permute-start(bf16[2,2,128,128]{3,2,1,0:T(8,128)(2,1)S(1)} %fusion.8), channel_id=1, source_target_pairs={{0,192},{8,200},{16,208},{24,216},{32,224},{40,232},{48,240},{56,2... | collective-permute-start | bytes 393224 | tf_op jit(solution)/shard_map/ppermute | solution.py:141
  62.5 7.9 %collective-permute-start.17 = (bf16[2,2,128,128]{3,2,1,0:T(8,128)(2,1)S(1)}, bf16[2,2,128,128]{3,2,1,0:T(8,128)(2,1)S(1)}, u32[]{:S(2)}, u32[]{:S(2)}) collective-permute-start(bf16[2,2,128,128]{3,2,1,0:T(8,128)(2,1)S(1)} %fusion.17), channel_id=1, source_target_pairs={{0,64},{8,72},{16,80},{24,88},{32,96},{40,104},{48,112},{56,120},{... | collective-permute-start | bytes 393224 | tf_op jit(solution)/shard_map/ppermute | solution.py:141
  63.8 8.7 %collective-permute-start.18 = (bf16[2,2,128,128]{3,2,1,0:T(8,128)(2,1)S(1)}, bf16[2,2,128,128]{3,2,1,0:T(8,128)(2,1)S(1)}, u32[]{:S(2)}, u32[]{:S(2)}) collective-permute-start(bf16[2,2,128,128]{3,2,1,0:T(8,128)(2,1)S(1)} %fusion.17), channel_id=1, source_target_pairs={{0,128},{8,136},{16,144},{24,152},{32,160},{40,168},{48,176},{56,1... | collective-permute-start | bytes 393224 | tf_op jit(solution)/shard_map/ppermute | solution.py:141
  66.3 10.1 %collective-permute-start.19 = (bf16[2,2,128,128]{3,2,1,0:T(8,128)(2,1)S(1)}, bf16[2,2,128,128]{3,2,1,0:T(8,128)(2,1)S(1)}, u32[]{:S(2)}, u32[]{:S(2)}) collective-permute-start(bf16[2,2,128,128]{3,2,1,0:T(8,128)(2,1)S(1)} %fusion.17), channel_id=1, source_target_pairs={{0,192},{8,200},{16,208},{24,216},{32,224},{40,232},{48,240},{56,2... | collective-permute-start | bytes 393224 | tf_op jit(solution)/shard_map/ppermute | solution.py:141
  80.5 8.6 %collective-permute-start.20 = (bf16[4,2,256,512]{3,2,1,0:T(8,128)(2,1)S(1)}, bf16[4,2,256,512]{3,2,1,0:T(8,128)(2,1)S(1)}, u32[]{:S(2)}, u32[]{:S(2)}) collective-permute-start(bf16[4,2,256,512]{3,2,1,0:T(8,128)(2,1)S(1)} %shard_map.107), channel_id=1, source_target_pairs={{0,1},{1,0},{2,3},{3,2},{4,5},{5,4},{6,7},{7,6},{8,9},{9,8},{10,11... | collective-permute-start | bytes 6291464 | tf_op jit(solution)/shard_map/ppermute | solution.py:226
  89.2 8.3 %collective-permute-start.25 = (bf16[256,512]{1,0:T(8,128)(2,1)S(1)}, bf16[256,512]{1,0:T(8,128)(2,1)S(1)}, u32[]{:S(2)}, u32[]{:S(2)}) collective-permute-start(bf16[256,512]{1,0:T(8,128)(2,1)S(1)} %get-tuple-element.34), channel_id=1, source_target_pairs={{0,6},{1,7},{2,0},{3,1},{4,2},{5,3},{6,4},{7,5},{8,14},{9,15},{10,... | collective-permute-start | bytes 786440 | tf_op jit(solution)/shard_map/ppermute | solution.py:223
  92.0 9.1 %collective-permute-start.22 = (bf16[256,512]{1,0:T(8,128)(2,1)S(1)}, bf16[256,512]{1,0:T(8,128)(2,1)S(1)}, u32[]{:S(2)}, u32[]{:S(2)}) collective-permute-start(bf16[256,512]{1,0:T(8,128)(2,1)S(1)} %get-tuple-element.32), channel_id=1, source_target_pairs={{0,2},{1,3},{2,4},{3,5},{4,6},{5,7},{6,0},{7,1},{8,10},{9,11},{10,... | collective-permute-start | bytes 786440 | tf_op jit(solution)/shard_map/ppermute | solution.py:223
  92.2 11.0 %collective-permute-start.21 = (bf16[256,512]{1,0:T(8,128)(2,1)S(1)}, bf16[256,512]{1,0:T(8,128)(2,1)S(1)}, u32[]{:S(2)}, u32[]{:S(2)}) collective-permute-start(bf16[256,512]{1,0:T(8,128)(2,1)S(1)} %get-tuple-element.31), channel_id=1, source_target_pairs={{0,6},{1,7},{2,0},{3,1},{4,2},{5,3},{6,4},{7,5},{8,14},{9,15},{10,... | collective-permute-start | bytes 786440 | tf_op jit(solution)/shard_map/ppermute | solution.py:223
  94.9 11.3 %collective-permute-start.24 = (bf16[256,512]{1,0:T(8,128)(2,1)S(1)}, bf16[256,512]{1,0:T(8,128)(2,1)S(1)}, u32[]{:S(2)}, u32[]{:S(2)}) collective-permute-start(bf16[256,512]{1,0:T(8,128)(2,1)S(1)} %get-tuple-element.33), channel_id=1, source_target_pairs={{0,2},{1,3},{2,4},{3,5},{4,6},{5,7},{6,0},{7,1},{8,10},{9,11},{10,... | collective-permute-start | bytes 786440 | tf_op jit(solution)/shard_map/ppermute | solution.py:223
  97.6 11.1 %collective-permute-start.26 = (bf16[256,512]{1,0:T(8,128)(2,1)S(1)}, bf16[256,512]{1,0:T(8,128)(2,1)S(1)}, u32[]{:S(2)}, u32[]{:S(2)}) collective-permute-start(bf16[256,512]{1,0:T(8,128)(2,1)S(1)} %shard_map.111), channel_id=1, source_target_pairs={{0,6},{1,7},{2,0},{3,1},{4,2},{5,3},{6,4},{7,5},{8,14},{9,15},{10,... | collective-permute-start | bytes 786440 | tf_op jit(solution)/shard_map/ppermute | solution.py:223
  101.2 10.6 %collective-permute-start.23 = (bf16[256,512]{1,0:T(8,128)(2,1)S(1)}, bf16[256,512]{1,0:T(8,128)(2,1)S(1)}, u32[]{:S(2)}, u32[]{:S(2)}) collective-permute-start(bf16[256,512]{1,0:T(8,128)(2,1)S(1)} %shard_map.110), channel_id=1, source_target_pairs={{0,2},{1,3},{2,4},{3,5},{4,6},{5,7},{6,0},{7,1},{8,10},{9,11},{10,... | collective-permute-start | bytes 786440 | tf_op jit(solution)/shard_map/ppermute | solution.py:223

commit v5 on v4

--- a/solution.py
+++ b/solution.py
@@ -7,7 +7,6 @@
 
 HD = 128
 MIB = 1024 * 1024
-RELATIVE = (0, -1, 1, 2)
 
 
 def params(mib=32):
@@ -145,8 +144,8 @@
         return jnp.where(take, x.astype(jnp.float32), 0.0)
 
     total, entering = state, jnp.zeros(state.shape, jnp.float32)
-    for bit, by in ((1, 1), (2, 2), (4, 7)):
-        theirs = swap(total, by)
+    for bit in (1, 2, 4):
+        theirs = swap(total, bit)
         entering = entering + counted(theirs, bit)
         total = (total.astype(jnp.float32) + theirs.astype(jnp.float32)).astype(jnp.bfloat16)
     swapped = [swap(total, by) for by in (8, 16, 24)]
@@ -205,7 +204,6 @@
     head_count = columns // HD
     features = grad_out.shape[2]
     peers = lax.axis_size("head")
-    ring = peers // 2
     factor = (lax.axis_size("seq") * rows) ** (-0.5)
     bf16, f32 = jnp.bfloat16, jnp.float32
     state_shape = (seq_count, head_count, HD, HD)
@@ -215,23 +213,23 @@
     y, lane = here // 2, here % 2
     places = jnp.arange(8, dtype=jnp.int32)
     offset = places % 4
-    offset = jnp.where(offset == 1, ring - 1, jnp.where(offset == 2, 1, jnp.where(offset == 3, 2, 0)))
-    table = 2 * ((y + offset) % ring) + jnp.where(places < 4, 1 - lane, lane)
+    offset = offset ^ (offset >> 1)
+    table = 2 * (y ^ offset) + jnp.where(places < 4, 1 - lane, lane)
     table = table.astype(jnp.int32)
 
     def along_y(x, by):
-        return lax.ppermute(x, "head", [(i, (i + 2 * by) % peers) for i in range(peers)])
+        return lax.ppermute(x, "head", [(i, i ^ (2 * by)) for i in range(peers)])
 
     def other_core(x):
         return lax.ppermute(x, "head", [(i, i ^ 1) for i in range(peers)])
 
     g0, g1 = grad_out[0], grad_out[1]
     a0 = along_y(g0, 1)
-    b1 = along_y(g1, -1)
+    b1 = along_y(g1, 3)
     a1 = along_y(g1, 1)
-    b0 = along_y(g0, -1)
-    c0 = along_y(a0, 1)
-    c1 = along_y(b1, -1)
+    b0 = along_y(g0, 3)
+    c0 = along_y(a0, 3)
+    c1 = along_y(b1, 1)
 
     w_pick = pl.pallas_call(
         pick_kernel,
@@ -340,16 +338,16 @@
         return [(own, place, s), (theirs, place, s)]
 
     far0, far1 = sums([chip(3, 0), chip(3, 1)], flat)
-    up_far = along_y(far0, 1)
-    down_far = along_y(far1, -1)
-    near1, near0 = sums([chip(2, 1), chip(1, 0)], flat)
-    up_near = along_y(near1, 1)
-    down_near = along_y(near0, -1)
-    (last0,) = sums([chip(2, 0) + [up_far]], flat)
-    (last1,) = sums([chip(1, 1) + [down_far]], flat)
-    up_last = along_y(last0, 1)
-    down_last = along_y(last1, -1)
-    return sums([chip(0, 0) + [down_near, up_last], chip(0, 1) + [up_near, down_last]], flat, stacked=True)
+    through0 = along_y(far0, 1)
+    through1 = along_y(far1, 3)
+    near0, near1 = sums([chip(1, 0), chip(2, 1)], flat)
+    direct0 = along_y(near0, 1)
+    direct1 = along_y(near1, 3)
+    (last0,) = sums([chip(2, 0) + [through0]], flat)
+    (last1,) = sums([chip(1, 1) + [through1]], flat)
+    joined0 = along_y(last0, 3)
+    joined1 = along_y(last1, 1)
+    return sums([chip(0, 0) + [direct0, joined0], chip(0, 1) + [direct1, joined1]], flat, stacked=True)
 
 
 def solution(mesh):

time: 113 us -> 113 us (level)
    ppermute x12, starting transfers between devices: 17.2 us -> 10.9 us  [along_y(): return lax.ppermute(x, 'head', [(i, i ^ 2 * by) for i in range(peers)])]
    ppermute x12, starting transfers between devices: 18.6 us -> 24.6 us  [swap(): return lax.ppermute(x, 'seq', [(i, i ^ by) for i in range(peers)])]
    ppermute x12, waiting for transfers between devices: 23.2 us -> 27.6 us  [along_y(): return lax.ppermute(x, 'head', [(i, i ^ 2 * by) for i in range(peers)])]
    ppermute x12, waiting for transfers between devices: 19.8 us -> 16.8 us  [swap(): return lax.ppermute(x, 'seq', [(i, i ^ by) for i in range(peers)])]
  transfers between devices with their start and end apart: 27 -> 27, of which waited for: 17 -> 14; matrix products, arithmetic and copies ran while one was open for 2% -> 2% of each run, Pallas kernels for 9% -> 10%
where the time goes in v5:
time: 113 us; the launch traced here: 112 us
  waiting for transfers between devices  44.9 us (40%)
  starting transfers between devices  43.9 us (39%)
  Pallas kernels  18.4 us (16%)
  local copies, waits for them, and re-layouts  2.61 us (2%)
  other arithmetic  2.37 us (2%)
    ppermute x12, waiting for transfers between devices, along_y(): return lax.ppermute(x, 'head', [(i, i ^ 2 * by) for i in range(peers)])  27.6 us
    ppermute x12, starting transfers between devices, swap(): return lax.ppermute(x, 'seq', [(i, i ^ by) for i in range(peers)])  24.6 us
    ppermute x12, waiting for transfers between devices, swap(): return lax.ppermute(x, 'seq', [(i, i ^ by) for i in range(peers)])  16.8 us
    ppermute x12, starting transfers between devices, along_y(): return lax.ppermute(x, 'head', [(i, i ^ 2 * by) for i in range(peers)])  10.9 us
    ppermute x3, starting transfers between devices, other_core(): return lax.ppermute(x, 'head', [(i, i ^ 1) for i in range(peers)])  8.48 us
    pallas_call x2, Pallas kernels, project(): pl.pallas_call(make_project_kernel(factor), out_shape=jax.ShapeDtypeStruc...  7.8 us
    unnamed x20, local copies, waits for them, and re-layouts  2.57 us
    pallas_call x1, Pallas kernels, body(): pl.pallas_call(make_inner_kernel(factor), out_shape=[jax.ShapeDtypeStruct...  2.55 us
  transfers between devices with their start and end apart: 27, of which 14 were waited for; matrix products, arithmetic and copies ran while one was open for 2% of the time, Pallas kernels for 10%

profile of v5, /device:TPU:1, one launch (start us, length us, event | category | flops | bytes accessed | tf_op | source)
XLA Modules:
  0.0 112.4 jit_solution(7386924662737174986)
XLA Ops:
  0.0 1.6 %copy-done = bf16[256,4096]{1,0:T(8,128)(2,1)S(1)} copy-done((bf16[256,4096]{1,0:T(8,128)(2,1)S(1)}, bf16[256,4096]{1,0:T(8,128)(2,1)}, u32[]{:S(2)}) %copy-start) | copy-done | bytes 2097176
  1.6 0.8 shard_map.100
  2.4 3.3 %collective-permute-start.4 = (bf16[4,256,512]{2,1,0:T(8,128)(2,1)S(1)}, bf16[4,256,512]{2,1,0:T(8,128)(2,1)S(1)}, u32[]{:S(2)}, u32[]{:S(2)}) collective-permute-start(bf16[4,256,512]{2,1,0:T(8,128)(2,1)S(1)} %shard_map.100), channel_id=1, source_target_pairs={{0,1},{1,0},{2,3},{3,2},{4,5},{5,4},{6,7},{7,6},{8,9},{9,8},{10,11... | collective-permute-start | bytes 3145736 | tf_op jit(solution)/shard_map/ppermute | solution.py:224
  5.9 1.5 %collective-permute-start.3 = (bf16[256,512]{1,0:T(8,128)(2,1)S(1)}, bf16[256,512]{1,0:T(8,128)(2,1)S(1)}, u32[]{:S(2)}, u32[]{:S(2)}) collective-permute-start(bf16[256,512]{1,0:T(8,128)(2,1)S(1)} %get-tuple-element.35), channel_id=1, source_target_pairs={{0,6},{1,7},{2,4},{3,5},{4,2},{5,3},{6,0},{7,1},{8,14},{9,15},{10,... | collective-permute-start | bytes 786440 | tf_op jit(solution)/shard_map/ppermute | solution.py:221
  7.3 0.4 collective-permute-start.1
  7.7 1.7 %collective-permute-start.2 = (bf16[256,512]{1,0:T(8,128)(2,1)S(1)}, bf16[256,512]{1,0:T(8,128)(2,1)S(1)}, u32[]{:S(2)}, u32[]{:S(2)}) collective-permute-start(bf16[256,512]{1,0:T(8,128)(2,1)S(1)} %get-tuple-element.36), channel_id=1, source_target_pairs={{0,6},{1,7},{2,4},{3,5},{4,2},{5,3},{6,0},{7,1},{8,14},{9,15},{10,... | collective-permute-start | bytes 786440 | tf_op jit(solution)/shard_map/ppermute | solution.py:221
  9.4 4.2 %collective-permute-done.a0 = bf16[256,512]{1,0:T(8,128)(2,1)S(1)} collective-permute-done((bf16[256,512]{1,0:T(8,128)(2,1)S(1)}, bf16[256,512]{1,0:T(8,128)(2,1)S(1)}, u32[]{:S(2)}, u32[]{:S(2)}) %collective-permute-start) | collective-permute-done | bytes 262176 | tf_op jit(solution)/shard_map/ppermute | solution.py:221
  13.6 1.0 collective-permute-start.5
  14.6 0.3 collective-permute-done.3.b1
  15.0 4.3 %collective-permute-done.1.a1 = bf16[256,512]{1,0:T(8,128)(2,1)S(1)} collective-permute-done((bf16[256,512]{1,0:T(8,128)(2,1)S(1)}, bf16[256,512]{1,0:T(8,128)(2,1)S(1)}, u32[]{:S(2)}, u32[]{:S(2)}) %collective-permute-start.1) | collective-permute-done | bytes 262176 | tf_op jit(solution)/shard_map/ppermute | solution.py:221
  19.3 1.3 %collective-permute-done.2.b0 = bf16[256,512]{1,0:T(8,128)(2,1)S(1)} collective-permute-done((bf16[256,512]{1,0:T(8,128)(2,1)S(1)}, bf16[256,512]{1,0:T(8,128)(2,1)S(1)}, u32[]{:S(2)}, u32[]{:S(2)}) %collective-permute-start.2) | collective-permute-done | bytes 262176 | tf_op jit(solution)/shard_map/ppermute | solution.py:221
  20.6 2.1 %shard_map.101 = (f32[2,256,256]{2,1,0:T(8,128)S(1)}, f32[2,256,256]{2,1,0:T(8,128)S(1)}) custom-call(s32[8]{0:T(128)S(1)} %fusion.20.table_ref, bf16[2,256,512]{2,1,0:T(8,128)(2,1)S(1)} %copy-done.7, bf16[256,512]{1,0:T(8,128)(2,1)S(1)} %collective-permute-done.a0, bf16[256,512]{1,0:T(8,128)(2,1)S(1)} %collective-permute-done.1.a1, ...), custom_call_target="tpu_custom_call" | custom-call | flops 805306368 | bytes 4194304 | tf_op jit(solution)/shard_map/pallas_call | solution.py:259
  22.7 3.5 %collective-permute-done.5.c0 = bf16[256,512]{1,0:T(8,128)(2,1)S(1)} collective-permute-done((bf16[256,512]{1,0:T(8,128)(2,1)S(1)}, bf16[256,512]{1,0:T(8,128)(2,1)S(1)}, u32[]{:S(2)}, u32[]{:S(2)}) %collective-permute-start.5) | collective-permute-done | bytes 262176 | tf_op jit(solution)/shard_map/ppermute | solution.py:221
  26.2 1.8 %shard_map.102 = (f32[2,256,256]{2,1,0:T(8,128)S(1)}, f32[2,256,256]{2,1,0:T(8,128)}) custom-call(s32[8]{0:T(128)S(1)} %fusion.20.table_ref, f32[2,256,256]{2,1,0:T(8,128)S(1)} %get-tuple-element.20.mine_in, f32[2,256,256]{2,1,0:T(8,128)S(1)} %get-tuple-element.21.other_in, bf16[256,512]{1,0:T(8,128)(2,1)S(1)} %collective-permute-done.5.c0, ...), custom_call_target="tpu_custom_call" | custom-call | flops 268435456 | bytes 3145728 | tf_op jit(solution)/shard_map/pallas_call | solution.py:276
  28.0 1.0 collective-permute-start.7
  29.0 0.3 shard_map.104
  29.3 1.2 %collective-permute-start.8 = (bf16[2,2,128,128]{3,2,1,0:T(8,128)(2,1)S(1)}, bf16[2,2,128,128]{3,2,1,0:T(8,128)(2,1)}, u32[]{:S(2)}, u32[]{:S(2)}) collective-permute-start(bf16[2,2,128,128]{3,2,1,0:T(8,128)(2,1)S(1)} %shard_map.104), channel_id=1, source_target_pairs={{0,8},{8,0},{16,24},{24,16},{32,40},{40,32},{48,56},{56,48},{64,72... | collective-permute-start | bytes 393224 | tf_op jit(solution)/shard_map/ppermute | solution.py:140
  30.4 0.4 collective-permute-done.7.theirs_ref
  30.9 0.9 copy-done.9
  31.8 1.5 %shard_map.103 = (bf16[2,256,256]{2,1,0:T(8,128)(2,1)S(1)}, f32[2,256,256]{2,1,0:T(8,128)S(1)}, bf16[2,2,128,128]{3,2,1,0:T(8,128)(2,1)S(1)}) custom-call(f32[2,256,256]{2,1,0:T(8,128)S(1)} %get-tuple-element.22.mine_ref, f32[2,256,256]{2,1,0:T(8,128)} %collective-permute-done.7.theirs_ref, bf16[2,256,256]{2,1,0:T(8,128)(2,1)S(1)} %copy-done.9, ...), custom_call_target="tpu_custom_call" | custom-call | flops 33554432 | bytes 3145728 | tf_op jit(solution)/shard_map/pallas_call | solution.py:295
  33.3 1.2 %collective-permute-start.14 = (bf16[2,2,128,128]{3,2,1,0:T(8,128)(2,1)S(1)}, bf16[2,2,128,128]{3,2,1,0:T(8,128)(2,1)S(1)}, u32[]{:S(2)}, u32[]{:S(2)}) collective-permute-start(bf16[2,2,128,128]{3,2,1,0:T(8,128)(2,1)S(1)} %get-tuple-element.30), channel_id=1, source_target_pairs={{0,8},{8,0},{16,24},{24,16},{32,40},{40,32},{48,56},{56,48},{64,72... | collective-permute-start | bytes 393224 | tf_op jit(solution)/shard_map/ppermute | solution.py:140
  34.6 0.9 fusion.6
  35.5 3.0 %collective-permute-start.9 = (bf16[2,2,128,128]{3,2,1,0:T(8,128)(2,1)S(1)}, bf16[2,2,128,128]{3,2,1,0:T(8,128)(2,1)S(1)}, u32[]{:S(2)}, u32[]{:S(2)}) collective-permute-start(bf16[2,2,128,128]{3,2,1,0:T(8,128)(2,1)S(1)} %fusion.6), channel_id=1, source_target_pairs={{0,16},{8,24},{16,0},{24,8},{32,48},{40,56},{48,32},{56,40},{64,80... | collective-permute-start | bytes 393224 | tf_op jit(solution)/shard_map/ppermute | solution.py:140
  38.6 2.4 %collective-permute-start.15 = (bf16[2,2,128,128]{3,2,1,0:T(8,128)(2,1)S(1)}, bf16[2,2,128,128]{3,2,1,0:T(8,128)(2,1)S(1)}, u32[]{:S(2)}, u32[]{:S(2)}) collective-permute-start(bf16[2,2,128,128]{3,2,1,0:T(8,128)(2,1)S(1)} %fusion.15), channel_id=1, source_target_pairs={{0,16},{8,24},{16,0},{24,8},{32,48},{40,56},{48,32},{56,40},{64,80... | collective-permute-start | bytes 393224 | tf_op jit(solution)/shard_map/ppermute | solution.py:140
  41.0 6.4 %collective-permute-done.9 = bf16[2,2,128,128]{3,2,1,0:T(8,128)(2,1)S(1)} collective-permute-done((bf16[2,2,128,128]{3,2,1,0:T(8,128)(2,1)S(1)}, bf16[2,2,128,128]{3,2,1,0:T(8,128)(2,1)S(1)}, u32[]{:S(2)}, u32[]{:S(2)}) %collective-permute-start.9) | collective-permute-done | bytes 131104 | tf_op jit(solution)/shard_map/ppermute | solution.py:140
  47.5 5.9 %collective-permute-start.10 = (bf16[2,2,128,128]{3,2,1,0:T(8,128)(2,1)S(1)}, bf16[2,2,128,128]{3,2,1,0:T(8,128)(2,1)S(1)}, u32[]{:S(2)}, u32[]{:S(2)}) collective-permute-start(bf16[2,2,128,128]{3,2,1,0:T(8,128)(2,1)S(1)} %fusion.7), channel_id=1, source_target_pairs={{0,32},{8,40},{16,48},{24,56},{32,0},{40,8},{48,16},{56,24},{64,96... | collective-permute-start | bytes 393224 | tf_op jit(solution)/shard_map/ppermute | solution.py:140
  53.4 2.8 %collective-permute-start.16 = (bf16[2,2,128,128]{3,2,1,0:T(8,128)(2,1)S(1)}, bf16[2,2,128,128]{3,2,1,0:T(8,128)(2,1)S(1)}, u32[]{:S(2)}, u32[]{:S(2)}) collective-permute-start(bf16[2,2,128,128]{3,2,1,0:T(8,128)(2,1)S(1)} %fusion.16), channel_id=1, source_target_pairs={{0,32},{8,40},{16,48},{24,56},{32,0},{40,8},{48,16},{56,24},{64,96... | collective-permute-start | bytes 393224 | tf_op jit(solution)/shard_map/ppermute | solution.py:140
  56.2 1.3 %collective-permute-start.11 = (bf16[2,2,128,128]{3,2,1,0:T(8,128)(2,1)S(1)}, bf16[2,2,128,128]{3,2,1,0:T(8,128)(2,1)S(1)}, u32[]{:S(2)}, u32[]{:S(2)}) collective-permute-start(bf16[2,2,128,128]{3,2,1,0:T(8,128)(2,1)S(1)} %fusion.8), channel_id=1, source_target_pairs={{0,64},{8,72},{16,80},{24,88},{32,96},{40,104},{48,112},{56,120},{... | collective-permute-start | bytes 393224 | tf_op jit(solution)/shard_map/ppermute | solution.py:140
  57.5 2.5 %collective-permute-start.12 = (bf16[2,2,128,128]{3,2,1,0:T(8,128)(2,1)S(1)}, bf16[2,2,128,128]{3,2,1,0:T(8,128)(2,1)S(1)}, u32[]{:S(2)}, u32[]{:S(2)}) collective-permute-start(bf16[2,2,128,128]{3,2,1,0:T(8,128)(2,1)S(1)} %fusion.8), channel_id=1, source_target_pairs={{0,128},{8,136},{16,144},{24,152},{32,160},{40,168},{48,176},{56,1... | collective-permute-start | bytes 393224 | tf_op jit(solution)/shard_map/ppermute | solution.py:140
  60.2 3.7 %collective-permute-done.16 = bf16[2,2,128,128]{3,2,1,0:T(8,128)(2,1)S(1)} collective-permute-done((bf16[2,2,128,128]{3,2,1,0:T(8,128)(2,1)S(1)}, bf16[2,2,128,128]{3,2,1,0:T(8,128)(2,1)S(1)}, u32[]{:S(2)}, u32[]{:S(2)}) %collective-permute-start.16) | collective-permute-done | bytes 131104 | tf_op jit(solution)/shard_map/ppermute | solution.py:140
  63.9 1.5 %collective-permute-start.17 = (bf16[2,2,128,128]{3,2,1,0:T(8,128)(2,1)S(1)}, bf16[2,2,128,128]{3,2,1,0:T(8,128)(2,1)S(1)}, u32[]{:S(2)}, u32[]{:S(2)}) collective-permute-start(bf16[2,2,128,128]{3,2,1,0:T(8,128)(2,1)S(1)} %fusion.17), channel_id=1, source_target_pairs={{0,64},{8,72},{16,80},{24,88},{32,96},{40,104},{48,112},{56,120},{... | collective-permute-start | bytes 393224 | tf_op jit(solution)/shard_map/ppermute | solution.py:140
  65.4 2.5 %collective-permute-start.18 = (bf16[2,2,128,128]{3,2,1,0:T(8,128)(2,1)S(1)}, bf16[2,2,128,128]{3,2,1,0:T(8,128)(2,1)S(1)}, u32[]{:S(2)}, u32[]{:S(2)}) collective-permute-start(bf16[2,2,128,128]{3,2,1,0:T(8,128)(2,1)S(1)} %fusion.17), channel_id=1, source_target_pairs={{0,128},{8,136},{16,144},{24,152},{32,160},{40,168},{48,176},{56,1... | collective-permute-start | bytes 393224 | tf_op jit(solution)/shard_map/ppermute | solution.py:140
  67.9 0.2 collective-permute-start.19
  68.1 1.1 fusion.5.prefix_ref
  69.2 2.5 %shard_map.105 = (bf16[2,256,256]{2,1,0:T(8,128)(2,1)S(1)}, bf16[2,256,256]{2,1,0:T(8,128)(2,1)S(1)}, f32[2,256,256]{2,1,0:T(8,128)S(1)}, f32[2,256,256]{2,1,0:T(8,128)S(1)}) custom-call(bf16[2,256,256]{2,1,0:T(8,128)(2,1)S(1)} %copy-done.8, bf16[2,256,256]{2,1,0:T(8,128)(2,1)S(1)} %copy-done.5, bf16[2,256,256]{2,1,0:T(8,128)(2,1)S(1)} %copy-done.6, ...), custom_call_target="tpu_custom_call" | custom-call | flops 402653184 | bytes 3145728 | tf_op jit(solution)/shard_map/pallas_call | solution.py:308
  71.7 2.7 %collective-permute-done.18 = bf16[2,2,128,128]{3,2,1,0:T(8,128)(2,1)S(1)} collective-permute-done((bf16[2,2,128,128]{3,2,1,0:T(8,128)(2,1)S(1)}, bf16[2,2,128,128]{3,2,1,0:T(8,128)(2,1)S(1)}, u32[]{:S(2)}, u32[]{:S(2)}) %collective-permute-start.18) | collective-permute-done | bytes 131104 | tf_op jit(solution)/shard_map/ppermute | solution.py:140
  74.4 4.0 %collective-permute-done.19 = bf16[2,2,128,128]{3,2,1,0:T(8,128)(2,1)S(1)} collective-permute-done((bf16[2,2,128,128]{3,2,1,0:T(8,128)(2,1)S(1)}, bf16[2,2,128,128]{3,2,1,0:T(8,128)(2,1)S(1)}, u32[]{:S(2)}, u32[]{:S(2)}) %collective-permute-start.19) | collective-permute-done | bytes 131104 | tf_op jit(solution)/shard_map/ppermute | solution.py:140
  78.6 3.9 %shard_map.107 = bf16[4,2,256,512]{3,2,1,0:T(8,128)(2,1)S(1)} custom-call(s32[8]{0:T(128)S(1)} %fusion.20.table_ref, bf16[2,256,256]{2,1,0:T(8,128)(2,1)S(1)} %get-tuple-element.26.dq_ref, bf16[2,256,256]{2,1,0:T(8,128)(2,1)S(1)} %get-tuple-element.27.dg_ref, f32[2,256,256]{2,1,0:T(8,128)S(1)} %get-tuple-element.28.dk_part, ...), custom_call_target="tpu_custom_call" | custom-call | flops 2147483648 | bytes 8388608 | tf_op jit(solution)/shard_map/pallas_call | solution.py:320
  82.5 4.2 %collective-permute-start.20 = (bf16[4,2,256,512]{3,2,1,0:T(8,128)(2,1)S(1)}, bf16[4,2,256,512]{3,2,1,0:T(8,128)(2,1)S(1)}, u32[]{:S(2)}, u32[]{:S(2)}) collective-permute-start(bf16[4,2,256,512]{3,2,1,0:T(8,128)(2,1)S(1)} %shard_map.107), channel_id=1, source_target_pairs={{0,1},{1,0},{2,3},{3,2},{4,5},{5,4},{6,7},{7,6},{8,9},{9,8},{10,11... | collective-permute-start | bytes 6291464 | tf_op jit(solution)/shard_map/ppermute | solution.py:224
  86.7 3.9 %shard_map.106.refs_0_.refs_2_.refs_4_ = bf16[4,2,256,512]{3,2,1,0:T(8,128)(2,1)S(1)} custom-call(s32[8]{0:T(128)S(1)} %fusion.20.table_ref, bf16[2,256,256]{2,1,0:T(8,128)(2,1)S(1)} %get-tuple-element.26.dq_ref, bf16[2,256,256]{2,1,0:T(8,128)(2,1)S(1)} %get-tuple-element.27.dg_ref, f32[2,256,256]{2,1,0:T(8,128)S(1)} %get-tuple-element.28.dk_part, ...), custom_call_target="tpu_custom_call" | custom-call | flops 2147483648 | bytes 8388608 | tf_op jit(solution)/shard_map/pallas_call | solution.py:320
  90.7 2.0 %collective-permute-start.25 = (bf16[256,512]{1,0:T(8,128)(2,1)S(1)}, bf16[256,512]{1,0:T(8,128)(2,1)S(1)}, u32[]{:S(2)}, u32[]{:S(2)}) collective-permute-start(bf16[256,512]{1,0:T(8,128)(2,1)S(1)} %get-tuple-element.34), channel_id=1, source_target_pairs={{0,6},{1,7},{2,4},{3,5},{4,2},{5,3},{6,0},{7,1},{8,14},{9,15},{10,... | collective-permute-start | bytes 786440 | tf_op jit(solution)/shard_map/ppermute | solution.py:221
  92.9 1.5 %collective-permute-start.21 = (bf16[256,512]{1,0:T(8,128)(2,1)S(1)}, bf16[256,512]{1,0:T(8,128)(2,1)S(1)}, u32[]{:S(2)}, u32[]{:S(2)}) collective-permute-start(bf16[256,512]{1,0:T(8,128)(2,1)S(1)} %get-tuple-element.31), channel_id=1, source_target_pairs={{0,2},{1,3},{2,0},{3,1},{4,6},{5,7},{6,4},{7,5},{8,10},{9,11},{10,... | collective-permute-start | bytes 786440 | tf_op jit(solution)/shard_map/ppermute | solution.py:221
  94.4 0.8 collective-permute-start.24
  95.2 4.5 %collective-permute-done.25.refs_2_ = bf16[256,512]{1,0:T(8,128)(2,1)S(1)} collective-permute-done((bf16[256,512]{1,0:T(8,128)(2,1)S(1)}, bf16[256,512]{1,0:T(8,128)(2,1)S(1)}, u32[]{:S(2)}, u32[]{:S(2)}) %collective-permute-start.25) | collective-permute-done | bytes 262176 | tf_op jit(solution)/shard_map/ppermute | solution.py:221
  100.2 1.8 %collective-permute-start.23 = (bf16[256,512]{1,0:T(8,128)(2,1)S(1)}, bf16[256,512]{1,0:T(8,128)(2,1)S(1)}, u32[]{:S(2)}, u32[]{:S(2)}) collective-permute-start(bf16[256,512]{1,0:T(8,128)(2,1)S(1)} %shard_map.110), channel_id=1, source_target_pairs={{0,6},{1,7},{2,4},{3,5},{4,2},{5,3},{6,0},{7,1},{8,14},{9,15},{10,... | collective-permute-start | bytes 786440 | tf_op jit(solution)/shard_map/ppermute | solution.py:221
  102.0 3.7 %collective-permute-done.21.refs_2_ = bf16[256,512]{1,0:T(8,128)(2,1)S(1)} collective-permute-done((bf16[256,512]{1,0:T(8,128)(2,1)S(1)}, bf16[256,512]{1,0:T(8,128)(2,1)S(1)}, u32[]{:S(2)}, u32[]{:S(2)}) %collective-permute-start.21) | collective-permute-done | bytes 262176 | tf_op jit(solution)/shard_map/ppermute | solution.py:221
  105.7 5.6 %collective-permute-done.26.refs_7_ = bf16[256,512]{1,0:T(8,128)(2,1)S(1)} collective-permute-done((bf16[256,512]{1,0:T(8,128)(2,1)S(1)}, bf16[256,512]{1,0:T(8,128)(2,1)S(1)}, u32[]{:S(2)}, u32[]{:S(2)}) %collective-permute-start.26) | collective-permute-done | bytes 262176 | tf_op jit(solution)/shard_map/ppermute | solution.py:221
  111.3 1.1 shard_map.112
  (49 shorter events, 1.5 us)
Async XLA Ops:
  0.0 1.6 %copy-start = (bf16[256,4096]{1,0:T(8,128)(2,1)S(1)}, bf16[256,4096]{1,0:T(8,128)(2,1)}, u32[]{:S(2)}) copy-start(bf16[256,4096]{1,0:T(8,128)(2,1)} %w_ref.5) | copy-start | bytes 6291460
  1.6 4.1 %copy-start.7 = (bf16[2,256,512]{2,1,0:T(8,128)(2,1)S(1)}, bf16[2,256,512]{2,1,0:T(8,128)(2,1)}, u32[]{:S(2)}) copy-start(bf16[2,256,512]{2,1,0:T(8,128)(2,1)} %g_ref.1) | copy-start | bytes 1572868
  2.4 18.2 %collective-permute-start.4 = (bf16[4,256,512]{2,1,0:T(8,128)(2,1)S(1)}, bf16[4,256,512]{2,1,0:T(8,128)(2,1)S(1)}, u32[]{:S(2)}, u32[]{:S(2)}) collective-permute-start(bf16[4,256,512]{2,1,0:T(8,128)(2,1)S(1)} %shard_map.100), channel_id=1, source_target_pairs={{0,1},{1,0},{2,3},{3,2},{4,5},{5,4},{6,7},{7,6},{8,9},{9,8},{10,11... | collective-permute-start | bytes 3145736 | tf_op jit(solution)/shard_map/ppermute | solution.py:224
  5.8 7.9 %collective-permute-start = (bf16[256,512]{1,0:T(8,128)(2,1)S(1)}, bf16[256,512]{1,0:T(8,128)(2,1)S(1)}, u32[]{:S(2)}, u32[]{:S(2)}) collective-permute-start(bf16[256,512]{1,0:T(8,128)(2,1)S(1)} %get-tuple-element.36), channel_id=1, source_target_pairs={{0,2},{1,3},{2,0},{3,1},{4,6},{5,7},{6,4},{7,5},{8,10},{9,11},{10,... | collective-permute-start | bytes 786440 | tf_op jit(solution)/shard_map/ppermute | solution.py:221
  5.9 9.1 %collective-permute-start.3 = (bf16[256,512]{1,0:T(8,128)(2,1)S(1)}, bf16[256,512]{1,0:T(8,128)(2,1)S(1)}, u32[]{:S(2)}, u32[]{:S(2)}) collective-permute-start(bf16[256,512]{1,0:T(8,128)(2,1)S(1)} %get-tuple-element.35), channel_id=1, source_target_pairs={{0,6},{1,7},{2,4},{3,5},{4,2},{5,3},{6,0},{7,1},{8,14},{9,15},{10,... | collective-permute-start | bytes 786440 | tf_op jit(solution)/shard_map/ppermute | solution.py:221
  7.3 11.9 %collective-permute-start.1 = (bf16[256,512]{1,0:T(8,128)(2,1)S(1)}, bf16[256,512]{1,0:T(8,128)(2,1)S(1)}, u32[]{:S(2)}, u32[]{:S(2)}) collective-permute-start(bf16[256,512]{1,0:T(8,128)(2,1)S(1)} %get-tuple-element.35), channel_id=1, source_target_pairs={{0,2},{1,3},{2,0},{3,1},{4,6},{5,7},{6,4},{7,5},{8,10},{9,11},{10,... | collective-permute-start | bytes 786440 | tf_op jit(solution)/shard_map/ppermute | solution.py:221
  7.7 12.8 %collective-permute-start.2 = (bf16[256,512]{1,0:T(8,128)(2,1)S(1)}, bf16[256,512]{1,0:T(8,128)(2,1)S(1)}, u32[]{:S(2)}, u32[]{:S(2)}) collective-permute-start(bf16[256,512]{1,0:T(8,128)(2,1)S(1)} %get-tuple-element.36), channel_id=1, source_target_pairs={{0,6},{1,7},{2,4},{3,5},{4,2},{5,3},{6,0},{7,1},{8,14},{9,15},{10,... | collective-permute-start | bytes 786440 | tf_op jit(solution)/shard_map/ppermute | solution.py:221
  13.6 12.5 %collective-permute-start.5 = (bf16[256,512]{1,0:T(8,128)(2,1)S(1)}, bf16[256,512]{1,0:T(8,128)(2,1)S(1)}, u32[]{:S(2)}, u32[]{:S(2)}) collective-permute-start(bf16[256,512]{1,0:T(8,128)(2,1)S(1)} %collective-permute-done.a0), channel_id=1, source_target_pairs={{0,6},{1,7},{2,4},{3,5},{4,2},{5,3},{6,0},{7,1},{8,14},{9,15},{10,... | collective-permute-start | bytes 786440 | tf_op jit(solution)/shard_map/ppermute | solution.py:221
  14.9 11.2 %collective-permute-start.6 = (bf16[256,512]{1,0:T(8,128)(2,1)S(1)}, bf16[256,512]{1,0:T(8,128)(2,1)S(1)}, u32[]{:S(2)}, u32[]{:S(2)}) collective-permute-start(bf16[256,512]{1,0:T(8,128)(2,1)S(1)} %collective-permute-done.3.b1), channel_id=1, source_target_pairs={{0,2},{1,3},{2,0},{3,1},{4,6},{5,7},{6,4},{7,5},{8,10},{9,11},{10,... | collective-permute-start | bytes 786440 | tf_op jit(solution)/shard_map/ppermute | solution.py:221
  26.2 2.8 %copy-start.5 = (bf16[2,256,256]{2,1,0:T(8,128)(2,1)S(1)}, bf16[2,256,256]{2,1,0:T(8,128)(2,1)}, u32[]{:S(2)}) copy-start(bf16[2,256,256]{2,1,0:T(8,128)(2,1)} %k_ref.7) | copy-start | bytes 786436
  26.2 2.8 %copy-start.6 = (bf16[2,256,256]{2,1,0:T(8,128)(2,1)S(1)}, bf16[2,256,256]{2,1,0:T(8,128)(2,1)}, u32[]{:S(2)}) copy-start(bf16[2,256,256]{2,1,0:T(8,128)(2,1)} %v_ref.7) | copy-start | bytes 786436
  26.2 4.7 %copy-start.8 = (bf16[2,256,256]{2,1,0:T(8,128)(2,1)S(1)}, bf16[2,256,256]{2,1,0:T(8,128)(2,1)}, u32[]{:S(2)}) copy-start(bf16[2,256,256]{2,1,0:T(8,128)(2,1)} %q_ref.3) | copy-start | bytes 786436
  26.2 52.4 %copy-start.4 = (bf16[4096,256]{1,0:T(8,128)(2,1)S(1)}, bf16[4096,256]{1,0:T(8,128)(2,1)}, u32[]{:S(2)}) copy-start(bf16[4096,256]{1,0:T(8,128)(2,1)} %wg.3) | copy-start | bytes 6291460
  28.0 2.8 %collective-permute-start.7 = (f32[2,256,256]{2,1,0:T(8,128)}, f32[2,256,256]{2,1,0:T(8,128)}, u32[]{:S(2)}, u32[]{:S(2)}) collective-permute-start(f32[2,256,256]{2,1,0:T(8,128)} %get-tuple-element.23), channel_id=1, source_target_pairs={{0,1},{1,0},{2,3},{3,2},{4,5},{5,4},{6,7},{7,6},{8,9},{9,8},{10,11... | collective-permute-start | bytes 1572872 | tf_op jit(solution)/shard_map/ppermute | solution.py:224
  29.3 5.3 %collective-permute-start.8 = (bf16[2,2,128,128]{3,2,1,0:T(8,128)(2,1)S(1)}, bf16[2,2,128,128]{3,2,1,0:T(8,128)(2,1)}, u32[]{:S(2)}, u32[]{:S(2)}) collective-permute-start(bf16[2,2,128,128]{3,2,1,0:T(8,128)(2,1)S(1)} %shard_map.104), channel_id=1, source_target_pairs={{0,8},{8,0},{16,24},{24,16},{32,40},{40,32},{48,56},{56,48},{64,72... | collective-permute-start | bytes 393224 | tf_op jit(solution)/shard_map/ppermute | solution.py:140
  30.9 1.0 copy-start.9
  31.8 46.8 %copy-start.3 = (bf16[4096,256]{1,0:T(8,128)(2,1)S(1)}, bf16[4096,256]{1,0:T(8,128)(2,1)}, u32[]{:S(2)}) copy-start(bf16[4096,256]{1,0:T(8,128)(2,1)} %wv.3) | copy-start | bytes 6291460
  33.3 5.2 %collective-permute-start.14 = (bf16[2,2,128,128]{3,2,1,0:T(8,128)(2,1)S(1)}, bf16[2,2,128,128]{3,2,1,0:T(8,128)(2,1)S(1)}, u32[]{:S(2)}, u32[]{:S(2)}) collective-permute-start(bf16[2,2,128,128]{3,2,1,0:T(8,128)(2,1)S(1)} %get-tuple-element.30), channel_id=1, source_target_pairs={{0,8},{8,0},{16,24},{24,16},{32,40},{40,32},{48,56},{56,48},{64,72... | collective-permute-start | bytes 393224 | tf_op jit(solution)/shard_map/ppermute | solution.py:140
  35.5 11.9 %collective-permute-start.9 = (bf16[2,2,128,128]{3,2,1,0:T(8,128)(2,1)S(1)}, bf16[2,2,128,128]{3,2,1,0:T(8,128)(2,1)S(1)}, u32[]{:S(2)}, u32[]{:S(2)}) collective-permute-start(bf16[2,2,128,128]{3,2,1,0:T(8,128)(2,1)S(1)} %fusion.6), channel_id=1, source_target_pairs={{0,16},{8,24},{16,0},{24,8},{32,48},{40,56},{48,32},{56,40},{64,80... | collective-permute-start | bytes 393224 | tf_op jit(solution)/shard_map/ppermute | solution.py:140
  38.6 14.8 %collective-permute-start.15 = (bf16[2,2,128,128]{3,2,1,0:T(8,128)(2,1)S(1)}, bf16[2,2,128,128]{3,2,1,0:T(8,128)(2,1)S(1)}, u32[]{:S(2)}, u32[]{:S(2)}) collective-permute-start(bf16[2,2,128,128]{3,2,1,0:T(8,128)(2,1)S(1)} %fusion.15), channel_id=1, source_target_pairs={{0,16},{8,24},{16,0},{24,8},{32,48},{40,56},{48,32},{56,40},{64,80... | collective-permute-start | bytes 393224 | tf_op jit(solution)/shard_map/ppermute | solution.py:140
  47.5 8.7 %collective-permute-start.10 = (bf16[2,2,128,128]{3,2,1,0:T(8,128)(2,1)S(1)}, bf16[2,2,128,128]{3,2,1,0:T(8,128)(2,1)S(1)}, u32[]{:S(2)}, u32[]{:S(2)}) collective-permute-start(bf16[2,2,128,128]{3,2,1,0:T(8,128)(2,1)S(1)} %fusion.7), channel_id=1, source_target_pairs={{0,32},{8,40},{16,48},{24,56},{32,0},{40,8},{48,16},{56,24},{64,96... | collective-permute-start | bytes 393224 | tf_op jit(solution)/shard_map/ppermute | solution.py:140
  53.4 25.2 %copy-start.1 = (bf16[4096,256]{1,0:T(8,128)(2,1)S(1)}, bf16[4096,256]{1,0:T(8,128)(2,1)}, u32[]{:S(2)}) copy-start(bf16[4096,256]{1,0:T(8,128)(2,1)} %wq.3) | copy-start | bytes 6291460
  53.4 25.2 %copy-start.2 = (bf16[4096,256]{1,0:T(8,128)(2,1)S(1)}, bf16[4096,256]{1,0:T(8,128)(2,1)}, u32[]{:S(2)}) copy-start(bf16[4096,256]{1,0:T(8,128)(2,1)} %wk.3) | copy-start | bytes 6291460
  53.4 10.5 %collective-permute-start.16 = (bf16[2,2,128,128]{3,2,1,0:T(8,128)(2,1)S(1)}, bf16[2,2,128,128]{3,2,1,0:T(8,128)(2,1)S(1)}, u32[]{:S(2)}, u32[]{:S(2)}) collective-permute-start(bf16[2,2,128,128]{3,2,1,0:T(8,128)(2,1)S(1)} %fusion.16), channel_id=1, source_target_pairs={{0,32},{8,40},{16,48},{24,56},{32,0},{40,8},{48,16},{56,24},{64,96... | collective-permute-start | bytes 393224 | tf_op jit(solution)/shard_map/ppermute | solution.py:140
  56.2 11.6 %collective-permute-start.11 = (bf16[2,2,128,128]{3,2,1,0:T(8,128)(2,1)S(1)}, bf16[2,2,128,128]{3,2,1,0:T(8,128)(2,1)S(1)}, u32[]{:S(2)}, u32[]{:S(2)}) collective-permute-start(bf16[2,2,128,128]{3,2,1,0:T(8,128)(2,1)S(1)} %fusion.8), channel_id=1, source_target_pairs={{0,64},{8,72},{16,80},{24,88},{32,96},{40,104},{48,112},{56,120},{... | collective-permute-start | bytes 393224 | tf_op jit(solution)/shard_map/ppermute | solution.py:140
  57.5 10.6 %collective-permute-start.12 = (bf16[2,2,128,128]{3,2,1,0:T(8,128)(2,1)S(1)}, bf16[2,2,128,128]{3,2,1,0:T(8,128)(2,1)S(1)}, u32[]{:S(2)}, u32[]{:S(2)}) collective-permute-start(bf16[2,2,128,128]{3,2,1,0:T(8,128)(2,1)S(1)} %fusion.8), channel_id=1, source_target_pairs={{0,128},{8,136},{16,144},{24,152},{32,160},{40,168},{48,176},{56,1... | collective-permute-start | bytes 393224 | tf_op jit(solution)/shard_map/ppermute | solution.py:140
  60.0 8.1 %collective-permute-start.13 = (bf16[2,2,128,128]{3,2,1,0:T(8,128)(2,1)S(1)}, bf16[2,2,128,128]{3,2,1,0:T(8,128)(2,1)S(1)}, u32[]{:S(2)}, u32[]{:S(2)}) collective-permute-start(bf16[2,2,128,128]{3,2,1,0:T(8,128)(2,1)S(1)} %fusion.8), channel_id=1, source_target_pairs={{0,192},{8,200},{16,208},{24,216},{32,224},{40,232},{48,240},{56,2... | collective-permute-start | bytes 393224 | tf_op jit(solution)/shard_map/ppermute | solution.py:140
  63.9 7.8 %collective-permute-start.17 = (bf16[2,2,128,128]{3,2,1,0:T(8,128)(2,1)S(1)}, bf16[2,2,128,128]{3,2,1,0:T(8,128)(2,1)S(1)}, u32[]{:S(2)}, u32[]{:S(2)}) collective-permute-start(bf16[2,2,128,128]{3,2,1,0:T(8,128)(2,1)S(1)} %fusion.17), channel_id=1, source_target_pairs={{0,64},{8,72},{16,80},{24,88},{32,96},{40,104},{48,112},{56,120},{... | collective-permute-start | bytes 393224 | tf_op jit(solution)/shard_map/ppermute | solution.py:140
  65.4 9.0 %collective-permute-start.18 = (bf16[2,2,128,128]{3,2,1,0:T(8,128)(2,1)S(1)}, bf16[2,2,128,128]{3,2,1,0:T(8,128)(2,1)S(1)}, u32[]{:S(2)}, u32[]{:S(2)}) collective-permute-start(bf16[2,2,128,128]{3,2,1,0:T(8,128)(2,1)S(1)} %fusion.17), channel_id=1, source_target_pairs={{0,128},{8,136},{16,144},{24,152},{32,160},{40,168},{48,176},{56,1... | collective-permute-start | bytes 393224 | tf_op jit(solution)/shard_map/ppermute | solution.py:140
  67.9 10.5 %collective-permute-start.19 = (bf16[2,2,128,128]{3,2,1,0:T(8,128)(2,1)S(1)}, bf16[2,2,128,128]{3,2,1,0:T(8,128)(2,1)S(1)}, u32[]{:S(2)}, u32[]{:S(2)}) collective-permute-start(bf16[2,2,128,128]{3,2,1,0:T(8,128)(2,1)S(1)} %fusion.17), channel_id=1, source_target_pairs={{0,192},{8,200},{16,208},{24,216},{32,224},{40,232},{48,240},{56,2... | collective-permute-start | bytes 393224 | tf_op jit(solution)/shard_map/ppermute | solution.py:140
  82.5 8.1 %collective-permute-start.20 = (bf16[4,2,256,512]{3,2,1,0:T(8,128)(2,1)S(1)}, bf16[4,2,256,512]{3,2,1,0:T(8,128)(2,1)S(1)}, u32[]{:S(2)}, u32[]{:S(2)}) collective-permute-start(bf16[4,2,256,512]{3,2,1,0:T(8,128)(2,1)S(1)} %shard_map.107), channel_id=1, source_target_pairs={{0,1},{1,0},{2,3},{3,2},{4,5},{5,4},{6,7},{7,6},{8,9},{9,8},{10,11... | collective-permute-start | bytes 6291464 | tf_op jit(solution)/shard_map/ppermute | solution.py:224
  90.7 9.0 %collective-permute-start.25 = (bf16[256,512]{1,0:T(8,128)(2,1)S(1)}, bf16[256,512]{1,0:T(8,128)(2,1)S(1)}, u32[]{:S(2)}, u32[]{:S(2)}) collective-permute-start(bf16[256,512]{1,0:T(8,128)(2,1)S(1)} %get-tuple-element.34), channel_id=1, source_target_pairs={{0,6},{1,7},{2,4},{3,5},{4,2},{5,3},{6,0},{7,1},{8,14},{9,15},{10,... | collective-permute-start | bytes 786440 | tf_op jit(solution)/shard_map/ppermute | solution.py:221
  92.7 7.3 %collective-permute-start.22 = (bf16[256,512]{1,0:T(8,128)(2,1)S(1)}, bf16[256,512]{1,0:T(8,128)(2,1)S(1)}, u32[]{:S(2)}, u32[]{:S(2)}) collective-permute-start(bf16[256,512]{1,0:T(8,128)(2,1)S(1)} %get-tuple-element.32), channel_id=1, source_target_pairs={{0,2},{1,3},{2,0},{3,1},{4,6},{5,7},{6,4},{7,5},{8,10},{9,11},{10,... | collective-permute-start | bytes 786440 | tf_op jit(solution)/shard_map/ppermute | solution.py:221
  92.9 12.8 %collective-permute-start.21 = (bf16[256,512]{1,0:T(8,128)(2,1)S(1)}, bf16[256,512]{1,0:T(8,128)(2,1)S(1)}, u32[]{:S(2)}, u32[]{:S(2)}) collective-permute-start(bf16[256,512]{1,0:T(8,128)(2,1)S(1)} %get-tuple-element.31), channel_id=1, source_target_pairs={{0,2},{1,3},{2,0},{3,1},{4,6},{5,7},{6,4},{7,5},{8,10},{9,11},{10,... | collective-permute-start | bytes 786440 | tf_op jit(solution)/shard_map/ppermute | solution.py:221
  94.4 11.3 %collective-permute-start.24 = (bf16[256,512]{1,0:T(8,128)(2,1)S(1)}, bf16[256,512]{1,0:T(8,128)(2,1)S(1)}, u32[]{:S(2)}, u32[]{:S(2)}) collective-permute-start(bf16[256,512]{1,0:T(8,128)(2,1)S(1)} %get-tuple-element.33), channel_id=1, source_target_pairs={{0,6},{1,7},{2,4},{3,5},{4,2},{5,3},{6,0},{7,1},{8,14},{9,15},{10,... | collective-permute-start | bytes 786440 | tf_op jit(solution)/shard_map/ppermute | solution.py:221
  99.8 11.5 %collective-permute-start.26 = (bf16[256,512]{1,0:T(8,128)(2,1)S(1)}, bf16[256,512]{1,0:T(8,128)(2,1)S(1)}, u32[]{:S(2)}, u32[]{:S(2)}) collective-permute-start(bf16[256,512]{1,0:T(8,128)(2,1)S(1)} %shard_map.111), channel_id=1, source_target_pairs={{0,2},{1,3},{2,0},{3,1},{4,6},{5,7},{6,4},{7,5},{8,10},{9,11},{10,... | collective-permute-start | bytes 786440 | tf_op jit(solution)/shard_map/ppermute | solution.py:221
  100.2 11.1 %collective-permute-start.23 = (bf16[256,512]{1,0:T(8,128)(2,1)S(1)}, bf16[256,512]{1,0:T(8,128)(2,1)S(1)}, u32[]{:S(2)}, u32[]{:S(2)}) collective-permute-start(bf16[256,512]{1,0:T(8,128)(2,1)S(1)} %shard_map.110), channel_id=1, source_target_pairs={{0,6},{1,7},{2,4},{3,5},{4,2},{5,3},{6,0},{7,1},{8,14},{9,15},{10,... | collective-permute-start | bytes 786440 | tf_op jit(solution)/shard_map/ppermute | solution.py:221

commit v6 on v5

--- a/solution.py
+++ b/solution.py
@@ -9,7 +9,7 @@
 MIB = 1024 * 1024
 
 
-def params(mib=32):
+def params(mib=8):
     return pltpu.CompilerParams(vmem_limit_bytes=mib * MIB)
 
 
@@ -143,15 +143,23 @@
         take = (here & bit) == 0 if reverse else (here & bit) != 0
         return jnp.where(take, x.astype(jnp.float32), 0.0)
 
-    total, entering = state, jnp.zeros(state.shape, jnp.float32)
-    for bit in (1, 2, 4):
-        theirs = swap(total, bit)
-        entering = entering + counted(theirs, bit)
-        total = (total.astype(jnp.float32) + theirs.astype(jnp.float32)).astype(jnp.bfloat16)
+    odd = (here & 1) != 0
+    kept = jnp.where(odd, state[:, 1], state[:, 0])
+    theirs = swap(jnp.where(odd, state[:, 0], state[:, 1]), 1)
+    total = (kept.astype(jnp.float32) + theirs.astype(jnp.float32)).astype(jnp.bfloat16)
+    entering = jnp.zeros(kept.shape, jnp.float32)
+    for bit in (2, 4):
+        peer = swap(total, bit)
+        entering = entering + counted(peer, bit)
+        total = (total.astype(jnp.float32) + peer.astype(jnp.float32)).astype(jnp.bfloat16)
     swapped = [swap(total, by) for by in (8, 16, 24)]
-    for theirs, bit in zip(swapped, (8, 16, 16)):
-        entering = entering + counted(theirs, bit)
-    return entering.astype(jnp.bfloat16)
+    for peer, bit in zip(swapped, (8, 16, 16)):
+        entering = entering + counted(peer, bit)
+    meets = jnp.logical_not(odd) if reverse else odd
+    mine = (entering + jnp.where(meets, theirs.astype(jnp.float32), 0.0)).astype(jnp.bfloat16)
+    partners = (entering + jnp.where(meets, 0.0, kept.astype(jnp.float32))).astype(jnp.bfloat16)
+    other = swap(partners, 1)
+    return jnp.stack([jnp.where(odd, other, mine), jnp.where(odd, mine, other)], axis=1)
 
 
 def make_sum_kernel(counts):
@@ -311,7 +319,7 @@
         grid=(seq_count, head_count),
         in_specs=[block] * 5 + [pl.BlockSpec((1, 1, HD, HD), lambda s, h: (s, h, 0, 0))],
         out_specs=[block] * 4,
-        compiler_params=params(),
+        compiler_params=params(48),
         cost_estimate=cost(12 * seq_count * rows * rows * columns, 3 * 1024 * 1024),
     )(queries, keys, values, d_output, slope, prefix)
 
@@ -327,7 +335,7 @@
                 out_specs=pl.BlockSpec((1, seq_count, rows, features), lambda k, t: (k, 0, 0, 0)),
                 scratch_shapes=[pltpu.VMEM(cube, bf16)] * 2,
             ),
-            compiler_params=params(),
+            compiler_params=params(48),
             cost_estimate=cost(32 * seq_count * rows * columns * features, 8 * 1024 * 1024),
         )(table, d_query, d_gate, dk_part, dv_part, keys, values, suffix, w_query, w_key, w_value, w_gate)
 

time: 113 us -> 117 us (1.035)
  waiting for transfers between devices: 44.9 us -> 35.6 us
  Pallas kernels: 18.4 us -> 24.2 us
  starting transfers between devices: 43.9 us -> 49 us
  local copies, waits for them, and re-layouts: 2.61 us -> 6.43 us
  other arithmetic: 2.37 us -> 0.55 us
    ppermute x12 -> x14, waiting for transfers between devices: 16.8 us -> 9.52 us  [swap(): return lax.ppermute(x, 'seq', [(i, i ^ by) for i in range(peers)])]
    ppermute x3, starting transfers between devices: 8.48 us -> 13.5 us  [other_core(): return lax.ppermute(x, 'head', [(i, i ^ 1) for i in range(peers)])]
    pallas_call x2, Pallas kernels: 7.8 us -> 11.3 us  [project(): pl.pallas_call(make_project_kernel(factor), out_shape=jax.ShapeDtypeStruc...]
    unnamed x20 -> x24, local copies, waits for them, and re-layouts: 2.57 us -> 5.59 us
    convert_element_type x8, other arithmetic: 2.36 us -> 0.34 us  [the longest x2 0.19 us: across_seq(): (entering + jnp.where(meets, 0.0, kept.astype(jnp.float32))).astype(jnp.b...]
    ppermute x12, waiting for transfers between devices: 27.6 us -> 26.1 us  [along_y(): return lax.ppermute(x, 'head', [(i, i ^ 2 * by) for i in range(peers)])]
    pallas_call x1, Pallas kernels: 0.8 us -> 2.19 us  [body(): pl.pallas_call(pick_kernel, out_shape=jax.ShapeDtypeStruct((4, columns, f...]
    pallas_call x1, Pallas kernels: 1.53 us -> 0.34 us  [body(): pl.pallas_call(gate_kernel, out_shape=[jax.ShapeDtypeStruct(cube, bf16),...]
  transfers between devices with their start and end apart: 27 -> 29, of which waited for: 14 -> 15; matrix products, arithmetic and copies ran while one was open for 2% -> 1% of each run, Pallas kernels for 10% -> 11%
where the time goes in v6:
time: 117 us; the launch traced here: 116 us
  starting transfers between devices  49 us (42%)
  waiting for transfers between devices  35.6 us (30%)
  Pallas kernels  24.2 us (21%)
  local copies, waits for them, and re-layouts  6.43 us (5%)
    ppermute x12, waiting for transfers between devices, along_y(): return lax.ppermute(x, 'head', [(i, i ^ 2 * by) for i in range(peers)])  26.1 us
    ppermute x14, starting transfers between devices, swap(): return lax.ppermute(x, 'seq', [(i, i ^ by) for i in range(peers)])  24.7 us
    ppermute x3, starting transfers between devices, other_core(): return lax.ppermute(x, 'head', [(i, i ^ 1) for i in range(peers)])  13.5 us
    pallas_call x2, Pallas kernels, project(): pl.pallas_call(make_project_kernel(factor), out_shape=jax.ShapeDtypeStruc...  11.3 us
    ppermute x12, starting transfers between devices, along_y(): return lax.ppermute(x, 'head', [(i, i ^ 2 * by) for i in range(peers)])  10.8 us
    ppermute x14, waiting for transfers between devices, swap(): return lax.ppermute(x, 'seq', [(i, i ^ by) for i in range(peers)])  9.52 us
    unnamed x24, local copies, waits for them, and re-layouts  5.59 us
    pallas_call x1, Pallas kernels, body(): pl.pallas_call(gated_start_kernel, out_shape=two, grid_spec=pltpu.Prefetc...  3.22 us
  transfers between devices with their start and end apart: 29, of which 15 were waited for; matrix products, arithmetic and copies ran while one was open for 1% of the time, Pallas kernels for 11%

profile of v6, /device:TPU:1, one launch (start us, length us, event | category | flops | bytes accessed | tf_op | source)
XLA Modules:
  0.0 116.1 jit_solution(13204073900785893532)
XLA Ops:
  0.0 1.6 %copy-done = bf16[256,4096]{1,0:T(8,128)(2,1)S(1)} copy-done((bf16[256,4096]{1,0:T(8,128)(2,1)S(1)}, bf16[256,4096]{1,0:T(8,128)(2,1)}, u32[]{:S(2)}) %copy-start) | copy-done | bytes 2097176
  1.6 2.2 %shard_map.100 = bf16[4,256,512]{2,1,0:T(8,128)(2,1)} custom-call(s32[8]{0:T(128)S(1)} %fusion.24.table_ref, bf16[256,4096]{1,0:T(8,128)(2,1)S(1)} %copy-done), custom_call_target="tpu_custom_call" | custom-call | bytes 2097152 | tf_op jit(solution)/shard_map/pallas_call | solution.py:242
  3.8 3.2 %collective-permute-start.4 = (bf16[4,256,512]{2,1,0:T(8,128)(2,1)}, bf16[4,256,512]{2,1,0:T(8,128)(2,1)S(1)}, u32[]{:S(2)}, u32[]{:S(2)}) collective-permute-start(bf16[4,256,512]{2,1,0:T(8,128)(2,1)} %shard_map.100), channel_id=1, source_target_pairs={{0,1},{1,0},{2,3},{3,2},{4,5},{5,4},{6,7},{7,6},{8,9},{9,8},{10,11... | collective-permute-start | bytes 3145736 | tf_op jit(solution)/shard_map/ppermute | solution.py:232
  7.0 0.8 slice_bitcast_fusion
  7.9 1.5 %collective-permute-start.3 = (bf16[256,512]{1,0:T(8,128)(2,1)}, bf16[256,512]{1,0:T(8,128)(2,1)}, u32[]{:S(2)}, u32[]{:S(2)}) collective-permute-start(bf16[256,512]{1,0:T(8,128)(2,1)} %get-tuple-element.39), channel_id=1, source_target_pairs={{0,6},{1,7},{2,4},{3,5},{4,2},{5,3},{6,0},{7,1},{8,14},{9,15},{10,... | collective-permute-start | bytes 786440 | tf_op jit(solution)/shard_map/ppermute | solution.py:229
  9.3 0.4 collective-permute-start.1
  9.7 1.7 %collective-permute-start.2 = (bf16[256,512]{1,0:T(8,128)(2,1)}, bf16[256,512]{1,0:T(8,128)(2,1)}, u32[]{:S(2)}, u32[]{:S(2)}) collective-permute-start(bf16[256,512]{1,0:T(8,128)(2,1)} %get-tuple-element.40), channel_id=1, source_target_pairs={{0,6},{1,7},{2,4},{3,5},{4,2},{5,3},{6,0},{7,1},{8,14},{9,15},{10,... | collective-permute-start | bytes 786440 | tf_op jit(solution)/shard_map/ppermute | solution.py:229
  11.4 4.7 %collective-permute-done.a0 = bf16[256,512]{1,0:T(8,128)(2,1)S(1)} collective-permute-done((bf16[256,512]{1,0:T(8,128)(2,1)}, bf16[256,512]{1,0:T(8,128)(2,1)S(1)}, u32[]{:S(2)}, u32[]{:S(2)}) %collective-permute-start) | collective-permute-done | bytes 262176 | tf_op jit(solution)/shard_map/ppermute | solution.py:229
  16.1 1.0 collective-permute-start.5
  17.3 4.4 %collective-permute-done.1.a1 = bf16[256,512]{1,0:T(8,128)(2,1)} collective-permute-done((bf16[256,512]{1,0:T(8,128)(2,1)}, bf16[256,512]{1,0:T(8,128)(2,1)}, u32[]{:S(2)}, u32[]{:S(2)}) %collective-permute-start.1) | collective-permute-done | bytes 262176 | tf_op jit(solution)/shard_map/ppermute | solution.py:229
  21.7 1.2 %collective-permute-done.2.b0 = bf16[256,512]{1,0:T(8,128)(2,1)} collective-permute-done((bf16[256,512]{1,0:T(8,128)(2,1)}, bf16[256,512]{1,0:T(8,128)(2,1)}, u32[]{:S(2)}, u32[]{:S(2)}) %collective-permute-start.2) | collective-permute-done | bytes 262176 | tf_op jit(solution)/shard_map/ppermute | solution.py:229
  23.0 1.0 copy-done.6
  24.0 3.2 %shard_map.101 = (f32[2,256,256]{2,1,0:T(8,128)S(1)}, f32[2,256,256]{2,1,0:T(8,128)S(1)}) custom-call(s32[8]{0:T(128)S(1)} %fusion.24.table_ref, bf16[2,256,512]{2,1,0:T(8,128)(2,1)S(1)} %copy-done.6, bf16[256,512]{1,0:T(8,128)(2,1)S(1)} %collective-permute-done.a0, bf16[256,512]{1,0:T(8,128)(2,1)} %collective-permute-done.1.a1, ...), custom_call_target="tpu_custom_call" | custom-call | flops 805306368 | bytes 4194304 | tf_op jit(solution)/shard_map/pallas_call | solution.py:267
  27.2 1.3 %collective-permute-done.5.c0 = bf16[256,512]{1,0:T(8,128)(2,1)} collective-permute-done((bf16[256,512]{1,0:T(8,128)(2,1)S(1)}, bf16[256,512]{1,0:T(8,128)(2,1)}, u32[]{:S(2)}, u32[]{:S(2)}) %collective-permute-start.5) | collective-permute-done | bytes 262176 | tf_op jit(solution)/shard_map/ppermute | solution.py:229
  28.6 2.8 %shard_map.102 = (f32[2,256,256]{2,1,0:T(8,128)S(1)}, f32[2,256,256]{2,1,0:T(8,128)}) custom-call(s32[8]{0:T(128)S(1)} %fusion.24.table_ref, f32[2,256,256]{2,1,0:T(8,128)S(1)} %get-tuple-element.20.mine_in, f32[2,256,256]{2,1,0:T(8,128)S(1)} %get-tuple-element.21.other_in, bf16[256,512]{1,0:T(8,128)(2,1)} %collective-permute-done.5.c0, ...), custom_call_target="tpu_custom_call" | custom-call | flops 268435456 | bytes 3145728 | tf_op jit(solution)/shard_map/pallas_call | solution.py:284
  31.4 0.8 collective-permute-start.7
  32.5 1.3 %collective-permute-start.8 = (bf16[2,128,128]{2,1,0:T(8,128)(2,1)S(1)}, bf16[2,128,128]{2,1,0:T(8,128)(2,1)S(1)}, u32[]{:S(2)}, u32[]{:S(2)}) collective-permute-start(bf16[2,128,128]{2,1,0:T(8,128)(2,1)S(1)} %select_bitcast_fusion.5), channel_id=1, source_target_pairs={{0,8},{8,0},{16,24},{24,16},{32,40},{40,32},{48,56},{56,48},{64,72... | collective-permute-start | bytes 196616 | tf_op jit(solution)/shard_map/ppermute | solution.py:140
  33.8 1.9 %collective-permute-done.8 = bf16[2,128,128]{2,1,0:T(8,128)(2,1)S(1)} collective-permute-done((bf16[2,128,128]{2,1,0:T(8,128)(2,1)S(1)}, bf16[2,128,128]{2,1,0:T(8,128)(2,1)S(1)}, u32[]{:S(2)}, u32[]{:S(2)}) %collective-permute-start.8) | collective-permute-done | bytes 65568 | tf_op jit(solution)/shard_map/ppermute | solution.py:140
  35.8 2.8 %collective-permute-start.9 = (bf16[2,128,128]{2,1,0:T(8,128)(2,1)S(1)}, bf16[2,128,128]{2,1,0:T(8,128)(2,1)S(1)}, u32[]{:S(2)}, u32[]{:S(2)}) collective-permute-start(bf16[2,128,128]{2,1,0:T(8,128)(2,1)S(1)} %fusion.16), channel_id=1, source_target_pairs={{0,16},{8,24},{16,0},{24,8},{32,48},{40,56},{48,32},{56,40},{64,80... | collective-permute-start | bytes 196616 | tf_op jit(solution)/shard_map/ppermute | solution.py:140
  38.6 0.9 copy-done.7
  39.5 1.0 copy-done.10
  40.6 0.9 copy-done.11
  41.9 1.5 %collective-permute-start.15 = (bf16[2,128,128]{2,1,0:T(8,128)(2,1)S(1)}, bf16[2,128,128]{2,1,0:T(8,128)(2,1)S(1)}, u32[]{:S(2)}, u32[]{:S(2)}) collective-permute-start(bf16[2,128,128]{2,1,0:T(8,128)(2,1)S(1)} %select_bitcast_fusion.2), channel_id=1, source_target_pairs={{0,8},{8,0},{16,24},{24,16},{32,40},{40,32},{48,56},{56,48},{64,72... | collective-permute-start | bytes 196616 | tf_op jit(solution)/shard_map/ppermute | solution.py:140
  43.5 4.3 %collective-permute-start.10 = (bf16[2,128,128]{2,1,0:T(8,128)(2,1)S(1)}, bf16[2,128,128]{2,1,0:T(8,128)(2,1)S(1)}, u32[]{:S(2)}, u32[]{:S(2)}) collective-permute-start(bf16[2,128,128]{2,1,0:T(8,128)(2,1)S(1)} %fusion.6), channel_id=1, source_target_pairs={{0,32},{8,40},{16,48},{24,56},{32,0},{40,8},{48,16},{56,24},{64,96... | collective-permute-start | bytes 196616 | tf_op jit(solution)/shard_map/ppermute | solution.py:140
  47.8 1.3 %collective-permute-start.16 = (bf16[2,128,128]{2,1,0:T(8,128)(2,1)S(1)}, bf16[2,128,128]{2,1,0:T(8,128)(2,1)S(1)}, u32[]{:S(2)}, u32[]{:S(2)}) collective-permute-start(bf16[2,128,128]{2,1,0:T(8,128)(2,1)S(1)} %fusion.19), channel_id=1, source_target_pairs={{0,16},{8,24},{16,0},{24,8},{32,48},{40,56},{48,32},{56,40},{64,80... | collective-permute-start | bytes 196616 | tf_op jit(solution)/shard_map/ppermute | solution.py:140
  49.1 1.6 %collective-permute-done.10 = bf16[2,128,128]{2,1,0:T(8,128)(2,1)S(1)} collective-permute-done((bf16[2,128,128]{2,1,0:T(8,128)(2,1)S(1)}, bf16[2,128,128]{2,1,0:T(8,128)(2,1)S(1)}, u32[]{:S(2)}, u32[]{:S(2)}) %collective-permute-start.10) | collective-permute-done | bytes 65568 | tf_op jit(solution)/shard_map/ppermute | solution.py:140
  50.7 1.3 %collective-permute-start.11 = (bf16[2,128,128]{2,1,0:T(8,128)(2,1)S(1)}, bf16[2,128,128]{2,1,0:T(8,128)(2,1)S(1)}, u32[]{:S(2)}, u32[]{:S(2)}) collective-permute-start(bf16[2,128,128]{2,1,0:T(8,128)(2,1)S(1)} %fusion.7), channel_id=1, source_target_pairs={{0,64},{8,72},{16,80},{24,88},{32,96},{40,104},{48,112},{56,120},{... | collective-permute-start | bytes 196616 | tf_op jit(solution)/shard_map/ppermute | solution.py:140
  52.0 2.5 %collective-permute-start.12 = (bf16[2,128,128]{2,1,0:T(8,128)(2,1)S(1)}, bf16[2,128,128]{2,1,0:T(8,128)(2,1)S(1)}, u32[]{:S(2)}, u32[]{:S(2)}) collective-permute-start(bf16[2,128,128]{2,1,0:T(8,128)(2,1)S(1)} %fusion.7), channel_id=1, source_target_pairs={{0,128},{8,136},{16,144},{24,152},{32,160},{40,168},{48,176},{56,1... | collective-permute-start | bytes 196616 | tf_op jit(solution)/shard_map/ppermute | solution.py:140
  54.6 4.3 %collective-permute-start.17 = (bf16[2,128,128]{2,1,0:T(8,128)(2,1)S(1)}, bf16[2,128,128]{2,1,0:T(8,128)(2,1)S(1)}, u32[]{:S(2)}, u32[]{:S(2)}) collective-permute-start(bf16[2,128,128]{2,1,0:T(8,128)(2,1)S(1)} %fusion.14), channel_id=1, source_target_pairs={{0,32},{8,40},{16,48},{24,56},{32,0},{40,8},{48,16},{56,24},{64,96... | collective-permute-start | bytes 196616 | tf_op jit(solution)/shard_map/ppermute | solution.py:140
  59.1 1.1 collective-permute-start.14
  60.2 1.5 %collective-permute-done.17 = bf16[2,128,128]{2,1,0:T(8,128)(2,1)S(1)} collective-permute-done((bf16[2,128,128]{2,1,0:T(8,128)(2,1)S(1)}, bf16[2,128,128]{2,1,0:T(8,128)(2,1)S(1)}, u32[]{:S(2)}, u32[]{:S(2)}) %collective-permute-start.17) | collective-permute-done | bytes 65568 | tf_op jit(solution)/shard_map/ppermute | solution.py:140
  61.8 1.0 collective-permute-start.18
  62.8 2.7 %collective-permute-start.19 = (bf16[2,128,128]{2,1,0:T(8,128)(2,1)S(1)}, bf16[2,128,128]{2,1,0:T(8,128)(2,1)S(1)}, u32[]{:S(2)}, u32[]{:S(2)}) collective-permute-start(bf16[2,128,128]{2,1,0:T(8,128)(2,1)S(1)} %fusion.15), channel_id=1, source_target_pairs={{0,128},{8,136},{16,144},{24,152},{32,160},{40,168},{48,176},{56,1... | collective-permute-start | bytes 196616 | tf_op jit(solution)/shard_map/ppermute | solution.py:140
  65.8 2.1 %collective-permute-done.19 = bf16[2,128,128]{2,1,0:T(8,128)(2,1)S(1)} collective-permute-done((bf16[2,128,128]{2,1,0:T(8,128)(2,1)S(1)}, bf16[2,128,128]{2,1,0:T(8,128)(2,1)S(1)}, u32[]{:S(2)}, u32[]{:S(2)}) %collective-permute-start.19) | collective-permute-done | bytes 65568 | tf_op jit(solution)/shard_map/ppermute | solution.py:140
  67.9 2.0 %collective-permute-done.20 = bf16[2,128,128]{2,1,0:T(8,128)(2,1)S(1)} collective-permute-done((bf16[2,128,128]{2,1,0:T(8,128)(2,1)S(1)}, bf16[2,128,128]{2,1,0:T(8,128)(2,1)S(1)}, u32[]{:S(2)}, u32[]{:S(2)}) %collective-permute-start.20) | collective-permute-done | bytes 65568 | tf_op jit(solution)/shard_map/ppermute | solution.py:140
  70.2 2.5 %shard_map.105 = (bf16[2,256,256]{2,1,0:T(8,128)(2,1)S(1)}, bf16[2,256,256]{2,1,0:T(8,128)(2,1)S(1)}, f32[2,256,256]{2,1,0:T(8,128)S(1)}, f32[2,256,256]{2,1,0:T(8,128)S(1)}) custom-call(bf16[2,256,256]{2,1,0:T(8,128)(2,1)S(1)} %copy-done.8, bf16[2,256,256]{2,1,0:T(8,128)(2,1)S(1)} %copy-done.2, bf16[2,256,256]{2,1,0:T(8,128)(2,1)S(1)} %copy-done.4, ...), custom_call_target="tpu_custom_call" | custom-call | flops 402653184 | bytes 3145728 | tf_op jit(solution)/shard_map/pallas_call | solution.py:316
  72.7 0.4 collective-permute-done.21
  73.3 5.7 %shard_map.107 = bf16[4,2,256,512]{3,2,1,0:T(8,128)(2,1)S(1)} custom-call(s32[8]{0:T(128)S(1)} %fusion.24.table_ref, bf16[2,256,256]{2,1,0:T(8,128)(2,1)S(1)} %get-tuple-element.26.dq_ref, bf16[2,256,256]{2,1,0:T(8,128)(2,1)S(1)} %get-tuple-element.27.dg_ref, f32[2,256,256]{2,1,0:T(8,128)S(1)} %get-tuple-element.28.dk_part, ...), custom_call_target="tpu_custom_call" | custom-call | flops 2147483648 | bytes 8388608 | tf_op jit(solution)/shard_map/pallas_call | solution.py:328
  78.9 9.5 %collective-permute-start.22 = (bf16[4,2,256,512]{3,2,1,0:T(8,128)(2,1)S(1)}, bf16[4,2,256,512]{3,2,1,0:T(8,128)(2,1)S(1)}, u32[]{:S(2)}, u32[]{:S(2)}) collective-permute-start(bf16[4,2,256,512]{3,2,1,0:T(8,128)(2,1)S(1)} %shard_map.107), channel_id=1, source_target_pairs={{0,1},{1,0},{2,3},{3,2},{4,5},{5,4},{6,7},{7,6},{8,9},{9,8},{10,11... | collective-permute-start | bytes 6291464 | tf_op jit(solution)/shard_map/ppermute | solution.py:232
  88.4 5.6 %shard_map.106.refs_0_.refs_2_.refs_4_ = bf16[4,2,256,512]{3,2,1,0:T(8,128)(2,1)S(1)} custom-call(s32[8]{0:T(128)S(1)} %fusion.24.table_ref, bf16[2,256,256]{2,1,0:T(8,128)(2,1)S(1)} %get-tuple-element.26.dq_ref, bf16[2,256,256]{2,1,0:T(8,128)(2,1)S(1)} %get-tuple-element.27.dg_ref, f32[2,256,256]{2,1,0:T(8,128)S(1)} %get-tuple-element.28.dk_part, ...), custom_call_target="tpu_custom_call" | custom-call | flops 2147483648 | bytes 8388608 | tf_op jit(solution)/shard_map/pallas_call | solution.py:328
  94.2 2.0 %collective-permute-start.27 = (bf16[256,512]{1,0:T(8,128)(2,1)S(1)}, bf16[256,512]{1,0:T(8,128)(2,1)S(1)}, u32[]{:S(2)}, u32[]{:S(2)}) collective-permute-start(bf16[256,512]{1,0:T(8,128)(2,1)S(1)} %get-tuple-element.34), channel_id=1, source_target_pairs={{0,6},{1,7},{2,4},{3,5},{4,2},{5,3},{6,0},{7,1},{8,14},{9,15},{10,... | collective-permute-start | bytes 786440 | tf_op jit(solution)/shard_map/ppermute | solution.py:229
  96.4 1.5 %collective-permute-start.23 = (bf16[256,512]{1,0:T(8,128)(2,1)S(1)}, bf16[256,512]{1,0:T(8,128)(2,1)S(1)}, u32[]{:S(2)}, u32[]{:S(2)}) collective-permute-start(bf16[256,512]{1,0:T(8,128)(2,1)S(1)} %get-tuple-element.31), channel_id=1, source_target_pairs={{0,2},{1,3},{2,0},{3,1},{4,6},{5,7},{6,4},{7,5},{8,10},{9,11},{10,... | collective-permute-start | bytes 786440 | tf_op jit(solution)/shard_map/ppermute | solution.py:229
  97.9 0.8 collective-permute-start.26
  98.7 4.8 %collective-permute-done.27.refs_2_ = bf16[256,512]{1,0:T(8,128)(2,1)S(1)} collective-permute-done((bf16[256,512]{1,0:T(8,128)(2,1)S(1)}, bf16[256,512]{1,0:T(8,128)(2,1)S(1)}, u32[]{:S(2)}, u32[]{:S(2)}) %collective-permute-start.27) | collective-permute-done | bytes 262176 | tf_op jit(solution)/shard_map/ppermute | solution.py:229
  103.9 1.8 %collective-permute-start.25 = (bf16[256,512]{1,0:T(8,128)(2,1)S(1)}, bf16[256,512]{1,0:T(8,128)(2,1)S(1)}, u32[]{:S(2)}, u32[]{:S(2)}) collective-permute-start(bf16[256,512]{1,0:T(8,128)(2,1)S(1)} %shard_map.110), channel_id=1, source_target_pairs={{0,6},{1,7},{2,4},{3,5},{4,2},{5,3},{6,0},{7,1},{8,14},{9,15},{10,... | collective-permute-start | bytes 786440 | tf_op jit(solution)/shard_map/ppermute | solution.py:229
  105.8 3.7 %collective-permute-done.23.refs_2_ = bf16[256,512]{1,0:T(8,128)(2,1)S(1)} collective-permute-done((bf16[256,512]{1,0:T(8,128)(2,1)S(1)}, bf16[256,512]{1,0:T(8,128)(2,1)S(1)}, u32[]{:S(2)}, u32[]{:S(2)}) %collective-permute-start.23) | collective-permute-done | bytes 262176 | tf_op jit(solution)/shard_map/ppermute | solution.py:229
  109.4 5.6 %collective-permute-done.28.refs_7_ = bf16[256,512]{1,0:T(8,128)(2,1)S(1)} collective-permute-done((bf16[256,512]{1,0:T(8,128)(2,1)S(1)}, bf16[256,512]{1,0:T(8,128)(2,1)S(1)}, u32[]{:S(2)}, u32[]{:S(2)}) %collective-permute-start.28) | collective-permute-done | bytes 262176 | tf_op jit(solution)/shard_map/ppermute | solution.py:229
  115.1 1.1 shard_map.112
  (65 shorter events, 2.8 us)
Async XLA Ops:
  0.0 1.6 %copy-start = (bf16[256,4096]{1,0:T(8,128)(2,1)S(1)}, bf16[256,4096]{1,0:T(8,128)(2,1)}, u32[]{:S(2)}) copy-start(bf16[256,4096]{1,0:T(8,128)(2,1)} %w_ref.5) | copy-start | bytes 6291460
  1.6 5.4 %copy-start.5 = (bf16[2,256,512]{2,1,0:T(8,128)(2,1)S(1)}, bf16[2,256,512]{2,1,0:T(8,128)(2,1)}, u32[]{:S(2)}) copy-start(bf16[2,256,512]{2,1,0:T(8,128)(2,1)} %g_ref.1) | copy-start | bytes 1572868
  1.6 21.4 %copy-start.1 = (bf16[256,4096]{1,0:T(8,128)(2,1)S(1)}, bf16[256,4096]{1,0:T(8,128)(2,1)}, u32[]{:S(2)}) copy-start(bf16[256,4096]{1,0:T(8,128)(2,1)} %w_ref.5) | copy-start | bytes 6291460
  3.8 19.2 %collective-permute-start.4 = (bf16[4,256,512]{2,1,0:T(8,128)(2,1)}, bf16[4,256,512]{2,1,0:T(8,128)(2,1)S(1)}, u32[]{:S(2)}, u32[]{:S(2)}) collective-permute-start(bf16[4,256,512]{2,1,0:T(8,128)(2,1)} %shard_map.100), channel_id=1, source_target_pairs={{0,1},{1,0},{2,3},{3,2},{4,5},{5,4},{6,7},{7,6},{8,9},{9,8},{10,11... | collective-permute-start | bytes 3145736 | tf_op jit(solution)/shard_map/ppermute | solution.py:232
  7.9 8.3 %collective-permute-start = (bf16[256,512]{1,0:T(8,128)(2,1)}, bf16[256,512]{1,0:T(8,128)(2,1)S(1)}, u32[]{:S(2)}, u32[]{:S(2)}) collective-permute-start(bf16[256,512]{1,0:T(8,128)(2,1)} %get-tuple-element.40), channel_id=1, source_target_pairs={{0,2},{1,3},{2,0},{3,1},{4,6},{5,7},{6,4},{7,5},{8,10},{9,11},{10,... | collective-permute-start | bytes 786440 | tf_op jit(solution)/shard_map/ppermute | solution.py:229
  7.9 9.5 %collective-permute-start.3 = (bf16[256,512]{1,0:T(8,128)(2,1)}, bf16[256,512]{1,0:T(8,128)(2,1)}, u32[]{:S(2)}, u32[]{:S(2)}) collective-permute-start(bf16[256,512]{1,0:T(8,128)(2,1)} %get-tuple-element.39), channel_id=1, source_target_pairs={{0,6},{1,7},{2,4},{3,5},{4,2},{5,3},{6,0},{7,1},{8,14},{9,15},{10,... | collective-permute-start | bytes 786440 | tf_op jit(solution)/shard_map/ppermute | solution.py:229
  9.3 12.4 %collective-permute-start.1 = (bf16[256,512]{1,0:T(8,128)(2,1)}, bf16[256,512]{1,0:T(8,128)(2,1)}, u32[]{:S(2)}, u32[]{:S(2)}) collective-permute-start(bf16[256,512]{1,0:T(8,128)(2,1)} %get-tuple-element.39), channel_id=1, source_target_pairs={{0,2},{1,3},{2,0},{3,1},{4,6},{5,7},{6,4},{7,5},{8,10},{9,11},{10,... | collective-permute-start | bytes 786440 | tf_op jit(solution)/shard_map/ppermute | solution.py:229
  9.7 13.2 %collective-permute-start.2 = (bf16[256,512]{1,0:T(8,128)(2,1)}, bf16[256,512]{1,0:T(8,128)(2,1)}, u32[]{:S(2)}, u32[]{:S(2)}) collective-permute-start(bf16[256,512]{1,0:T(8,128)(2,1)} %get-tuple-element.40), channel_id=1, source_target_pairs={{0,6},{1,7},{2,4},{3,5},{4,2},{5,3},{6,0},{7,1},{8,14},{9,15},{10,... | collective-permute-start | bytes 786440 | tf_op jit(solution)/shard_map/ppermute | solution.py:229
  16.1 12.4 %collective-permute-start.5 = (bf16[256,512]{1,0:T(8,128)(2,1)S(1)}, bf16[256,512]{1,0:T(8,128)(2,1)}, u32[]{:S(2)}, u32[]{:S(2)}) collective-permute-start(bf16[256,512]{1,0:T(8,128)(2,1)S(1)} %collective-permute-done.a0), channel_id=1, source_target_pairs={{0,6},{1,7},{2,4},{3,5},{4,2},{5,3},{6,0},{7,1},{8,14},{9,15},{10,... | collective-permute-start | bytes 786440 | tf_op jit(solution)/shard_map/ppermute | solution.py:229
  17.3 11.2 %collective-permute-start.6 = (bf16[256,512]{1,0:T(8,128)(2,1)}, bf16[256,512]{1,0:T(8,128)(2,1)}, u32[]{:S(2)}, u32[]{:S(2)}) collective-permute-start(bf16[256,512]{1,0:T(8,128)(2,1)} %collective-permute-done.3.b1), channel_id=1, source_target_pairs={{0,2},{1,3},{2,0},{3,1},{4,6},{5,7},{6,4},{7,5},{8,10},{9,11},{10,... | collective-permute-start | bytes 786440 | tf_op jit(solution)/shard_map/ppermute | solution.py:229
  23.0 1.0 copy-start.6
  28.6 3.6 %copy-start.2 = (bf16[2,256,256]{2,1,0:T(8,128)(2,1)S(1)}, bf16[2,256,256]{2,1,0:T(8,128)(2,1)}, u32[]{:S(2)}) copy-start(bf16[2,256,256]{2,1,0:T(8,128)(2,1)} %k_ref.7) | copy-start | bytes 786436
  28.6 3.6 %copy-start.3 = (bf16[2,256,256]{2,1,0:T(8,128)(2,1)S(1)}, bf16[2,256,256]{2,1,0:T(8,128)(2,1)}, u32[]{:S(2)}) copy-start(bf16[2,256,256]{2,1,0:T(8,128)(2,1)} %v_ref.7) | copy-start | bytes 786436
  31.4 1.1 copy-start.9
  31.4 7.2 %collective-permute-start.7 = (f32[2,256,256]{2,1,0:T(8,128)}, f32[2,256,256]{2,1,0:T(8,128)S(1)}, u32[]{:S(2)}, u32[]{:S(2)}) collective-permute-start(f32[2,256,256]{2,1,0:T(8,128)} %get-tuple-element.23), channel_id=1, source_target_pairs={{0,1},{1,0},{2,3},{3,2},{4,5},{5,4},{6,7},{7,6},{8,9},{9,8},{10,11... | collective-permute-start | bytes 1572872 | tf_op jit(solution)/shard_map/ppermute | solution.py:232
  32.5 3.2 %collective-permute-start.8 = (bf16[2,128,128]{2,1,0:T(8,128)(2,1)S(1)}, bf16[2,128,128]{2,1,0:T(8,128)(2,1)S(1)}, u32[]{:S(2)}, u32[]{:S(2)}) collective-permute-start(bf16[2,128,128]{2,1,0:T(8,128)(2,1)S(1)} %select_bitcast_fusion.5), channel_id=1, source_target_pairs={{0,8},{8,0},{16,24},{24,16},{32,40},{40,32},{48,56},{56,48},{64,72... | collective-permute-start | bytes 196616 | tf_op jit(solution)/shard_map/ppermute | solution.py:140
  35.8 7.7 %collective-permute-start.9 = (bf16[2,128,128]{2,1,0:T(8,128)(2,1)S(1)}, bf16[2,128,128]{2,1,0:T(8,128)(2,1)S(1)}, u32[]{:S(2)}, u32[]{:S(2)}) collective-permute-start(bf16[2,128,128]{2,1,0:T(8,128)(2,1)S(1)} %fusion.16), channel_id=1, source_target_pairs={{0,16},{8,24},{16,0},{24,8},{32,48},{40,56},{48,32},{56,40},{64,80... | collective-permute-start | bytes 196616 | tf_op jit(solution)/shard_map/ppermute | solution.py:140
  38.6 1.0 copy-start.7
  39.5 1.0 copy-start.10
  40.6 0.9 copy-start.11
  41.5 28.7 %copy-start.4 = (bf16[2,256,256]{2,1,0:T(8,128)(2,1)S(1)}, bf16[2,256,256]{2,1,0:T(8,128)(2,1)}, u32[]{:S(2)}) copy-start(bf16[2,256,256]{2,1,0:T(8,128)(2,1)} %v_ref.7) | copy-start | bytes 786436
  41.5 28.7 %copy-start.8 = (bf16[2,256,256]{2,1,0:T(8,128)(2,1)S(1)}, bf16[2,256,256]{2,1,0:T(8,128)(2,1)}, u32[]{:S(2)}) copy-start(bf16[2,256,256]{2,1,0:T(8,128)(2,1)} %q_ref.3) | copy-start | bytes 786436
  41.9 5.9 %collective-permute-start.15 = (bf16[2,128,128]{2,1,0:T(8,128)(2,1)S(1)}, bf16[2,128,128]{2,1,0:T(8,128)(2,1)S(1)}, u32[]{:S(2)}, u32[]{:S(2)}) collective-permute-start(bf16[2,128,128]{2,1,0:T(8,128)(2,1)S(1)} %select_bitcast_fusion.2), channel_id=1, source_target_pairs={{0,8},{8,0},{16,24},{24,16},{32,40},{40,32},{48,56},{56,48},{64,72... | collective-permute-start | bytes 196616 | tf_op jit(solution)/shard_map/ppermute | solution.py:140
  43.5 7.2 %collective-permute-start.10 = (bf16[2,128,128]{2,1,0:T(8,128)(2,1)S(1)}, bf16[2,128,128]{2,1,0:T(8,128)(2,1)S(1)}, u32[]{:S(2)}, u32[]{:S(2)}) collective-permute-start(bf16[2,128,128]{2,1,0:T(8,128)(2,1)S(1)} %fusion.6), channel_id=1, source_target_pairs={{0,32},{8,40},{16,48},{24,56},{32,0},{40,8},{48,16},{56,24},{64,96... | collective-permute-start | bytes 196616 | tf_op jit(solution)/shard_map/ppermute | solution.py:140
  47.8 6.8 %collective-permute-start.16 = (bf16[2,128,128]{2,1,0:T(8,128)(2,1)S(1)}, bf16[2,128,128]{2,1,0:T(8,128)(2,1)S(1)}, u32[]{:S(2)}, u32[]{:S(2)}) collective-permute-start(bf16[2,128,128]{2,1,0:T(8,128)(2,1)S(1)} %fusion.19), channel_id=1, source_target_pairs={{0,16},{8,24},{16,0},{24,8},{32,48},{40,56},{48,32},{56,40},{64,80... | collective-permute-start | bytes 196616 | tf_op jit(solution)/shard_map/ppermute | solution.py:140
  50.7 8.3 %collective-permute-start.11 = (bf16[2,128,128]{2,1,0:T(8,128)(2,1)S(1)}, bf16[2,128,128]{2,1,0:T(8,128)(2,1)S(1)}, u32[]{:S(2)}, u32[]{:S(2)}) collective-permute-start(bf16[2,128,128]{2,1,0:T(8,128)(2,1)S(1)} %fusion.7), channel_id=1, source_target_pairs={{0,64},{8,72},{16,80},{24,88},{32,96},{40,104},{48,112},{56,120},{... | collective-permute-start | bytes 196616 | tf_op jit(solution)/shard_map/ppermute | solution.py:140
  52.0 7.0 %collective-permute-start.12 = (bf16[2,128,128]{2,1,0:T(8,128)(2,1)S(1)}, bf16[2,128,128]{2,1,0:T(8,128)(2,1)S(1)}, u32[]{:S(2)}, u32[]{:S(2)}) collective-permute-start(bf16[2,128,128]{2,1,0:T(8,128)(2,1)S(1)} %fusion.7), channel_id=1, source_target_pairs={{0,128},{8,136},{16,144},{24,152},{32,160},{40,168},{48,176},{56,1... | collective-permute-start | bytes 196616 | tf_op jit(solution)/shard_map/ppermute | solution.py:140
  54.4 4.6 %collective-permute-start.13 = (bf16[2,128,128]{2,1,0:T(8,128)(2,1)S(1)}, bf16[2,128,128]{2,1,0:T(8,128)(2,1)S(1)}, u32[]{:S(2)}, u32[]{:S(2)}) collective-permute-start(bf16[2,128,128]{2,1,0:T(8,128)(2,1)S(1)} %fusion.7), channel_id=1, source_target_pairs={{0,192},{8,200},{16,208},{24,216},{32,224},{40,232},{48,240},{56,2... | collective-permute-start | bytes 196616 | tf_op jit(solution)/shard_map/ppermute | solution.py:140
  54.6 7.1 %collective-permute-start.17 = (bf16[2,128,128]{2,1,0:T(8,128)(2,1)S(1)}, bf16[2,128,128]{2,1,0:T(8,128)(2,1)S(1)}, u32[]{:S(2)}, u32[]{:S(2)}) collective-permute-start(bf16[2,128,128]{2,1,0:T(8,128)(2,1)S(1)} %fusion.14), channel_id=1, source_target_pairs={{0,32},{8,40},{16,48},{24,56},{32,0},{40,8},{48,16},{56,24},{64,96... | collective-permute-start | bytes 196616 | tf_op jit(solution)/shard_map/ppermute | solution.py:140
  59.1 6.6 %collective-permute-start.14 = (bf16[2,128,128]{2,1,0:T(8,128)(2,1)S(1)}, bf16[2,128,128]{2,1,0:T(8,128)(2,1)S(1)}, u32[]{:S(2)}, u32[]{:S(2)}) collective-permute-start(bf16[2,128,128]{2,1,0:T(8,128)(2,1)S(1)} %get-tuple-element.37), channel_id=1, source_target_pairs={{0,8},{8,0},{16,24},{24,16},{32,40},{40,32},{48,56},{56,48},{64,72... | collective-permute-start | bytes 196616 | tf_op jit(solution)/shard_map/ppermute | solution.py:140
  61.8 4.0 %collective-permute-start.18 = (bf16[2,128,128]{2,1,0:T(8,128)(2,1)S(1)}, bf16[2,128,128]{2,1,0:T(8,128)(2,1)S(1)}, u32[]{:S(2)}, u32[]{:S(2)}) collective-permute-start(bf16[2,128,128]{2,1,0:T(8,128)(2,1)S(1)} %fusion.15), channel_id=1, source_target_pairs={{0,64},{8,72},{16,80},{24,88},{32,96},{40,104},{48,112},{56,120},{... | collective-permute-start | bytes 196616 | tf_op jit(solution)/shard_map/ppermute | solution.py:140
  62.8 5.1 %collective-permute-start.19 = (bf16[2,128,128]{2,1,0:T(8,128)(2,1)S(1)}, bf16[2,128,128]{2,1,0:T(8,128)(2,1)S(1)}, u32[]{:S(2)}, u32[]{:S(2)}) collective-permute-start(bf16[2,128,128]{2,1,0:T(8,128)(2,1)S(1)} %fusion.15), channel_id=1, source_target_pairs={{0,128},{8,136},{16,144},{24,152},{32,160},{40,168},{48,176},{56,1... | collective-permute-start | bytes 196616 | tf_op jit(solution)/shard_map/ppermute | solution.py:140
  65.5 4.3 %collective-permute-start.20 = (bf16[2,128,128]{2,1,0:T(8,128)(2,1)S(1)}, bf16[2,128,128]{2,1,0:T(8,128)(2,1)S(1)}, u32[]{:S(2)}, u32[]{:S(2)}) collective-permute-start(bf16[2,128,128]{2,1,0:T(8,128)(2,1)S(1)} %fusion.15), channel_id=1, source_target_pairs={{0,192},{8,200},{16,208},{24,216},{32,224},{40,232},{48,240},{56,2... | collective-permute-start | bytes 196616 | tf_op jit(solution)/shard_map/ppermute | solution.py:140
  69.9 3.2 %collective-permute-start.21 = (bf16[2,128,128]{2,1,0:T(8,128)(2,1)S(1)}, bf16[2,128,128]{2,1,0:T(8,128)(2,1)S(1)}, u32[]{:S(2)}, u32[]{:S(2)}) collective-permute-start(bf16[2,128,128]{2,1,0:T(8,128)(2,1)S(1)} %fusion.21), channel_id=1, source_target_pairs={{0,8},{8,0},{16,24},{24,16},{32,40},{40,32},{48,56},{56,48},{64,72... | collective-permute-start | bytes 196616 | tf_op jit(solution)/shard_map/ppermute | solution.py:140
  78.9 15.2 %collective-permute-start.22 = (bf16[4,2,256,512]{3,2,1,0:T(8,128)(2,1)S(1)}, bf16[4,2,256,512]{3,2,1,0:T(8,128)(2,1)S(1)}, u32[]{:S(2)}, u32[]{:S(2)}) collective-permute-start(bf16[4,2,256,512]{3,2,1,0:T(8,128)(2,1)S(1)} %shard_map.107), channel_id=1, source_target_pairs={{0,1},{1,0},{2,3},{3,2},{4,5},{5,4},{6,7},{7,6},{8,9},{9,8},{10,11... | collective-permute-start | bytes 6291464 | tf_op jit(solution)/shard_map/ppermute | solution.py:232
  94.2 9.2 %collective-permute-start.27 = (bf16[256,512]{1,0:T(8,128)(2,1)S(1)}, bf16[256,512]{1,0:T(8,128)(2,1)S(1)}, u32[]{:S(2)}, u32[]{:S(2)}) collective-permute-start(bf16[256,512]{1,0:T(8,128)(2,1)S(1)} %get-tuple-element.34), channel_id=1, source_target_pairs={{0,6},{1,7},{2,4},{3,5},{4,2},{5,3},{6,0},{7,1},{8,14},{9,15},{10,... | collective-permute-start | bytes 786440 | tf_op jit(solution)/shard_map/ppermute | solution.py:229
  96.2 7.6 %collective-permute-start.24 = (bf16[256,512]{1,0:T(8,128)(2,1)S(1)}, bf16[256,512]{1,0:T(8,128)(2,1)S(1)}, u32[]{:S(2)}, u32[]{:S(2)}) collective-permute-start(bf16[256,512]{1,0:T(8,128)(2,1)S(1)} %get-tuple-element.32), channel_id=1, source_target_pairs={{0,2},{1,3},{2,0},{3,1},{4,6},{5,7},{6,4},{7,5},{8,10},{9,11},{10,... | collective-permute-start | bytes 786440 | tf_op jit(solution)/shard_map/ppermute | solution.py:229
  96.4 13.1 %collective-permute-start.23 = (bf16[256,512]{1,0:T(8,128)(2,1)S(1)}, bf16[256,512]{1,0:T(8,128)(2,1)S(1)}, u32[]{:S(2)}, u32[]{:S(2)}) collective-permute-start(bf16[256,512]{1,0:T(8,128)(2,1)S(1)} %get-tuple-element.31), channel_id=1, source_target_pairs={{0,2},{1,3},{2,0},{3,1},{4,6},{5,7},{6,4},{7,5},{8,10},{9,11},{10,... | collective-permute-start | bytes 786440 | tf_op jit(solution)/shard_map/ppermute | solution.py:229
  97.9 11.5 %collective-permute-start.26 = (bf16[256,512]{1,0:T(8,128)(2,1)S(1)}, bf16[256,512]{1,0:T(8,128)(2,1)S(1)}, u32[]{:S(2)}, u32[]{:S(2)}) collective-permute-start(bf16[256,512]{1,0:T(8,128)(2,1)S(1)} %get-tuple-element.33), channel_id=1, source_target_pairs={{0,6},{1,7},{2,4},{3,5},{4,2},{5,3},{6,0},{7,1},{8,14},{9,15},{10,... | collective-permute-start | bytes 786440 | tf_op jit(solution)/shard_map/ppermute | solution.py:229
  103.5 11.5 %collective-permute-start.28 = (bf16[256,512]{1,0:T(8,128)(2,1)S(1)}, bf16[256,512]{1,0:T(8,128)(2,1)S(1)}, u32[]{:S(2)}, u32[]{:S(2)}) collective-permute-start(bf16[256,512]{1,0:T(8,128)(2,1)S(1)} %shard_map.111), channel_id=1, source_target_pairs={{0,2},{1,3},{2,0},{3,1},{4,6},{5,7},{6,4},{7,5},{8,10},{9,11},{10,... | collective-permute-start | bytes 786440 | tf_op jit(solution)/shard_map/ppermute | solution.py:229
  103.9 11.1 %collective-permute-start.25 = (bf16[256,512]{1,0:T(8,128)(2,1)S(1)}, bf16[256,512]{1,0:T(8,128)(2,1)S(1)}, u32[]{:S(2)}, u32[]{:S(2)}) collective-permute-start(bf16[256,512]{1,0:T(8,128)(2,1)S(1)} %shard_map.110), channel_id=1, source_target_pairs={{0,6},{1,7},{2,4},{3,5},{4,2},{5,3},{6,0},{7,1},{8,14},{9,15},{10,... | collective-permute-start | bytes 786440 | tf_op jit(solution)/shard_map/ppermute | solution.py:229

commit v7 on v6

--- a/solution.py
+++ b/solution.py
@@ -9,7 +9,7 @@
 MIB = 1024 * 1024
 
 
-def params(mib=8):
+def params(mib=32):
     return pltpu.CompilerParams(vmem_limit_bytes=mib * MIB)
 
 
@@ -133,7 +133,7 @@
     return project_kernel
 
 
-def across_seq(state, reverse):
+def across_seq(state, reverse, behind=None):
     peers, here = lax.axis_size("seq"), lax.axis_index("seq")
 
     def swap(x, by):
@@ -146,6 +146,8 @@
     odd = (here & 1) != 0
     kept = jnp.where(odd, state[:, 1], state[:, 0])
     theirs = swap(jnp.where(odd, state[:, 0], state[:, 1]), 1)
+    if behind is not None:
+        theirs, _ = lax.optimization_barrier((theirs, behind))
     total = (kept.astype(jnp.float32) + theirs.astype(jnp.float32)).astype(jnp.bfloat16)
     entering = jnp.zeros(kept.shape, jnp.float32)
     for bit in (2, 4):
@@ -259,7 +261,6 @@
         compiler_params=params(),
         cost_estimate=cost(2 * seq_count * rows * columns * HD, 4 * seq_count * rows * columns),
     )(keys, values)
-    prefix = across_seq(key_state, False)
 
     flat = (rows, features)
     two = [jax.ShapeDtypeStruct(cube, f32)] * 2
@@ -310,6 +311,7 @@
         compiler_params=params(),
         cost_estimate=cost(2 * seq_count * rows * columns * HD, 3 * 1024 * 1024),
     )(mine, theirs, gate_pre, queries)
+    prefix = across_seq(key_state, False, query_state)
     suffix = across_seq(query_state, True)
 
     block = pl.BlockSpec((1, rows, HD), lambda s, h: (s, 0, h))
@@ -319,7 +321,7 @@
         grid=(seq_count, head_count),
         in_specs=[block] * 5 + [pl.BlockSpec((1, 1, HD, HD), lambda s, h: (s, h, 0, 0))],
         out_specs=[block] * 4,
-        compiler_params=params(48),
+        compiler_params=params(),
         cost_estimate=cost(12 * seq_count * rows * rows * columns, 3 * 1024 * 1024),
     )(queries, keys, values, d_output, slope, prefix)
 
@@ -335,7 +337,7 @@
                 out_specs=pl.BlockSpec((1, seq_count, rows, features), lambda k, t: (k, 0, 0, 0)),
                 scratch_shapes=[pltpu.VMEM(cube, bf16)] * 2,
             ),
-            compiler_params=params(48),
+            compiler_params=params(),
             cost_estimate=cost(32 * seq_count * rows * columns * features, 8 * 1024 * 1024),
         )(table, d_query, d_gate, dk_part, dv_part, keys, values, suffix, w_query, w_key, w_value, w_gate)
 

time: 117 us -> 103 us (0.88)
  Pallas kernels: 24.2 us -> 18.4 us
  starting transfers between devices: 49 us -> 44.3 us
  local copies, waits for them, and re-layouts: 6.43 us -> 2.62 us
  other arithmetic: 0.55 us -> 2.85 us
  waiting for transfers between devices: 35.6 us -> 34.2 us
    ppermute x3, starting transfers between devices: 13.5 us -> 9.81 us  [other_core(): return lax.ppermute(x, 'head', [(i, i ^ 1) for i in range(peers)])]
    pallas_call x2, Pallas kernels: 11.3 us -> 7.8 us  [project(): pl.pallas_call(make_project_kernel(factor), out_shape=jax.ShapeDtypeStruc...]
    unnamed x24 -> x20, local copies, waits for them, and re-layouts: 5.59 us -> 2.57 us
    ppermute x14, waiting for transfers between devices: 9.52 us -> 6.57 us  [swap(): return lax.ppermute(x, 'seq', [(i, i ^ by) for i in range(peers)])]
    ppermute x12, waiting for transfers between devices: 26.1 us -> 27.6 us  [along_y(): return lax.ppermute(x, 'head', [(i, i ^ 2 * by) for i in range(peers)])]
    pallas_call x1, Pallas kernels: 2.19 us -> 0.8 us  [body(): pl.pallas_call(pick_kernel, out_shape=jax.ShapeDtypeStruct((4, columns, f...]
    pallas_call x1, Pallas kernels: 0.34 us -> 1.53 us  [body(): pl.pallas_call(gate_kernel, out_shape=[jax.ShapeDtypeStruct(cube, bf16),...]
  transfers between devices with their start and end apart: 29 -> 29, of which waited for: 15 -> 15; matrix products, arithmetic and copies ran while one was open for 1% -> 3% of each run, Pallas kernels for 11% -> 10%
where the time goes in v7:
time: 103 us
  starting transfers between devices  44.3 us (43%)
  waiting for transfers between devices  34.2 us (33%)
  Pallas kernels  18.4 us (18%)
  other arithmetic  2.85 us (3%)
  local copies, waits for them, and re-layouts  2.62 us (3%)
    ppermute x12, waiting for transfers between devices, along_y(): return lax.ppermute(x, 'head', [(i, i ^ 2 * by) for i in range(peers)])  27.6 us
    ppermute x14, starting transfers between devices, swap(): return lax.ppermute(x, 'seq', [(i, i ^ by) for i in range(peers)])  23.7 us
    ppermute x12, starting transfers between devices, along_y(): return lax.ppermute(x, 'head', [(i, i ^ 2 * by) for i in range(peers)])  10.9 us
    ppermute x3, starting transfers between devices, other_core(): return lax.ppermute(x, 'head', [(i, i ^ 1) for i in range(peers)])  9.81 us
    pallas_call x2, Pallas kernels, project(): pl.pallas_call(make_project_kernel(factor), out_shape=jax.ShapeDtypeStruc...  7.8 us
    ppermute x14, waiting for transfers between devices, swap(): return lax.ppermute(x, 'seq', [(i, i ^ by) for i in range(peers)])  6.57 us
    unnamed x20, local copies, waits for them, and re-layouts  2.57 us
    pallas_call x1, Pallas kernels, body(): pl.pallas_call(make_inner_kernel(factor), out_shape=[jax.ShapeDtypeStruct...  2.54 us
  transfers between devices with their start and end apart: 29, of which 15 were waited for; matrix products, arithmetic and copies ran while one was open for 3% of the time, Pallas kernels for 10%

profile of v7, /device:TPU:1, one launch (start us, length us, event | category | flops | bytes accessed | tf_op | source)
XLA Modules:
  0.0 102.7 jit_solution(17476440906665145390)
XLA Ops:
  0.0 1.6 %copy-done = bf16[256,4096]{1,0:T(8,128)(2,1)S(1)} copy-done((bf16[256,4096]{1,0:T(8,128)(2,1)S(1)}, bf16[256,4096]{1,0:T(8,128)(2,1)}, u32[]{:S(2)}) %copy-start) | copy-done | bytes 2097176
  1.6 0.8 shard_map.100
  2.4 3.3 %collective-permute-start.4 = (bf16[4,256,512]{2,1,0:T(8,128)(2,1)S(1)}, bf16[4,256,512]{2,1,0:T(8,128)(2,1)S(1)}, u32[]{:S(2)}, u32[]{:S(2)}) collective-permute-start(bf16[4,256,512]{2,1,0:T(8,128)(2,1)S(1)} %shard_map.100), channel_id=1, source_target_pairs={{0,1},{1,0},{2,3},{3,2},{4,5},{5,4},{6,7},{7,6},{8,9},{9,8},{10,11... | collective-permute-start | bytes 3145736 | tf_op jit(solution)/shard_map/ppermute | solution.py:234
  5.9 1.5 %collective-permute-start.3 = (bf16[256,512]{1,0:T(8,128)(2,1)S(1)}, bf16[256,512]{1,0:T(8,128)(2,1)S(1)}, u32[]{:S(2)}, u32[]{:S(2)}) collective-permute-start(bf16[256,512]{1,0:T(8,128)(2,1)S(1)} %get-tuple-element.41), channel_id=1, source_target_pairs={{0,6},{1,7},{2,4},{3,5},{4,2},{5,3},{6,0},{7,1},{8,14},{9,15},{10,... | collective-permute-start | bytes 786440 | tf_op jit(solution)/shard_map/ppermute | solution.py:231
  7.3 0.4 collective-permute-start.1
  7.7 1.7 %collective-permute-start.2 = (bf16[256,512]{1,0:T(8,128)(2,1)S(1)}, bf16[256,512]{1,0:T(8,128)(2,1)S(1)}, u32[]{:S(2)}, u32[]{:S(2)}) collective-permute-start(bf16[256,512]{1,0:T(8,128)(2,1)S(1)} %get-tuple-element.42), channel_id=1, source_target_pairs={{0,6},{1,7},{2,4},{3,5},{4,2},{5,3},{6,0},{7,1},{8,14},{9,15},{10,... | collective-permute-start | bytes 786440 | tf_op jit(solution)/shard_map/ppermute | solution.py:231
  9.4 4.2 %collective-permute-done.a0 = bf16[256,512]{1,0:T(8,128)(2,1)S(1)} collective-permute-done((bf16[256,512]{1,0:T(8,128)(2,1)S(1)}, bf16[256,512]{1,0:T(8,128)(2,1)S(1)}, u32[]{:S(2)}, u32[]{:S(2)}) %collective-permute-start) | collective-permute-done | bytes 262176 | tf_op jit(solution)/shard_map/ppermute | solution.py:231
  13.6 1.0 collective-permute-start.5
  14.6 0.3 collective-permute-done.3.b1
  15.0 4.3 %collective-permute-done.1.a1 = bf16[256,512]{1,0:T(8,128)(2,1)S(1)} collective-permute-done((bf16[256,512]{1,0:T(8,128)(2,1)S(1)}, bf16[256,512]{1,0:T(8,128)(2,1)S(1)}, u32[]{:S(2)}, u32[]{:S(2)}) %collective-permute-start.1) | collective-permute-done | bytes 262176 | tf_op jit(solution)/shard_map/ppermute | solution.py:231
  19.3 1.3 %collective-permute-done.2.b0 = bf16[256,512]{1,0:T(8,128)(2,1)S(1)} collective-permute-done((bf16[256,512]{1,0:T(8,128)(2,1)S(1)}, bf16[256,512]{1,0:T(8,128)(2,1)S(1)}, u32[]{:S(2)}, u32[]{:S(2)}) %collective-permute-start.2) | collective-permute-done | bytes 262176 | tf_op jit(solution)/shard_map/ppermute | solution.py:231
  20.6 2.1 %shard_map.101 = (f32[2,256,256]{2,1,0:T(8,128)S(1)}, f32[2,256,256]{2,1,0:T(8,128)S(1)}) custom-call(s32[8]{0:T(128)S(1)} %fusion.24.table_ref, bf16[2,256,512]{2,1,0:T(8,128)(2,1)S(1)} %copy-done.7, bf16[256,512]{1,0:T(8,128)(2,1)S(1)} %collective-permute-done.a0, bf16[256,512]{1,0:T(8,128)(2,1)S(1)} %collective-permute-done.1.a1, ...), custom_call_target="tpu_custom_call" | custom-call | flops 805306368 | bytes 4194304 | tf_op jit(solution)/shard_map/pallas_call | solution.py:268
  22.7 3.5 %collective-permute-done.5.c0 = bf16[256,512]{1,0:T(8,128)(2,1)S(1)} collective-permute-done((bf16[256,512]{1,0:T(8,128)(2,1)S(1)}, bf16[256,512]{1,0:T(8,128)(2,1)S(1)}, u32[]{:S(2)}, u32[]{:S(2)}) %collective-permute-start.5) | collective-permute-done | bytes 262176 | tf_op jit(solution)/shard_map/ppermute | solution.py:231
  26.2 1.8 %shard_map.102 = (f32[2,256,256]{2,1,0:T(8,128)S(1)}, f32[2,256,256]{2,1,0:T(8,128)}) custom-call(s32[8]{0:T(128)S(1)} %fusion.24.table_ref, f32[2,256,256]{2,1,0:T(8,128)S(1)} %get-tuple-element.21.mine_in, f32[2,256,256]{2,1,0:T(8,128)S(1)} %get-tuple-element.22.other_in, bf16[256,512]{1,0:T(8,128)(2,1)S(1)} %collective-permute-done.5.c0, ...), custom_call_target="tpu_custom_call" | custom-call | flops 268435456 | bytes 3145728 | tf_op jit(solution)/shard_map/pallas_call | solution.py:285
  28.0 1.0 collective-permute-start.7
  29.0 0.3 shard_map.104
  29.2 0.6 select_bitcast_fusion.5
  29.9 1.1 %collective-permute-start.8 = (bf16[2,128,128]{2,1,0:T(8,128)(2,1)}, bf16[2,128,128]{2,1,0:T(8,128)(2,1)}, u32[]{:S(2)}, u32[]{:S(2)}) collective-permute-start(bf16[2,128,128]{2,1,0:T(8,128)(2,1)} %select_bitcast_fusion.5), channel_id=1, source_target_pairs={{0,8},{8,0},{16,24},{24,16},{32,40},{40,32},{48,56},{56,48},{64,72... | collective-permute-start | bytes 196616 | tf_op jit(solution)/shard_map/ppermute | solution.py:140
  31.0 0.9 copy-done.9
  31.9 1.5 %shard_map.103 = (bf16[2,256,256]{2,1,0:T(8,128)(2,1)S(1)}, f32[2,256,256]{2,1,0:T(8,128)S(1)}, bf16[2,2,128,128]{3,2,1,0:T(8,128)(2,1)S(1)}) custom-call(f32[2,256,256]{2,1,0:T(8,128)S(1)} %get-tuple-element.23.mine_ref, f32[2,256,256]{2,1,0:T(8,128)} %collective-permute-done.7.theirs_ref, bf16[2,256,256]{2,1,0:T(8,128)(2,1)S(1)} %copy-done.9, ...), custom_call_target="tpu_custom_call" | custom-call | flops 33554432 | bytes 3145728 | tf_op jit(solution)/shard_map/pallas_call | solution.py:304
  33.5 1.0 %collective-permute-start.15 = (bf16[2,128,128]{2,1,0:T(8,128)(2,1)S(1)}, bf16[2,128,128]{2,1,0:T(8,128)(2,1)S(1)}, u32[]{:S(2)}, u32[]{:S(2)}) collective-permute-start(bf16[2,128,128]{2,1,0:T(8,128)(2,1)S(1)} %select_bitcast_fusion.2), channel_id=1, source_target_pairs={{0,8},{8,0},{16,24},{24,16},{32,40},{40,32},{48,56},{56,48},{64,72... | collective-permute-start | bytes 196616 | tf_op jit(solution)/shard_map/ppermute | solution.py:140
  34.6 0.9 fusion.16
  35.4 3.1 %collective-permute-start.9 = (bf16[2,128,128]{2,1,0:T(8,128)(2,1)S(1)}, bf16[2,128,128]{2,1,0:T(8,128)(2,1)S(1)}, u32[]{:S(2)}, u32[]{:S(2)}) collective-permute-start(bf16[2,128,128]{2,1,0:T(8,128)(2,1)S(1)} %fusion.16), channel_id=1, source_target_pairs={{0,16},{8,24},{16,0},{24,8},{32,48},{40,56},{48,32},{56,40},{64,80... | collective-permute-start | bytes 196616 | tf_op jit(solution)/shard_map/ppermute | solution.py:140
  38.5 1.3 %collective-permute-start.16 = (bf16[2,128,128]{2,1,0:T(8,128)(2,1)S(1)}, bf16[2,128,128]{2,1,0:T(8,128)(2,1)S(1)}, u32[]{:S(2)}, u32[]{:S(2)}) collective-permute-start(bf16[2,128,128]{2,1,0:T(8,128)(2,1)S(1)} %fusion.19), channel_id=1, source_target_pairs={{0,16},{8,24},{16,0},{24,8},{32,48},{40,56},{48,32},{56,40},{64,80... | collective-permute-start | bytes 196616 | tf_op jit(solution)/shard_map/ppermute | solution.py:140
  39.8 2.2 %collective-permute-done.9 = bf16[2,128,128]{2,1,0:T(8,128)(2,1)S(1)} collective-permute-done((bf16[2,128,128]{2,1,0:T(8,128)(2,1)S(1)}, bf16[2,128,128]{2,1,0:T(8,128)(2,1)S(1)}, u32[]{:S(2)}, u32[]{:S(2)}) %collective-permute-start.9) | collective-permute-done | bytes 65568 | tf_op jit(solution)/shard_map/ppermute | solution.py:140
  42.1 4.7 %collective-permute-start.10 = (bf16[2,128,128]{2,1,0:T(8,128)(2,1)S(1)}, bf16[2,128,128]{2,1,0:T(8,128)(2,1)S(1)}, u32[]{:S(2)}, u32[]{:S(2)}) collective-permute-start(bf16[2,128,128]{2,1,0:T(8,128)(2,1)S(1)} %fusion.6), channel_id=1, source_target_pairs={{0,32},{8,40},{16,48},{24,56},{32,0},{40,8},{48,16},{56,24},{64,96... | collective-permute-start | bytes 196616 | tf_op jit(solution)/shard_map/ppermute | solution.py:140
  46.8 4.2 %collective-permute-start.17 = (bf16[2,128,128]{2,1,0:T(8,128)(2,1)S(1)}, bf16[2,128,128]{2,1,0:T(8,128)(2,1)S(1)}, u32[]{:S(2)}, u32[]{:S(2)}) collective-permute-start(bf16[2,128,128]{2,1,0:T(8,128)(2,1)S(1)} %fusion.14), channel_id=1, source_target_pairs={{0,32},{8,40},{16,48},{24,56},{32,0},{40,8},{48,16},{56,24},{64,96... | collective-permute-start | bytes 196616 | tf_op jit(solution)/shard_map/ppermute | solution.py:140
  51.0 1.3 %collective-permute-start.11 = (bf16[2,128,128]{2,1,0:T(8,128)(2,1)S(1)}, bf16[2,128,128]{2,1,0:T(8,128)(2,1)S(1)}, u32[]{:S(2)}, u32[]{:S(2)}) collective-permute-start(bf16[2,128,128]{2,1,0:T(8,128)(2,1)S(1)} %fusion.7), channel_id=1, source_target_pairs={{0,64},{8,72},{16,80},{24,88},{32,96},{40,104},{48,112},{56,120},{... | collective-permute-start | bytes 196616 | tf_op jit(solution)/shard_map/ppermute | solution.py:140
  52.3 2.5 %collective-permute-start.12 = (bf16[2,128,128]{2,1,0:T(8,128)(2,1)S(1)}, bf16[2,128,128]{2,1,0:T(8,128)(2,1)S(1)}, u32[]{:S(2)}, u32[]{:S(2)}) collective-permute-start(bf16[2,128,128]{2,1,0:T(8,128)(2,1)S(1)} %fusion.7), channel_id=1, source_target_pairs={{0,128},{8,136},{16,144},{24,152},{32,160},{40,168},{48,176},{56,1... | collective-permute-start | bytes 196616 | tf_op jit(solution)/shard_map/ppermute | solution.py:140
  54.8 0.2 collective-permute-start.13
  55.2 1.5 %collective-permute-start.18 = (bf16[2,128,128]{2,1,0:T(8,128)(2,1)S(1)}, bf16[2,128,128]{2,1,0:T(8,128)(2,1)S(1)}, u32[]{:S(2)}, u32[]{:S(2)}) collective-permute-start(bf16[2,128,128]{2,1,0:T(8,128)(2,1)S(1)} %fusion.15), channel_id=1, source_target_pairs={{0,64},{8,72},{16,80},{24,88},{32,96},{40,104},{48,112},{56,120},{... | collective-permute-start | bytes 196616 | tf_op jit(solution)/shard_map/ppermute | solution.py:140
  56.6 2.5 %collective-permute-start.19 = (bf16[2,128,128]{2,1,0:T(8,128)(2,1)S(1)}, bf16[2,128,128]{2,1,0:T(8,128)(2,1)S(1)}, u32[]{:S(2)}, u32[]{:S(2)}) collective-permute-start(bf16[2,128,128]{2,1,0:T(8,128)(2,1)S(1)} %fusion.15), channel_id=1, source_target_pairs={{0,128},{8,136},{16,144},{24,152},{32,160},{40,168},{48,176},{56,1... | collective-permute-start | bytes 196616 | tf_op jit(solution)/shard_map/ppermute | solution.py:140
  59.6 1.8 %collective-permute-done.19 = bf16[2,128,128]{2,1,0:T(8,128)(2,1)S(1)} collective-permute-done((bf16[2,128,128]{2,1,0:T(8,128)(2,1)S(1)}, bf16[2,128,128]{2,1,0:T(8,128)(2,1)S(1)}, u32[]{:S(2)}, u32[]{:S(2)}) %collective-permute-start.19) | collective-permute-done | bytes 65568 | tf_op jit(solution)/shard_map/ppermute | solution.py:140
  61.4 2.0 %collective-permute-done.20 = bf16[2,128,128]{2,1,0:T(8,128)(2,1)S(1)} collective-permute-done((bf16[2,128,128]{2,1,0:T(8,128)(2,1)S(1)}, bf16[2,128,128]{2,1,0:T(8,128)(2,1)S(1)}, u32[]{:S(2)}, u32[]{:S(2)}) %collective-permute-start.20) | collective-permute-done | bytes 65568 | tf_op jit(solution)/shard_map/ppermute | solution.py:140
  63.6 0.9 select_bitcast_fusion.4
  64.5 2.5 %shard_map.105 = (bf16[2,256,256]{2,1,0:T(8,128)(2,1)S(1)}, bf16[2,256,256]{2,1,0:T(8,128)(2,1)S(1)}, f32[2,256,256]{2,1,0:T(8,128)S(1)}, f32[2,256,256]{2,1,0:T(8,128)S(1)}) custom-call(bf16[2,256,256]{2,1,0:T(8,128)(2,1)S(1)} %copy-done.8, bf16[2,256,256]{2,1,0:T(8,128)(2,1)S(1)} %copy-done.5, bf16[2,256,256]{2,1,0:T(8,128)(2,1)S(1)} %copy-done.6, ...), custom_call_target="tpu_custom_call" | custom-call | flops 402653184 | bytes 3145728 | tf_op jit(solution)/shard_map/pallas_call | solution.py:318
  67.1 0.3 collective-permute-done.21
  67.5 3.9 %shard_map.107 = bf16[4,2,256,512]{3,2,1,0:T(8,128)(2,1)S(1)} custom-call(s32[8]{0:T(128)S(1)} %fusion.24.table_ref, bf16[2,256,256]{2,1,0:T(8,128)(2,1)S(1)} %get-tuple-element.29.dq_ref, bf16[2,256,256]{2,1,0:T(8,128)(2,1)S(1)} %get-tuple-element.30.dg_ref, f32[2,256,256]{2,1,0:T(8,128)S(1)} %get-tuple-element.31.dk_part, ...), custom_call_target="tpu_custom_call" | custom-call | flops 2147483648 | bytes 8388608 | tf_op jit(solution)/shard_map/pallas_call | solution.py:330
  71.4 5.5 %collective-permute-start.22 = (bf16[4,2,256,512]{3,2,1,0:T(8,128)(2,1)S(1)}, bf16[4,2,256,512]{3,2,1,0:T(8,128)(2,1)S(1)}, u32[]{:S(2)}, u32[]{:S(2)}) collective-permute-start(bf16[4,2,256,512]{3,2,1,0:T(8,128)(2,1)S(1)} %shard_map.107), channel_id=1, source_target_pairs={{0,1},{1,0},{2,3},{3,2},{4,5},{5,4},{6,7},{7,6},{8,9},{9,8},{10,11... | collective-permute-start | bytes 6291464 | tf_op jit(solution)/shard_map/ppermute | solution.py:234
  77.0 3.9 %shard_map.106.refs_0_.refs_2_.refs_4_ = bf16[4,2,256,512]{3,2,1,0:T(8,128)(2,1)S(1)} custom-call(s32[8]{0:T(128)S(1)} %fusion.24.table_ref, bf16[2,256,256]{2,1,0:T(8,128)(2,1)S(1)} %get-tuple-element.29.dq_ref, bf16[2,256,256]{2,1,0:T(8,128)(2,1)S(1)} %get-tuple-element.30.dg_ref, f32[2,256,256]{2,1,0:T(8,128)S(1)} %get-tuple-element.31.dk_part, ...), custom_call_target="tpu_custom_call" | custom-call | flops 2147483648 | bytes 8388608 | tf_op jit(solution)/shard_map/pallas_call | solution.py:330
  81.0 2.0 %collective-permute-start.27 = (bf16[256,512]{1,0:T(8,128)(2,1)S(1)}, bf16[256,512]{1,0:T(8,128)(2,1)S(1)}, u32[]{:S(2)}, u32[]{:S(2)}) collective-permute-start(bf16[256,512]{1,0:T(8,128)(2,1)S(1)} %get-tuple-element.36), channel_id=1, source_target_pairs={{0,6},{1,7},{2,4},{3,5},{4,2},{5,3},{6,0},{7,1},{8,14},{9,15},{10,... | collective-permute-start | bytes 786440 | tf_op jit(solution)/shard_map/ppermute | solution.py:231
  83.1 1.5 %collective-permute-start.23 = (bf16[256,512]{1,0:T(8,128)(2,1)S(1)}, bf16[256,512]{1,0:T(8,128)(2,1)S(1)}, u32[]{:S(2)}, u32[]{:S(2)}) collective-permute-start(bf16[256,512]{1,0:T(8,128)(2,1)S(1)} %get-tuple-element.33), channel_id=1, source_target_pairs={{0,2},{1,3},{2,0},{3,1},{4,6},{5,7},{6,4},{7,5},{8,10},{9,11},{10,... | collective-permute-start | bytes 786440 | tf_op jit(solution)/shard_map/ppermute | solution.py:231
  84.7 0.8 collective-permute-start.26
  85.5 4.5 %collective-permute-done.27.refs_2_ = bf16[256,512]{1,0:T(8,128)(2,1)S(1)} collective-permute-done((bf16[256,512]{1,0:T(8,128)(2,1)S(1)}, bf16[256,512]{1,0:T(8,128)(2,1)S(1)}, u32[]{:S(2)}, u32[]{:S(2)}) %collective-permute-start.27) | collective-permute-done | bytes 262176 | tf_op jit(solution)/shard_map/ppermute | solution.py:231
  90.5 1.8 %collective-permute-start.25 = (bf16[256,512]{1,0:T(8,128)(2,1)S(1)}, bf16[256,512]{1,0:T(8,128)(2,1)S(1)}, u32[]{:S(2)}, u32[]{:S(2)}) collective-permute-start(bf16[256,512]{1,0:T(8,128)(2,1)S(1)} %shard_map.110), channel_id=1, source_target_pairs={{0,6},{1,7},{2,4},{3,5},{4,2},{5,3},{6,0},{7,1},{8,14},{9,15},{10,... | collective-permute-start | bytes 786440 | tf_op jit(solution)/shard_map/ppermute | solution.py:231
  92.3 3.7 %collective-permute-done.23.refs_2_ = bf16[256,512]{1,0:T(8,128)(2,1)S(1)} collective-permute-done((bf16[256,512]{1,0:T(8,128)(2,1)S(1)}, bf16[256,512]{1,0:T(8,128)(2,1)S(1)}, u32[]{:S(2)}, u32[]{:S(2)}) %collective-permute-start.23) | collective-permute-done | bytes 262176 | tf_op jit(solution)/shard_map/ppermute | solution.py:231
  96.0 5.6 %collective-permute-done.28.refs_7_ = bf16[256,512]{1,0:T(8,128)(2,1)S(1)} collective-permute-done((bf16[256,512]{1,0:T(8,128)(2,1)S(1)}, bf16[256,512]{1,0:T(8,128)(2,1)S(1)}, u32[]{:S(2)}, u32[]{:S(2)}) %collective-permute-start.28) | collective-permute-done | bytes 262176 | tf_op jit(solution)/shard_map/ppermute | solution.py:231
  101.6 1.1 %shard_map.112 = bf16[2,256,512]{2,1,0:T(8,128)(2,1)} custom-call(bf16[4,2,256,512]{3,2,1,0:T(8,128)(2,1)S(1)} %shard_map.106.refs_0_.refs_2_.refs_4_, bf16[4,2,256,512]{3,2,1,0:T(8,128)(2,1)S(1)} %collective-permute-done.22.refs_1_.refs_3_.refs_5_, bf16[256,512]{1,0:T(8,128)(2,1)S(1)} %collective-permute-done.23.refs_2_, ...), custom_call_target="tpu_custom_call" | custom-call | bytes 2621440 | tf_op jit(solution)/shard_map/pallas_call | solution.py:201
  (61 shorter events, 2.0 us)
Async XLA Ops:
  0.0 1.6 %copy-start = (bf16[256,4096]{1,0:T(8,128)(2,1)S(1)}, bf16[256,4096]{1,0:T(8,128)(2,1)}, u32[]{:S(2)}) copy-start(bf16[256,4096]{1,0:T(8,128)(2,1)} %w_ref.5) | copy-start | bytes 6291460
  1.6 4.1 %copy-start.7 = (bf16[2,256,512]{2,1,0:T(8,128)(2,1)S(1)}, bf16[2,256,512]{2,1,0:T(8,128)(2,1)}, u32[]{:S(2)}) copy-start(bf16[2,256,512]{2,1,0:T(8,128)(2,1)} %g_ref.1) | copy-start | bytes 1572868
  2.4 18.2 %collective-permute-start.4 = (bf16[4,256,512]{2,1,0:T(8,128)(2,1)S(1)}, bf16[4,256,512]{2,1,0:T(8,128)(2,1)S(1)}, u32[]{:S(2)}, u32[]{:S(2)}) collective-permute-start(bf16[4,256,512]{2,1,0:T(8,128)(2,1)S(1)} %shard_map.100), channel_id=1, source_target_pairs={{0,1},{1,0},{2,3},{3,2},{4,5},{5,4},{6,7},{7,6},{8,9},{9,8},{10,11... | collective-permute-start | bytes 3145736 | tf_op jit(solution)/shard_map/ppermute | solution.py:234
  5.8 7.9 %collective-permute-start = (bf16[256,512]{1,0:T(8,128)(2,1)S(1)}, bf16[256,512]{1,0:T(8,128)(2,1)S(1)}, u32[]{:S(2)}, u32[]{:S(2)}) collective-permute-start(bf16[256,512]{1,0:T(8,128)(2,1)S(1)} %get-tuple-element.42), channel_id=1, source_target_pairs={{0,2},{1,3},{2,0},{3,1},{4,6},{5,7},{6,4},{7,5},{8,10},{9,11},{10,... | collective-permute-start | bytes 786440 | tf_op jit(solution)/shard_map/ppermute | solution.py:231
  5.9 9.1 %collective-permute-start.3 = (bf16[256,512]{1,0:T(8,128)(2,1)S(1)}, bf16[256,512]{1,0:T(8,128)(2,1)S(1)}, u32[]{:S(2)}, u32[]{:S(2)}) collective-permute-start(bf16[256,512]{1,0:T(8,128)(2,1)S(1)} %get-tuple-element.41), channel_id=1, source_target_pairs={{0,6},{1,7},{2,4},{3,5},{4,2},{5,3},{6,0},{7,1},{8,14},{9,15},{10,... | collective-permute-start | bytes 786440 | tf_op jit(solution)/shard_map/ppermute | solution.py:231
  7.3 11.9 %collective-permute-start.1 = (bf16[256,512]{1,0:T(8,128)(2,1)S(1)}, bf16[256,512]{1,0:T(8,128)(2,1)S(1)}, u32[]{:S(2)}, u32[]{:S(2)}) collective-permute-start(bf16[256,512]{1,0:T(8,128)(2,1)S(1)} %get-tuple-element.41), channel_id=1, source_target_pairs={{0,2},{1,3},{2,0},{3,1},{4,6},{5,7},{6,4},{7,5},{8,10},{9,11},{10,... | collective-permute-start | bytes 786440 | tf_op jit(solution)/shard_map/ppermute | solution.py:231
  7.7 12.8 %collective-permute-start.2 = (bf16[256,512]{1,0:T(8,128)(2,1)S(1)}, bf16[256,512]{1,0:T(8,128)(2,1)S(1)}, u32[]{:S(2)}, u32[]{:S(2)}) collective-permute-start(bf16[256,512]{1,0:T(8,128)(2,1)S(1)} %get-tuple-element.42), channel_id=1, source_target_pairs={{0,6},{1,7},{2,4},{3,5},{4,2},{5,3},{6,0},{7,1},{8,14},{9,15},{10,... | collective-permute-start | bytes 786440 | tf_op jit(solution)/shard_map/ppermute | solution.py:231
  13.6 12.5 %collective-permute-start.5 = (bf16[256,512]{1,0:T(8,128)(2,1)S(1)}, bf16[256,512]{1,0:T(8,128)(2,1)S(1)}, u32[]{:S(2)}, u32[]{:S(2)}) collective-permute-start(bf16[256,512]{1,0:T(8,128)(2,1)S(1)} %collective-permute-done.a0), channel_id=1, source_target_pairs={{0,6},{1,7},{2,4},{3,5},{4,2},{5,3},{6,0},{7,1},{8,14},{9,15},{10,... | collective-permute-start | bytes 786440 | tf_op jit(solution)/shard_map/ppermute | solution.py:231
  14.9 11.2 %collective-permute-start.6 = (bf16[256,512]{1,0:T(8,128)(2,1)S(1)}, bf16[256,512]{1,0:T(8,128)(2,1)S(1)}, u32[]{:S(2)}, u32[]{:S(2)}) collective-permute-start(bf16[256,512]{1,0:T(8,128)(2,1)S(1)} %collective-permute-done.3.b1), channel_id=1, source_target_pairs={{0,2},{1,3},{2,0},{3,1},{4,6},{5,7},{6,4},{7,5},{8,10},{9,11},{10,... | collective-permute-start | bytes 786440 | tf_op jit(solution)/shard_map/ppermute | solution.py:231
  26.2 2.8 %copy-start.5 = (bf16[2,256,256]{2,1,0:T(8,128)(2,1)S(1)}, bf16[2,256,256]{2,1,0:T(8,128)(2,1)}, u32[]{:S(2)}) copy-start(bf16[2,256,256]{2,1,0:T(8,128)(2,1)} %k_ref.7) | copy-start | bytes 786436
  26.2 2.8 %copy-start.6 = (bf16[2,256,256]{2,1,0:T(8,128)(2,1)S(1)}, bf16[2,256,256]{2,1,0:T(8,128)(2,1)}, u32[]{:S(2)}) copy-start(bf16[2,256,256]{2,1,0:T(8,128)(2,1)} %v_ref.7) | copy-start | bytes 786436
  26.2 4.8 %copy-start.8 = (bf16[2,256,256]{2,1,0:T(8,128)(2,1)S(1)}, bf16[2,256,256]{2,1,0:T(8,128)(2,1)}, u32[]{:S(2)}) copy-start(bf16[2,256,256]{2,1,0:T(8,128)(2,1)} %q_ref.3) | copy-start | bytes 786436
  28.0 3.0 %collective-permute-start.7 = (f32[2,256,256]{2,1,0:T(8,128)}, f32[2,256,256]{2,1,0:T(8,128)}, u32[]{:S(2)}, u32[]{:S(2)}) collective-permute-start(f32[2,256,256]{2,1,0:T(8,128)} %get-tuple-element.24), channel_id=1, source_target_pairs={{0,1},{1,0},{2,3},{3,2},{4,5},{5,4},{6,7},{7,6},{8,9},{9,8},{10,11... | collective-permute-start | bytes 1572872 | tf_op jit(solution)/shard_map/ppermute | solution.py:234
  29.0 38.5 %copy-start.4 = (bf16[4096,256]{1,0:T(8,128)(2,1)S(1)}, bf16[4096,256]{1,0:T(8,128)(2,1)}, u32[]{:S(2)}) copy-start(bf16[4096,256]{1,0:T(8,128)(2,1)} %wg.3) | copy-start | bytes 6291460
  29.9 4.7 %collective-permute-start.8 = (bf16[2,128,128]{2,1,0:T(8,128)(2,1)}, bf16[2,128,128]{2,1,0:T(8,128)(2,1)}, u32[]{:S(2)}, u32[]{:S(2)}) collective-permute-start(bf16[2,128,128]{2,1,0:T(8,128)(2,1)} %select_bitcast_fusion.5), channel_id=1, source_target_pairs={{0,8},{8,0},{16,24},{24,16},{32,40},{40,32},{48,56},{56,48},{64,72... | collective-permute-start | bytes 196616 | tf_op jit(solution)/shard_map/ppermute | solution.py:140
  31.0 1.0 copy-start.9
  31.9 35.6 %copy-start.3 = (bf16[4096,256]{1,0:T(8,128)(2,1)S(1)}, bf16[4096,256]{1,0:T(8,128)(2,1)}, u32[]{:S(2)}) copy-start(bf16[4096,256]{1,0:T(8,128)(2,1)} %wv.3) | copy-start | bytes 6291460
  33.5 5.0 %collective-permute-start.15 = (bf16[2,128,128]{2,1,0:T(8,128)(2,1)S(1)}, bf16[2,128,128]{2,1,0:T(8,128)(2,1)S(1)}, u32[]{:S(2)}, u32[]{:S(2)}) collective-permute-start(bf16[2,128,128]{2,1,0:T(8,128)(2,1)S(1)} %select_bitcast_fusion.2), channel_id=1, source_target_pairs={{0,8},{8,0},{16,24},{24,16},{32,40},{40,32},{48,56},{56,48},{64,72... | collective-permute-start | bytes 196616 | tf_op jit(solution)/shard_map/ppermute | solution.py:140
  35.4 6.6 %collective-permute-start.9 = (bf16[2,128,128]{2,1,0:T(8,128)(2,1)S(1)}, bf16[2,128,128]{2,1,0:T(8,128)(2,1)S(1)}, u32[]{:S(2)}, u32[]{:S(2)}) collective-permute-start(bf16[2,128,128]{2,1,0:T(8,128)(2,1)S(1)} %fusion.16), channel_id=1, source_target_pairs={{0,16},{8,24},{16,0},{24,8},{32,48},{40,56},{48,32},{56,40},{64,80... | collective-permute-start | bytes 196616 | tf_op jit(solution)/shard_map/ppermute | solution.py:140
  38.5 8.3 %collective-permute-start.16 = (bf16[2,128,128]{2,1,0:T(8,128)(2,1)S(1)}, bf16[2,128,128]{2,1,0:T(8,128)(2,1)S(1)}, u32[]{:S(2)}, u32[]{:S(2)}) collective-permute-start(bf16[2,128,128]{2,1,0:T(8,128)(2,1)S(1)} %fusion.19), channel_id=1, source_target_pairs={{0,16},{8,24},{16,0},{24,8},{32,48},{40,56},{48,32},{56,40},{64,80... | collective-permute-start | bytes 196616 | tf_op jit(solution)/shard_map/ppermute | solution.py:140
  42.1 8.9 %collective-permute-start.10 = (bf16[2,128,128]{2,1,0:T(8,128)(2,1)S(1)}, bf16[2,128,128]{2,1,0:T(8,128)(2,1)S(1)}, u32[]{:S(2)}, u32[]{:S(2)}) collective-permute-start(bf16[2,128,128]{2,1,0:T(8,128)(2,1)S(1)} %fusion.6), channel_id=1, source_target_pairs={{0,32},{8,40},{16,48},{24,56},{32,0},{40,8},{48,16},{56,24},{64,96... | collective-permute-start | bytes 196616 | tf_op jit(solution)/shard_map/ppermute | solution.py:140
  46.8 8.3 %collective-permute-start.17 = (bf16[2,128,128]{2,1,0:T(8,128)(2,1)S(1)}, bf16[2,128,128]{2,1,0:T(8,128)(2,1)S(1)}, u32[]{:S(2)}, u32[]{:S(2)}) collective-permute-start(bf16[2,128,128]{2,1,0:T(8,128)(2,1)S(1)} %fusion.14), channel_id=1, source_target_pairs={{0,32},{8,40},{16,48},{24,56},{32,0},{40,8},{48,16},{56,24},{64,96... | collective-permute-start | bytes 196616 | tf_op jit(solution)/shard_map/ppermute | solution.py:140
  51.0 8.0 %collective-permute-start.11 = (bf16[2,128,128]{2,1,0:T(8,128)(2,1)S(1)}, bf16[2,128,128]{2,1,0:T(8,128)(2,1)S(1)}, u32[]{:S(2)}, u32[]{:S(2)}) collective-permute-start(bf16[2,128,128]{2,1,0:T(8,128)(2,1)S(1)} %fusion.7), channel_id=1, source_target_pairs={{0,64},{8,72},{16,80},{24,88},{32,96},{40,104},{48,112},{56,120},{... | collective-permute-start | bytes 196616 | tf_op jit(solution)/shard_map/ppermute | solution.py:140
  52.3 7.0 %collective-permute-start.12 = (bf16[2,128,128]{2,1,0:T(8,128)(2,1)S(1)}, bf16[2,128,128]{2,1,0:T(8,128)(2,1)S(1)}, u32[]{:S(2)}, u32[]{:S(2)}) collective-permute-start(bf16[2,128,128]{2,1,0:T(8,128)(2,1)S(1)} %fusion.7), channel_id=1, source_target_pairs={{0,128},{8,136},{16,144},{24,152},{32,160},{40,168},{48,176},{56,1... | collective-permute-start | bytes 196616 | tf_op jit(solution)/shard_map/ppermute | solution.py:140
  54.8 4.6 %collective-permute-start.13 = (bf16[2,128,128]{2,1,0:T(8,128)(2,1)S(1)}, bf16[2,128,128]{2,1,0:T(8,128)(2,1)S(1)}, u32[]{:S(2)}, u32[]{:S(2)}) collective-permute-start(bf16[2,128,128]{2,1,0:T(8,128)(2,1)S(1)} %fusion.7), channel_id=1, source_target_pairs={{0,192},{8,200},{16,208},{24,216},{32,224},{40,232},{48,240},{56,2... | collective-permute-start | bytes 196616 | tf_op jit(solution)/shard_map/ppermute | solution.py:140
  55.2 4.5 %collective-permute-start.18 = (bf16[2,128,128]{2,1,0:T(8,128)(2,1)S(1)}, bf16[2,128,128]{2,1,0:T(8,128)(2,1)S(1)}, u32[]{:S(2)}, u32[]{:S(2)}) collective-permute-start(bf16[2,128,128]{2,1,0:T(8,128)(2,1)S(1)} %fusion.15), channel_id=1, source_target_pairs={{0,64},{8,72},{16,80},{24,88},{32,96},{40,104},{48,112},{56,120},{... | collective-permute-start | bytes 196616 | tf_op jit(solution)/shard_map/ppermute | solution.py:140
  56.6 4.8 %collective-permute-start.19 = (bf16[2,128,128]{2,1,0:T(8,128)(2,1)S(1)}, bf16[2,128,128]{2,1,0:T(8,128)(2,1)S(1)}, u32[]{:S(2)}, u32[]{:S(2)}) collective-permute-start(bf16[2,128,128]{2,1,0:T(8,128)(2,1)S(1)} %fusion.15), channel_id=1, source_target_pairs={{0,128},{8,136},{16,144},{24,152},{32,160},{40,168},{48,176},{56,1... | collective-permute-start | bytes 196616 | tf_op jit(solution)/shard_map/ppermute | solution.py:140
  59.1 4.3 %collective-permute-start.20 = (bf16[2,128,128]{2,1,0:T(8,128)(2,1)S(1)}, bf16[2,128,128]{2,1,0:T(8,128)(2,1)S(1)}, u32[]{:S(2)}, u32[]{:S(2)}) collective-permute-start(bf16[2,128,128]{2,1,0:T(8,128)(2,1)S(1)} %fusion.15), channel_id=1, source_target_pairs={{0,192},{8,200},{16,208},{24,216},{32,224},{40,232},{48,240},{56,2... | collective-permute-start | bytes 196616 | tf_op jit(solution)/shard_map/ppermute | solution.py:140
  59.5 8.0 %copy-start.1 = (bf16[4096,256]{1,0:T(8,128)(2,1)S(1)}, bf16[4096,256]{1,0:T(8,128)(2,1)}, u32[]{:S(2)}) copy-start(bf16[4096,256]{1,0:T(8,128)(2,1)} %wq.3) | copy-start | bytes 6291460
  59.5 8.0 %copy-start.2 = (bf16[4096,256]{1,0:T(8,128)(2,1)S(1)}, bf16[4096,256]{1,0:T(8,128)(2,1)}, u32[]{:S(2)}) copy-start(bf16[4096,256]{1,0:T(8,128)(2,1)} %wk.3) | copy-start | bytes 6291460
  59.5 4.1 %collective-permute-start.14 = (bf16[2,128,128]{2,1,0:T(8,128)(2,1)S(1)}, bf16[2,128,128]{2,1,0:T(8,128)(2,1)S(1)}, u32[]{:S(2)}, u32[]{:S(2)}) collective-permute-start(bf16[2,128,128]{2,1,0:T(8,128)(2,1)S(1)} %get-tuple-element.39), channel_id=1, source_target_pairs={{0,8},{8,0},{16,24},{24,16},{32,40},{40,32},{48,56},{56,48},{64,72... | collective-permute-start | bytes 196616 | tf_op jit(solution)/shard_map/ppermute | solution.py:140
  63.5 3.8 %collective-permute-start.21 = (bf16[2,128,128]{2,1,0:T(8,128)(2,1)S(1)}, bf16[2,128,128]{2,1,0:T(8,128)(2,1)S(1)}, u32[]{:S(2)}, u32[]{:S(2)}) collective-permute-start(bf16[2,128,128]{2,1,0:T(8,128)(2,1)S(1)} %fusion.21), channel_id=1, source_target_pairs={{0,8},{8,0},{16,24},{24,16},{32,40},{40,32},{48,56},{56,48},{64,72... | collective-permute-start | bytes 196616 | tf_op jit(solution)/shard_map/ppermute | solution.py:140
  71.4 9.4 %collective-permute-start.22 = (bf16[4,2,256,512]{3,2,1,0:T(8,128)(2,1)S(1)}, bf16[4,2,256,512]{3,2,1,0:T(8,128)(2,1)S(1)}, u32[]{:S(2)}, u32[]{:S(2)}) collective-permute-start(bf16[4,2,256,512]{3,2,1,0:T(8,128)(2,1)S(1)} %shard_map.107), channel_id=1, source_target_pairs={{0,1},{1,0},{2,3},{3,2},{4,5},{5,4},{6,7},{7,6},{8,9},{9,8},{10,11... | collective-permute-start | bytes 6291464 | tf_op jit(solution)/shard_map/ppermute | solution.py:234
  81.0 9.0 %collective-permute-start.27 = (bf16[256,512]{1,0:T(8,128)(2,1)S(1)}, bf16[256,512]{1,0:T(8,128)(2,1)S(1)}, u32[]{:S(2)}, u32[]{:S(2)}) collective-permute-start(bf16[256,512]{1,0:T(8,128)(2,1)S(1)} %get-tuple-element.36), channel_id=1, source_target_pairs={{0,6},{1,7},{2,4},{3,5},{4,2},{5,3},{6,0},{7,1},{8,14},{9,15},{10,... | collective-permute-start | bytes 786440 | tf_op jit(solution)/shard_map/ppermute | solution.py:231
  83.0 7.3 %collective-permute-start.24 = (bf16[256,512]{1,0:T(8,128)(2,1)S(1)}, bf16[256,512]{1,0:T(8,128)(2,1)S(1)}, u32[]{:S(2)}, u32[]{:S(2)}) collective-permute-start(bf16[256,512]{1,0:T(8,128)(2,1)S(1)} %get-tuple-element.34), channel_id=1, source_target_pairs={{0,2},{1,3},{2,0},{3,1},{4,6},{5,7},{6,4},{7,5},{8,10},{9,11},{10,... | collective-permute-start | bytes 786440 | tf_op jit(solution)/shard_map/ppermute | solution.py:231
  83.1 12.8 %collective-permute-start.23 = (bf16[256,512]{1,0:T(8,128)(2,1)S(1)}, bf16[256,512]{1,0:T(8,128)(2,1)S(1)}, u32[]{:S(2)}, u32[]{:S(2)}) collective-permute-start(bf16[256,512]{1,0:T(8,128)(2,1)S(1)} %get-tuple-element.33), channel_id=1, source_target_pairs={{0,2},{1,3},{2,0},{3,1},{4,6},{5,7},{6,4},{7,5},{8,10},{9,11},{10,... | collective-permute-start | bytes 786440 | tf_op jit(solution)/shard_map/ppermute | solution.py:231
  84.7 11.3 %collective-permute-start.26 = (bf16[256,512]{1,0:T(8,128)(2,1)S(1)}, bf16[256,512]{1,0:T(8,128)(2,1)S(1)}, u32[]{:S(2)}, u32[]{:S(2)}) collective-permute-start(bf16[256,512]{1,0:T(8,128)(2,1)S(1)} %get-tuple-element.35), channel_id=1, source_target_pairs={{0,6},{1,7},{2,4},{3,5},{4,2},{5,3},{6,0},{7,1},{8,14},{9,15},{10,... | collective-permute-start | bytes 786440 | tf_op jit(solution)/shard_map/ppermute | solution.py:231
  90.1 11.5 %collective-permute-start.28 = (bf16[256,512]{1,0:T(8,128)(2,1)S(1)}, bf16[256,512]{1,0:T(8,128)(2,1)S(1)}, u32[]{:S(2)}, u32[]{:S(2)}) collective-permute-start(bf16[256,512]{1,0:T(8,128)(2,1)S(1)} %shard_map.111), channel_id=1, source_target_pairs={{0,2},{1,3},{2,0},{3,1},{4,6},{5,7},{6,4},{7,5},{8,10},{9,11},{10,... | collective-permute-start | bytes 786440 | tf_op jit(solution)/shard_map/ppermute | solution.py:231
  90.5 11.1 %collective-permute-start.25 = (bf16[256,512]{1,0:T(8,128)(2,1)S(1)}, bf16[256,512]{1,0:T(8,128)(2,1)S(1)}, u32[]{:S(2)}, u32[]{:S(2)}) collective-permute-start(bf16[256,512]{1,0:T(8,128)(2,1)S(1)} %shard_map.110), channel_id=1, source_target_pairs={{0,6},{1,7},{2,4},{3,5},{4,2},{5,3},{6,0},{7,1},{8,14},{9,15},{10,... | collective-permute-start | bytes 786440 | tf_op jit(solution)/shard_map/ppermute | solution.py:231
